TPU v7x, 32 devices: a whole 2x2x4 slice. The times are simulated.
32 devices in a mesh: ctx: 8 (over y, x, core), wt: 4 (over z).
Axes of the slice: x: 2, y: 2, z: 4, core: 2. Of those that a mesh axis runs over, the one named last changes fastest.
Arguments:
- tokens: bfloat16 [2, 4, 1024, 768], P(None, 'wt', 'ctx'), may hold values from -6 to 6
- doc_lengths: int32 [2, 4, 16], P(None, 'wt'), may hold values from 1 to 512, 1024 in all within a row
- query_weight: bfloat16 [768, 768], P('wt'), may hold values from -0.3125 to 0.3125
- query_bias: bfloat16 [768], P('wt'), may hold values from -1.5 to 1.5
- key_weight: bfloat16 [768, 768], P('wt'), may hold values from -0.3125 to 0.3125
- value_weight: bfloat16 [768, 768], P('wt'), may hold values from -0.21875 to 0.21875
- value_bias: bfloat16 [768], P('wt'), may hold values from -1.5 to 1.5
- out_weight: bfloat16 [768, 768], P('wt'), may hold values from -1.25 to 1.25
- out_bias: bfloat16 [768], P('wt'), may hold values from -1.5 to 1.5
- first_gain: bfloat16 [768], P('wt'), may hold values from 0.5 to 1.5
- first_shift: bfloat16 [768], P('wt'), may hold values from -1.5 to 1.5
- inner_weight: bfloat16 [768, 3072], P('wt'), may hold values from -0.21875 to 0.21875
- inner_bias: bfloat16 [3072], P('wt'), may hold values from -1.5 to 1.5
- outer_weight: bfloat16 [3072, 768], P('wt'), may hold values from -0.109375 to 0.109375
- outer_bias: bfloat16 [768], P('wt'), may hold values from -1.5 to 1.5
- second_gain: bfloat16 [768], P('wt'), may hold values from 0.5 to 1.5
- second_shift: bfloat16 [768], P('wt'), may hold values from -1.5 to 1.5
- cotangent: bfloat16 [2, 4, 1024, 768], P(None, 'wt', 'ctx'), may hold values from -6 to 6
Outputs:
- block_output: bfloat16 [2, 4, 1024, 768], P(None, 'wt', 'ctx')
- tokens_gradient: float32 [2, 4, 1024, 768], P(None, 'wt', 'ctx')
- query_weight_gradient: float32 [768, 768], P('wt')
- query_bias_gradient: float32 [768], P('wt')
- key_weight_gradient: float32 [768, 768], P('wt')
- value_weight_gradient: float32 [768, 768], P('wt')
- value_bias_gradient: float32 [768], P('wt')
- out_weight_gradient: float32 [768, 768], P('wt')
- out_bias_gradient: float32 [768], P('wt')
- first_gain_gradient: float32 [768], P('wt')
- first_shift_gradient: float32 [768], P('wt')
- inner_weight_gradient: float32 [768, 3072], P('wt')
- inner_bias_gradient: float32 [3072], P('wt')
- outer_weight_gradient: float32 [3072, 768], P('wt')
- outer_bias_gradient: float32 [768], P('wt')
- second_gain_gradient: float32 [768], P('wt')
- second_shift_gradient: float32 [768], P('wt')
Inputs may be any that keep to these rules, and one draw needn't show every extreme that they name: `doc_lengths`: each row holds the lengths of the 16 documents of one packed sequence in order; a row sums to 1024 and its longest document has exactly 512 tokens.
All inputs are finite; a program needn't handle non-finite values.
Results may differ from a plain program's by a relative error of at most 0.02.
Values may be sent and summed in bfloat16 or wider, within the bound.
No kernel may reach another device: no remote copies, remote signals or barrier semaphores. Data moves between devices by JAX's collectives and lax.ppermute only.
A program may use at most 256 MiB of HBM per device.

v0:
```python
import math

import jax
import jax.numpy as jnp
from jax import lax
from jax.experimental import pallas as pl
from jax.experimental.pallas import tpu as pltpu
from jax.sharding import PartitionSpec as P


HEADS = 12
HEAD_DIM = 64


EPS = 1e-12
NEG = -1e30
ROOT_HALF = 0.7071067811865476


def for_sending(shard):

    def short(part):
        return part.astype(jnp.bfloat16) if part.dtype == jnp.float32 else part

    return jax.tree.map(short, shard)


def normalize(rows, gain, shift):
    mean = jnp.mean(rows, axis=-1, keepdims=True)
    centered = rows - mean
    spread = jnp.mean(centered * centered, axis=-1, keepdims=True)
    return centered * lax.rsqrt(spread + EPS) * gain + shift


def gelu(inner):
    return 0.5 * inner * (1.0 + lax.erf(inner * ROOT_HALF))


def segment_of(starts, positions):
    found = (starts[:, None, :] <= positions[:, :, None]).astype(jnp.int32)
    return jnp.sum(found, axis=-1) - 1


def project(inputs, weight):
    return jnp.einsum("btd,de->bte", inputs, weight, preferred_element_type=jnp.float32)


def project_back(grads, weight):
    return jnp.einsum("bte,de->btd", grads, weight, preferred_element_type=jnp.float32)


def outer_sum(inputs, grads):
    return jnp.einsum("btd,bte->de", inputs, grads, preferred_element_type=jnp.float32)


def row_sum(grads):
    return jnp.sum(grads.astype(jnp.float32), axis=(0, 1))


def heads_of(array):
    return array.reshape(array.shape[0], array.shape[1], HEADS, HEAD_DIM)


def block_loop(width, carry, visit):
    block = math.gcd(width, 512)

    def step(state, index):
        return (visit(state, index * block, block), None)

    carry, _ = lax.scan(step, carry, jnp.arange(width // block, dtype=jnp.int32))
    return carry


def reaches(starts, own_seg, first, count):
    positions = first + jnp.arange(count, dtype=jnp.int32)
    other = segment_of(starts, jnp.broadcast_to(positions, (starts.shape[0], count)))
    touch = jnp.any((other[:, 0] <= own_seg[:, -1]) & (other[:, -1] >= own_seg[:, 0]))
    return (other, touch)


def keep_state(state):
    return state


def forward_attention(queries, query_seg, starts, keys, values):
    scale = HEAD_DIM ** (-0.5)
    batch, rows = (queries.shape[0], queries.shape[1])
    query_heads = heads_of(queries)

    def forward_fold(carry, piece, start):
        key_piece, value_piece = piece

        def visit(state, offset, count):
            other, touch = reaches(starts, query_seg, offset, count)

            def compute(state):
                top, total, accum = state
                key_block = heads_of(lax.dynamic_slice_in_dim(key_piece, offset, count, 1))
                value_block = heads_of(lax.dynamic_slice_in_dim(value_piece, offset, count, 1))
                scores = (
                    jnp.einsum(
                        "bqhd,bkhd->bhqk",
                        query_heads,
                        key_block,
                        preferred_element_type=jnp.float32,
                    )
                    * scale
                )
                mask = (query_seg[:, :, None] == other[:, None, :])[:, None]
                scores = jnp.where(mask, scores, NEG)
                new_top = jnp.maximum(top, jnp.max(scores, axis=-1))
                expd = jnp.where(mask, jnp.exp(scores - new_top[..., None]), 0.0)
                factor = jnp.exp(top - new_top)
                total = total * factor + jnp.sum(expd, axis=-1)
                added = jnp.einsum(
                    "bhqk,bkhd->bqhd",
                    expd.astype(jnp.bfloat16),
                    value_block,
                    preferred_element_type=jnp.float32,
                )
                accum = accum * jnp.transpose(factor, (0, 2, 1))[..., None] + added
                return (new_top, total, accum)

            return lax.cond(touch, compute, keep_state, state)

        return block_loop(key_piece.shape[1], carry, visit)

    init = (
        jnp.full((batch, HEADS, rows), NEG, jnp.float32),
        jnp.zeros((batch, HEADS, rows), jnp.float32),
        jnp.zeros((batch, rows, HEADS, HEAD_DIM), jnp.float32),
    )
    whole = (keys, values)
    top, total, accum = forward_fold(
        init,
        (
            lax.all_gather(keys, "ctx", axis=1, tiled=True),
            lax.all_gather(values, "ctx", axis=1, tiled=True),
        ),
        jnp.int32(0),
    )
    mixed = accum / jnp.transpose(total, (0, 2, 1))[..., None]
    return (mixed, top + jnp.log(total), whole)


def query_gradient(queries, query_seg, starts, keys, values, dmixed, logsum, delta):
    scale = HEAD_DIM ** (-0.5)
    query_heads = heads_of(queries)
    grad_heads = heads_of(dmixed)

    def query_fold(carry, piece, start):
        key_piece, value_piece = piece

        def visit(state, offset, count):
            other, touch = reaches(starts, query_seg, offset, count)

            def compute(state):
                key_block = heads_of(lax.dynamic_slice_in_dim(key_piece, offset, count, 1))
                value_block = heads_of(lax.dynamic_slice_in_dim(value_piece, offset, count, 1))
                scores = (
                    jnp.einsum(
                        "bqhd,bkhd->bhqk",
                        query_heads,
                        key_block,
                        preferred_element_type=jnp.float32,
                    )
                    * scale
                )
                mask = (query_seg[:, :, None] == other[:, None, :])[:, None]
                probs = jnp.where(
                    mask, jnp.exp(jnp.where(mask, scores, NEG) - logsum[..., None]), 0.0
                )
                dprobs = jnp.einsum(
                    "bqhd,bkhd->bhqk", grad_heads, value_block, preferred_element_type=jnp.float32
                )
                dscores = (probs * (dprobs - delta[..., None])).astype(jnp.bfloat16)
                return (
                    state
                    + jnp.einsum(
                        "bhqk,bkhd->bqhd", dscores, key_block, preferred_element_type=jnp.float32
                    )
                    * scale
                )

            return lax.cond(touch, compute, keep_state, state)

        return block_loop(key_piece.shape[1], carry, visit)

    init = jnp.zeros(query_heads.shape, jnp.float32)
    return query_fold(
        init,
        (
            lax.all_gather(keys, "ctx", axis=1, tiled=True),
            lax.all_gather(values, "ctx", axis=1, tiled=True),
        ),
        jnp.int32(0),
    )


def key_gradient(keys, values, key_seg, starts, queries, dmixed, logsum, delta):
    scale = HEAD_DIM ** (-0.5)
    key_heads = heads_of(keys)
    value_heads = heads_of(values)
    every_top, every_delta = (
        lax.all_gather(logsum, "ctx", axis=2, tiled=True),
        lax.all_gather(delta, "ctx", axis=2, tiled=True),
    )

    def key_fold(carry, piece, start):
        query_piece, grad_piece = piece

        def visit(state, offset, count):
            other, touch = reaches(starts, key_seg, offset, count)

            def compute(state):
                dkeys, dvalues = state
                query_block = heads_of(lax.dynamic_slice_in_dim(query_piece, offset, count, 1))
                grad_block = heads_of(lax.dynamic_slice_in_dim(grad_piece, offset, count, 1))
                top_block = lax.dynamic_slice_in_dim(every_top, offset, count, 2)
                delta_block = lax.dynamic_slice_in_dim(every_delta, offset, count, 2)
                scores = (
                    jnp.einsum(
                        "bqhd,bkhd->bhqk",
                        query_block,
                        key_heads,
                        preferred_element_type=jnp.float32,
                    )
                    * scale
                )
                mask = (other[:, :, None] == key_seg[:, None, :])[:, None]
                probs = jnp.where(
                    mask, jnp.exp(jnp.where(mask, scores, NEG) - top_block[..., None]), 0.0
                )
                dvalues = dvalues + jnp.einsum(
                    "bhqk,bqhd->bkhd",
                    probs.astype(jnp.bfloat16),
                    grad_block,
                    preferred_element_type=jnp.float32,
                )
                dprobs = jnp.einsum(
                    "bqhd,bkhd->bhqk", grad_block, value_heads, preferred_element_type=jnp.float32
                )
                dscores = (probs * (dprobs - delta_block[..., None])).astype(jnp.bfloat16)
                dkeys = (
                    dkeys
                    + jnp.einsum(
                        "bhqk,bqhd->bkhd", dscores, query_block, preferred_element_type=jnp.float32
                    )
                    * scale
                )
                return (dkeys, dvalues)

            return lax.cond(touch, compute, keep_state, state)

        return block_loop(query_piece.shape[1], carry, visit)

    empty = jnp.zeros(key_heads.shape, jnp.float32)
    return key_fold(
        (empty, empty),
        (
            lax.all_gather(queries, "ctx", axis=1, tiled=True),
            lax.all_gather(dmixed, "ctx", axis=1, tiled=True),
        ),
        jnp.int32(0),
    )


def forward_pass(tokens, starts, weights, base):
    (
        query_weight,
        query_bias,
        key_weight,
        value_weight,
        value_bias,
        out_weight,
        out_bias,
        first_gain,
        first_shift,
        inner_weight,
        inner_bias,
        outer_weight,
        outer_bias,
        second_gain,
        second_shift,
    ) = weights
    rows = tokens.shape[1]
    positions = base + jnp.arange(rows, dtype=jnp.int32)
    query_seg = segment_of(starts, jnp.broadcast_to(positions, (tokens.shape[0], rows)))
    queries = (project(tokens, query_weight) + query_bias.astype(jnp.float32)).astype(jnp.bfloat16)
    keys = project(tokens, key_weight).astype(jnp.bfloat16)
    values = (project(tokens, value_weight) + value_bias.astype(jnp.float32)).astype(jnp.bfloat16)
    mixed, logsum, whole = forward_attention(queries, query_seg, starts, keys, values)
    mixed_low = mixed.reshape(tokens.shape).astype(jnp.bfloat16)
    first_sum = (
        tokens.astype(jnp.float32) + project(mixed_low, out_weight) + out_bias.astype(jnp.float32)
    )
    first = normalize(first_sum, first_gain.astype(jnp.float32), first_shift.astype(jnp.float32))
    first_low = first.astype(jnp.bfloat16)
    inner = project(first_low, inner_weight) + inner_bias.astype(jnp.float32)
    active = gelu(inner).astype(jnp.bfloat16)
    second_sum = first + project(active, outer_weight) + outer_bias.astype(jnp.float32)
    output = normalize(
        second_sum, second_gain.astype(jnp.float32), second_shift.astype(jnp.float32)
    ).astype(jnp.bfloat16)
    saved = (
        tokens,
        query_seg,
        queries,
        keys,
        values,
        mixed,
        logsum,
        mixed_low,
        first_sum,
        first_low,
        inner,
        active,
        second_sum,
        whole,
    )
    return (output, saved)


def backward_pass(saved, starts, weights, cotangent):
    (
        query_weight,
        _,
        key_weight,
        value_weight,
        _,
        out_weight,
        _,
        first_gain,
        first_shift,
        inner_weight,
        _,
        outer_weight,
        _,
        second_gain,
        second_shift,
    ) = weights
    (
        tokens,
        query_seg,
        queries,
        keys,
        values,
        mixed,
        logsum,
        mixed_low,
        first_sum,
        first_low,
        inner,
        active,
        second_sum,
        _,
    ) = saved
    unused, second_back = jax.vjp(
        normalize, second_sum, second_gain.astype(jnp.float32), second_shift.astype(jnp.float32)
    )
    dsecond, dgain_second, dshift_second = second_back(cotangent.astype(jnp.float32))
    douter = dsecond.astype(jnp.bfloat16)
    dactive = project_back(douter, outer_weight)
    unused, gelu_back = jax.vjp(gelu, inner)
    dinner = gelu_back(dactive)[0].astype(jnp.bfloat16)
    dfirst = dsecond + project_back(dinner, inner_weight)
    unused, first_back = jax.vjp(
        normalize, first_sum, first_gain.astype(jnp.float32), first_shift.astype(jnp.float32)
    )
    dfirst_sum, dgain_first, dshift_first = first_back(dfirst)
    dbranch = dfirst_sum.astype(jnp.bfloat16)
    dmixed = project_back(dbranch, out_weight).astype(jnp.bfloat16)
    delta = jnp.einsum("bqhd,bqhd->bhq", heads_of(dmixed).astype(jnp.float32), mixed)
    dqueries = query_gradient(queries, query_seg, starts, keys, values, dmixed, logsum, delta)
    dkeys, dvalues = key_gradient(keys, values, query_seg, starts, queries, dmixed, logsum, delta)
    dqueries = dqueries.reshape(tokens.shape).astype(jnp.bfloat16)
    dkeys = dkeys.reshape(tokens.shape).astype(jnp.bfloat16)
    dvalues = dvalues.reshape(tokens.shape).astype(jnp.bfloat16)
    tokens_grad = (
        dfirst_sum
        + project_back(dqueries, query_weight)
        + project_back(dkeys, key_weight)
        + project_back(dvalues, value_weight)
    )
    sums = (
        outer_sum(tokens, dqueries),
        row_sum(dqueries),
        outer_sum(tokens, dkeys),
        outer_sum(tokens, dvalues),
        row_sum(dvalues),
        outer_sum(mixed_low, dbranch),
        row_sum(dbranch),
        dgain_first,
        dshift_first,
        outer_sum(first_low, dinner),
        row_sum(dinner),
        outer_sum(active, douter),
        row_sum(douter),
        dgain_second,
        dshift_second,
    )
    return (tokens_grad, sums)


def general_device(
    tokens,
    doc_lengths,
    query_weight,
    query_bias,
    key_weight,
    value_weight,
    value_bias,
    out_weight,
    out_bias,
    first_gain,
    first_shift,
    inner_weight,
    inner_bias,
    outer_weight,
    outer_bias,
    second_gain,
    second_shift,
    cotangent,
):
    params = (
        query_weight,
        query_bias,
        key_weight,
        value_weight,
        value_bias,
        out_weight,
        out_bias,
        first_gain,
        first_shift,
        inner_weight,
        inner_bias,
        outer_weight,
        outer_bias,
        second_gain,
        second_shift,
    )
    rows = tokens.shape[2]
    base = lax.axis_index("ctx") * rows
    lengths = doc_lengths[:, 0]
    starts = jnp.cumsum(lengths, axis=-1) - lengths
    outputs = []
    token_parts = []
    sums = None
    for index in range(tokens.shape[0]):
        weights = (
            lax.all_gather(params[0], "wt", axis=0, tiled=True),
            lax.all_gather(params[1], "wt", axis=0, tiled=True),
            lax.all_gather(params[2], "wt", axis=0, tiled=True),
            lax.all_gather(params[3], "wt", axis=0, tiled=True),
            lax.all_gather(params[4], "wt", axis=0, tiled=True),
            lax.all_gather(params[5], "wt", axis=0, tiled=True),
            lax.all_gather(params[6], "wt", axis=0, tiled=True),
            lax.all_gather(params[7], "wt", axis=0, tiled=True),
            lax.all_gather(params[8], "wt", axis=0, tiled=True),
            lax.all_gather(params[9], "wt", axis=0, tiled=True),
            lax.all_gather(params[10], "wt", axis=0, tiled=True),
            lax.all_gather(params[11], "wt", axis=0, tiled=True),
            lax.all_gather(params[12], "wt", axis=0, tiled=True),
            lax.all_gather(params[13], "wt", axis=0, tiled=True),
            lax.all_gather(params[14], "wt", axis=0, tiled=True),
        )
        part_out, saved = forward_pass(
            tokens[index : index + 1, 0], starts[index : index + 1], weights, base
        )
        again = (
            lax.all_gather(params[0], "wt", axis=0, tiled=True),
            lax.all_gather(params[1], "wt", axis=0, tiled=True),
            lax.all_gather(params[2], "wt", axis=0, tiled=True),
            lax.all_gather(params[3], "wt", axis=0, tiled=True),
            lax.all_gather(params[4], "wt", axis=0, tiled=True),
            lax.all_gather(params[5], "wt", axis=0, tiled=True),
            lax.all_gather(params[6], "wt", axis=0, tiled=True),
            lax.all_gather(params[7], "wt", axis=0, tiled=True),
            lax.all_gather(params[8], "wt", axis=0, tiled=True),
            lax.all_gather(params[9], "wt", axis=0, tiled=True),
            lax.all_gather(params[10], "wt", axis=0, tiled=True),
            lax.all_gather(params[11], "wt", axis=0, tiled=True),
            lax.all_gather(params[12], "wt", axis=0, tiled=True),
            lax.all_gather(params[13], "wt", axis=0, tiled=True),
            lax.all_gather(params[14], "wt", axis=0, tiled=True),
        )
        part_grad, part_sums = backward_pass(
            saved, starts[index : index + 1], again, cotangent[index : index + 1, 0]
        )
        outputs.append(part_out)
        token_parts.append(part_grad)
        sums = part_sums if sums is None else jax.tree.map(jnp.add, sums, part_sums)
    output = jnp.concatenate(outputs, axis=0)
    tokens_grad = jnp.concatenate(token_parts, axis=0)
    shards = jax.tree.map(
        lambda part: part.astype(jnp.float32),
        lax.psum_scatter(for_sending(sums), "wt", scatter_dimension=0, tiled=True),
    )
    totals = lax.psum(shards, "ctx")
    return (output[:, None], tokens_grad[:, None]) + tuple(totals)


def flip(value, bits):
    return lax.ppermute(value, "ctx", [(i, i ^ bits) for i in range(8)])


def turn(value, step):
    return lax.ppermute(value, "wt", [(i, (i - step) % 4) for i in range(4)])


def pick(value, index, axis=0):
    return lax.dynamic_index_in_dim(value, index, axis, keepdims=False)


def pair(own, other, bit, axis=0):
    return jnp.where(bit == 0, jnp.stack([own, other], axis), jnp.stack([other, own], axis))


def short(value):
    return value.astype(jnp.bfloat16)


def wide(value):
    return value.astype(jnp.float32)


def dot(left, right):
    return jnp.dot(left, right, preferred_element_type=jnp.float32)


def dot_back(left, right):
    return lax.dot_general(
        left, right, (((1,), (1,)), ((), ())), preferred_element_type=jnp.float32
    )


def dot_sum(left, right):
    return lax.dot_general(
        left, right, (((0,), (0,)), ((), ())), preferred_element_type=jnp.float32
    )


def norm_parts(rows):
    mean = jnp.mean(rows, axis=-1, keepdims=True)
    centered = rows - mean
    spread = jnp.mean(centered * centered, axis=-1, keepdims=True)
    root = lax.rsqrt(spread + EPS)
    return centered * root, root


def norm_back(upstream, normed, root, gain):
    grad = upstream * gain
    mean = jnp.mean(grad, axis=-1, keepdims=True)
    along = jnp.mean(grad * normed, axis=-1, keepdims=True)
    return root * (grad - mean - normed * along)


def gelu_slope(inner):
    bell = jnp.exp(-0.5 * inner * inner) * (1.0 / math.sqrt(2.0 * math.pi))
    return 0.5 * (1.0 + lax.erf(inner * ROOT_HALF)) + inner * bell


def run(kernel, outs, args, scratch=(), scalars=()):
    shapes = tuple(jax.ShapeDtypeStruct(shape, dtype) for shape, dtype in outs)
    spaces = [pltpu.SMEM] * len(scalars) + [pltpu.VMEM] * len(args)
    return pl.pallas_call(
        kernel,
        out_shape=shapes,
        in_specs=[pl.BlockSpec(memory_space=space) for space in spaces],
        scratch_shapes=list(scratch),
    )(*scalars, *args)


BF = jnp.bfloat16
F32 = jnp.float32


def where_am_i():
    ctx, own = lax.axis_index("ctx"), lax.axis_index("wt")
    return ctx & 1, (ctx >> 1) & 3, ctx & 3, own


def some_rows(start, count):
    return pl.ds(pl.multiple_of(start, 16), count)


def prepare_kernel(wq, wk, wv, wo, wi, wo2, vec, heads_own, heads_send, w2_send, inner_half, outer_half):
    core, quarter, group, _ = where_am_i()
    shard, dim = wq.shape
    width, half = dim // 4, wo2.shape[0] // 2
    for index in range(4):

        @pl.when(group == index)
        def _():
            for slot, ref in enumerate((wq, wk, wv)):
                heads_own[:, slot * width : (slot + 1) * width] = ref[
                    :, index * width : (index + 1) * width
                ]

    for index in range(2):

        @pl.when(core == index)
        def _():
            for block in range(4):
                at = block * 2 * half + index * half
                inner_half[:, block * half : (block + 1) * half] = wi[:, at : at + half]
            outer_half[...] = wo2[index * half : (index + 1) * half, :]

    part = shard // 2
    heads_send[0:part, :] = heads_own[some_rows((quarter >> 1) * part, part), :]
    heads_send[part:, 0:width] = vec[...]
    heads_send[part:, width:] = jnp.zeros((16, 2 * width), BF)
    part = shard // 4
    rows = some_rows(quarter * part, part)
    w2_send[0:part, :] = inner_half[rows, 0:dim]
    w2_send[part : 2 * part, :] = inner_half[rows, dim:]
    step = half // 4
    w2_send[2 * part : 2 * part + step, :] = outer_half[some_rows(quarter * step, step), :]
    w2_send[2 * part + step :, :] = wo[rows, :]


CHUNK = 128
WINDOWS = (4, 6, 8)


def chunk_of(ctx, index):
    return ctx ^ ((index >> 2) | (index & 2) | ((index & 1) << 2))


def some_chunks(start, count):
    return pl.ds(pl.multiple_of(start * CHUNK, CHUNK), count * CHUNK)


def over_window(bounds, block, windows, visit):
    if len(windows) == 1:
        visit(pl.ds(0, windows[0] * CHUNK))
        return
    low, count = bounds[0, block], bounds[1, block]
    least = 0
    for size in windows:

        @pl.when((count > least) & (count <= size))
        def _(size=size):
            visit(some_chunks(jnp.minimum(low, windows[-1] - size), size))

        least = size


def attend_rows(qkv, seg_col, seg_row, far, outs, logsum, mixed):
    core, quarter, _, _ = where_am_i()
    scale = HEAD_DIM ** (-0.5)
    group = qkv.shape[0] // 3

    def step(side, carry):
        rows = some_chunks(2 * (2 * side + ((quarter & 1) ^ far)), 2)
        here = some_chunks(2 * side, 2)

        def one_head(head, carry):
            mask = seg_col[rows, :] == seg_row[...]
            scores = dot_back(qkv[head, rows, :], qkv[group + head])
            scores = jnp.where(mask, scores * scale, NEG)
            top = jnp.max(scores, axis=-1, keepdims=True)
            expd = jnp.exp(scores - top)
            total = jnp.sum(expd, axis=-1, keepdims=True)
            probs = short(expd * (1.0 / total))
            mixed[head, here, :] = short(dot(probs, qkv[2 * group + head]))
            lane = lax.broadcasted_iota(jnp.int32, (2 * CHUNK, 128), 1)
            logsum[here, :] = jnp.where(lane == head, top + jnp.log(total), logsum[here, :])
            return carry

        lax.fori_loop(0, group, one_head, 0)
        return carry

    logsum[...] = jnp.zeros_like(logsum)
    lax.fori_loop(0, 2, step, 0)
    y = quarter >> 1
    for index, out in enumerate(outs):
        for side in range(2):
            chunk = 2 * (y ^ side) + (core ^ index)
            for head in range(group):
                out[
                    side * CHUNK : (side + 1) * CHUNK, head * HEAD_DIM : (head + 1) * HEAD_DIM
                ] = mixed[head, some_chunks(chunk, 1), :]


def attend_near_kernel(
    mine, other, far, heads_own, g1, g2, g3, h1, h2, h3, bias, seg_col, seg_row,
    qkv, m0, m1, logsum, weight, mixed,
):
    _, quarter, _, own = where_am_i()
    ctx = lax.axis_index("ctx")
    shard = heads_own.shape[0]
    part = shard // 2
    y = quarter >> 1
    weight[some_rows(own * shard, shard), :] = heads_own[...]
    for step, near_half, far_half in ((1, g1, h1), (2, g2, h2), (3, g3, h3)):
        at = ((own + step) & 3) * shard
        weight[some_rows(at + part * y, part), :] = near_half[0:part, :]
        weight[some_rows(at + part * (1 - y), part), :] = far_half[0:part, :]
    index = 0
    for source in (mine, other, far):
        for first in range(0, source.shape[0], 2 * CHUNK):
            low = short(dot(source[first : first + 2 * CHUNK, :], weight[...]) + bias[...])
            for half in range(2):
                at = pl.multiple_of(chunk_of(ctx, index) * CHUNK, CHUNK)
                for slot in range(qkv.shape[0]):
                    qkv[slot, pl.ds(at, CHUNK), :] = low[
                        half * CHUNK : (half + 1) * CHUNK,
                        slot * HEAD_DIM : (slot + 1) * HEAD_DIM,
                    ]
                index += 1
    attend_rows(qkv, seg_col, seg_row, 0, (m0, m1), logsum, mixed)


def attend_far_kernel(qkv, seg_col, seg_row, m2, m3, logsum, mixed):
    attend_rows(qkv, seg_col, seg_row, 1, (m2, m3), logsum, mixed)


def project_kernel(m0, m1, m2, m3, mine, wo, vec, *refs):
    pieces, (first_sum, first_low, out_full) = refs[:12], refs[12:]
    _, quarter, group, own = where_am_i()
    shard = wo.shape[0]
    part = shard // 4
    out_full[some_rows(own * shard, shard), :] = wo[...]
    for index, piece in enumerate(pieces):
        at = ((own + 1 + index // 4) & 3) * shard + part * (quarter ^ (index % 4))
        out_full[some_rows(at, part), :] = piece[piece.shape[0] - part :, :]
    total = wide(mine[...]) + vec[2:3, :]
    for code, ref in enumerate((m0, m1, m2, m3)):
        total += dot(ref[...], out_full[some_rows((group ^ code) * shard, shard), :])
    first_sum[...] = total
    first_low[...] = short(norm_parts(total)[0] * vec[3:4, :] + vec[4:5, :])


def forward_kernel(near, far, inner_half, outer_half, bias, *refs):
    pieces, (keep, send, inner, active, wi_full, wo2_full) = refs[:12], refs[12:]
    _, quarter, _, own = where_am_i()
    shard, half = inner_half.shape[0], outer_half.shape[0]
    dim = keep.shape[1]
    part, step = shard // 4, half // 4
    wi_full[some_rows(own * shard, shard), :] = inner_half[...]
    wo2_full[some_rows(own * half, half), :] = outer_half[...]
    for index, piece in enumerate(pieces):
        row, spot = (own + 1 + index // 4) & 3, quarter ^ (index % 4)
        rows = some_rows(row * shard + part * spot, part)
        wi_full[rows, 0:dim] = piece[0:part, :]
        wi_full[rows, dim:] = piece[part : 2 * part, :]
        wo2_full[some_rows(row * half + step * spot, step), :] = piece[
            2 * part : 2 * part + step, :
        ]
    count = near.shape[0]
    chunk = 512
    for index, (source, out) in enumerate(((far, send), (near, keep))):
        at = (1 - index) * count
        total = None
        for lane in range(0, inner.shape[1], chunk):
            lanes = slice(lane, lane + chunk)
            value = dot(source[...], wi_full[:, lanes]) + bias[:, lanes]
            inner[at : at + count, lanes] = value
            low = short(gelu(value))
            active[at : at + count, lanes] = low
            added = dot(low, wo2_full[lanes, :])
            total = added if total is None else total + added
        out[...] = total


def turnaround_kernel(first_sum, keep, got, vec, cot0, cot1, out0, out1, dsecond, douter, sums):
    rows = cot0.shape[0]
    first = norm_parts(first_sum[...])[0] * vec[3:4, :] + vec[4:5, :]
    normed, root = norm_parts(first + vec[5:6, :] + keep[...] + got[...])
    output = short(normed * vec[6:7, :] + vec[7:8, :])
    out0[...] = output[:rows]
    out1[...] = output[rows:]
    upstream = jnp.concatenate([wide(cot0[...]), wide(cot1[...])])
    back = norm_back(upstream, normed, root, vec[6:7, :])
    low = short(back)
    dsecond[...] = back
    douter[...] = low
    sums[0:1, :] = jnp.sum(wide(low), axis=0, keepdims=True)
    sums[1:2, :] = jnp.sum(upstream * normed, axis=0, keepdims=True)
    sums[2:3, :] = jnp.sum(upstream, axis=0, keepdims=True)
    sums[3:, :] = jnp.zeros_like(sums[3:, :])


def backward_kernel(near, far, inner, wi_full, wo2_full, keep, send, dinner, sums):
    count, dim = near.shape
    chunk = 512
    for index, (source, out) in enumerate(((far, send), (near, keep))):
        at = (1 - index) * count
        total = None
        for lane in range(0, inner.shape[1], chunk):
            lanes = slice(lane, lane + chunk)
            slope = gelu_slope(inner[at : at + count, lanes])
            low = short(dot_back(source[...], wo2_full[lanes, :]) * slope)
            dinner[at : at + count, lanes] = low
            added = dot_back(low, wi_full[:, lanes])
            total = added if total is None else total + added
        out[...] = total
    total = jnp.sum(wide(dinner[...]), axis=0, keepdims=True)
    sums[0:1, :] = total[:, :dim]
    sums[1:2, :] = total[:, dim:]
    sums[2:, :] = jnp.zeros_like(sums[2:, :])


def weights_kernel(first0, first1, douter0, douter1, dinner, active, ak, az, bk, bz, left, right):
    _, quarter, _, _ = where_am_i()
    x, y = quarter & 1, quarter >> 1
    count = first0.shape[0]
    part, step = first0.shape[1] // 16, active.shape[1] // 16
    left[...] = short(dot_sum(first0[...], dinner[:count]) + dot_sum(first1[...], dinner[count:]))
    for block in range(8):
        rows = slice(block * part, (block + 1) * part)
        ak[rows, :] = left[some_rows((2 * block + x) * part, part), :]
        az[rows, :] = left[some_rows((2 * block + 1 - x) * part, part), :]
    right[...] = short(
        dot_sum(active[:count], douter0[...]) + dot_sum(active[count:], douter1[...])
    )
    for block in range(8):
        row, side = block // 2, block % 2
        rows = slice(block * step, (block + 1) * step)
        bk[rows, :] = right[some_rows((4 * row + 2 * y + side) * step, step), :]
        bz[rows, :] = right[some_rows((4 * row + 2 * (1 - y) + side) * step, step), :]


def branch_kernel(first_sum, dsecond, keep, got, vec, out_full, dfirst_sum, dbranch, d0, d1, d2, d3, sums):
    _, _, group, _ = where_am_i()
    shard = d0.shape[1]
    normed, root = norm_parts(first_sum[...])
    dfirst = dsecond[...] + keep[...] + got[...]
    back = norm_back(dfirst, normed, root, vec[3:4, :])
    low = short(back)
    dfirst_sum[...] = back
    dbranch[...] = low
    for code, ref in enumerate((d0, d1, d2, d3)):
        ref[...] = short(dot_back(low, out_full[some_rows((group ^ code) * shard, shard), :]))
    sums[0:1, :] = jnp.sum(wide(low), axis=0, keepdims=True)
    sums[1:2, :] = jnp.sum(dfirst * normed, axis=0, keepdims=True)
    sums[2:3, :] = jnp.sum(dfirst, axis=0, keepdims=True)
    sums[3:, :] = jnp.zeros_like(sums[3:, :])


def out_weight_kernel(m0, m1, m2, m3, dbranch, sums1, sums2, sums3, ck, cz, whole):
    core, _, group, _ = where_am_i()
    shard, dim = m0.shape[1], dbranch.shape[1]
    half = dim // 2
    for code, ref in enumerate((m0, m1, m2, m3)):
        whole[some_rows((group ^ code) * shard, shard), :] = short(
            dot_sum(ref[...], dbranch[...])
        )
    for side in range(2):

        @pl.when(core == side)
        def _():
            for ref, which in ((ck, side), (cz, 1 - side)):
                ref[0:dim, :] = whole[:, which * half : (which + 1) * half]

    rows = short(
        jnp.concatenate([sums1[0:3, :], sums2[0:3, :], sums3[0:2, :], jnp.zeros_like(sums1[...])])
    )
    for ref in (ck, cz):
        ref[dim : dim + 16, :] = rows[:, :half]
        ref[dim + 16 :, :] = rows[:, half:]


def out_split_kernel(packed, got, ck, cz):
    core, quarter, _, _ = where_am_i()
    x = quarter & 1
    dim = packed.shape[0] - 32
    part = dim // 16
    for block in range(8):
        rows = slice(block * part, (block + 1) * part)
        for ref, side in ((ck, x), (cz, 1 - x)):
            take = some_rows((2 * block + side) * part, part)
            ref[rows, :] = short(wide(packed[take, :]) + wide(got[take, :]))
    for lanes in range(2):
        at = dim + 16 * lanes
        mine, other = wide(packed[at : at + 16, :]), wide(got[at : at + 16, :])
        low = jnp.where(core == 0, mine, other)[6:8]
        high = jnp.where(core == 0, other, mine)[6:8]
        rows = jnp.concatenate([(mine + other)[0:6], low, high, jnp.zeros_like(mine[0:6])])
        at = 8 * part + 16 * lanes
        for ref in (ck, cz):
            ref[at : at + 16, :] = short(rows)


def reduce_rows(keep, got, outs, bit):
    size = keep.shape[0] // 8
    size -= size % 16
    width = keep.shape[1] // len(outs)
    for lane, pair_of in enumerate(outs):
        lanes = slice(lane * width, (lane + 1) * width)
        for block in range(4):
            for out, side in zip(pair_of, (bit, 1 - bit)):
                take = some_rows((2 * block + side) * size, size)
                out[block * size : (block + 1) * size, :] = short(
                    wide(keep[take, lanes]) + wide(got[take, lanes])
                )
        if keep.shape[0] > 8 * size:
            for out in pair_of:
                out[4 * size :, :] = short(
                    wide(keep[8 * size :, lanes]) + wide(got[8 * size :, lanes])
                )


def reduce_kernel(ak, ar, bk, br, *outs):
    _, quarter, _, _ = where_am_i()
    reduce_rows(ak, ar, (outs[0:2], outs[4:6]), quarter >> 1)
    reduce_rows(bk, br, (outs[2:4], outs[6:8]), quarter & 1)


def reduce_out_kernel(ck, cr, c2k, c2z):
    _, quarter, _, _ = where_am_i()
    reduce_rows(ck, cr, ((c2k, c2z),), quarter >> 1)


def owners_kernel(*refs):
    inputs, outs = refs[:-4], refs[-4:]
    _, _, _, own = where_am_i()
    ak, ar, bk, br = inputs[:4]
    half = bk.shape[1]
    part = ak.shape[0] // 4
    for index, out in enumerate(outs):
        row = (own - index) & 3
        rows = some_rows(row * part, part)
        out[0:part, :] = (wide(ak[rows, :]) + wide(ar[rows, :])).astype(out.dtype)
        for side in range(2):
            rows = some_rows((2 * row + side) * part, part)
            out[part : 2 * part, side * half : (side + 1) * half] = (
                wide(bk[rows, :]) + wide(br[rows, :])
            ).astype(out.dtype)
        if len(inputs) > 4:
            ck, cr = inputs[4:]
            at = 2 * part
            rows = some_rows(row * part, part)
            out[at:, 0:half] = (wide(ck[rows, :]) + wide(cr[rows, :])).astype(out.dtype)
            tail = wide(ck[4 * part :, :]) + wide(cr[4 * part :, :])
            out[at : at + 32, half:] = tail.astype(out.dtype)
            out[at + 32 :, half:] = jnp.zeros((part - 32, half), out.dtype)


def total_kernel(mine, *refs):
    total = wide(mine[...])
    for ref in refs[:-1]:
        total += wide(ref[...])
    refs[-1][...] = short(total)


def finish_kernel(*refs):
    pieces, (dwi, dwo2, dwo, small) = refs[:16], refs[16:]
    core, quarter, _, _ = where_am_i()
    part, half = dwi.shape[0] // 4, dwi.shape[1] // 8
    for side in range(2):

        @pl.when(core == side)
        def _():
            for index, piece in enumerate(pieces):
                lane, index = index // 8, index % 8
                spot = quarter ^ (index % 4)
                which = side if index < 4 else 1 - side
                rows = some_rows(spot * part, part)
                for block in range(2):
                    at = (2 * lane + block) * 2 * half + which * half
                    dwi[rows, at : at + half] = wide(piece[0:part, block * half : (block + 1) * half])
                    at = which * half + spot * 2 * part + block * part
                    dwo2[some_rows(at, part), lane * half : (lane + 1) * half] = wide(
                        piece[part : 2 * part, block * half : (block + 1) * half]
                    )
                if lane == 1:
                    dwo[rows, which * half : (which + 1) * half] = wide(piece[2 * part :, 0:half])

    last = pieces[8]
    small[:, 0:half] = wide(last[2 * part : 2 * part + 16, half:])
    small[:, half:] = wide(last[2 * part + 16 : 2 * part + 32, half:])


def attend_back_kernel(
    bounds, qkv, logsum0, logsum1, seg_col, seg_row, p0, p1, p2, p3, mine, other, far, weight,
    h0, h1, h2, h3, keep, send, grads, dqueries, dkeys, dvalues, dweight, dmixed, logsum, whole,
):
    _, quarter, _, own = where_am_i()
    ctx = lax.axis_index("ctx")
    x = quarter & 1
    scale = HEAD_DIM ** (-0.5)
    group = qkv.shape[0] // 3
    width = group * HEAD_DIM
    block = p0.shape[0]
    dkeys[...] = jnp.zeros_like(dkeys)
    dvalues[...] = jnp.zeros_like(dvalues)
    for index, part in enumerate((p0, p2, p1, p3)):
        for side in range(2):
            chunk = chunk_of(ctx, 2 * index + side)
            for head in range(group):
                dmixed[head, some_chunks(chunk, 1), :] = part[
                    side * CHUNK : (side + 1) * CHUNK, head * HEAD_DIM : (head + 1) * HEAD_DIM
                ]
    for side in range(2):
        rows = slice(2 * side * CHUNK, 2 * (side + 1) * CHUNK)
        logsum[some_chunks(2 * (2 * side + x), 2), :] = logsum0[rows, :]
        logsum[some_chunks(2 * (2 * side + 1 - x), 2), :] = logsum1[rows, :]

    def step(index, carry):
        rows = some_chunks(2 * index, 2)

        def visit(window):
            def one_head(head, carry):
                mask = seg_col[rows, :] == seg_row[:, window]
                query = qkv[head, rows, :]
                grad = dmixed[head, rows, :]
                keys = qkv[group + head, window, :]
                lane = lax.broadcasted_iota(jnp.int32, (2 * CHUNK, 128), 1)
                sums = jnp.sum(
                    jnp.where(lane == head, logsum[rows, :], 0.0), axis=-1, keepdims=True
                )
                scores = jnp.where(mask, dot_back(query, keys) * scale, NEG)
                probs = jnp.exp(scores - sums)
                dprobs = dot_back(grad, qkv[2 * group + head, window, :])
                delta = jnp.sum(probs * dprobs, axis=-1, keepdims=True)
                dscores = short(probs * (dprobs - delta))
                dqueries[head, rows, :] = short(dot(dscores, keys) * scale)
                dkeys[head, window, :] += dot_sum(dscores, query)
                dvalues[head, window, :] += dot_sum(short(probs), grad)
                return carry

            lax.fori_loop(0, group, one_head, 0)

        over_window(bounds, index, WINDOWS, visit)
        return carry

    lax.fori_loop(0, 4, step, 0)
    for head in range(group):
        whole[:, head * HEAD_DIM : (head + 1) * HEAD_DIM] = dqueries[head]
        at = width + head * HEAD_DIM
        whole[:, at : at + HEAD_DIM] = short(dkeys[head] * scale)
        whole[:, at + width : at + width + HEAD_DIM] = short(dvalues[head])
    for index in range(8):
        grads[index * CHUNK : (index + 1) * CHUNK, :] = whole[
            some_chunks(chunk_of(ctx, index), 1), :
        ]
    rows = 2 * block
    dweight[...] = (
        dot_sum(mine[...], grads[:block])
        + dot_sum(other[...], grads[block:rows])
        + dot_sum(far[...], grads[rows:])
    )
    sums = jnp.sum(wide(grads[...]), axis=0, keepdims=True)
    tail = jnp.concatenate([sums, jnp.zeros((15, sums.shape[1]), F32)])
    for index, out in enumerate((h0, h1, h2, h3)):
        take = pl.ds(pl.multiple_of(((own - index) & 3) * width, 16), width)
        out[0:width, :] = dweight[take, :].astype(out.dtype)
        out[width:, :] = tail.astype(out.dtype)
    keep[...] = dot_back(grads[:rows], weight[...])
    send[...] = short(dot_back(grads[rows:], weight[...]))


def merge_kernel(keep, got, base, near, far):
    total = keep[...] + wide(got[...])
    count = near.shape[0]
    near[...] = total[:count] + base[...]
    far[...] = short(total[count:])


def heads_kernel(s0, s1, s2, s3, dq, dk, dv, bias):
    _, _, group, own = where_am_i()
    shard = dq.shape[0]
    for index in range(4):

        @pl.when(group == index)
        def _():
            for code, ref in enumerate((s0, s1, s2, s3)):
                at = (index ^ code) * shard
                for slot, out in enumerate((dq, dk, dv)):
                    out[:, at : at + shard] = wide(
                        ref[0:shard, slot * shard : (slot + 1) * shard]
                    )

                @pl.when(own == index ^ code)
                def _():
                    bias[...] = wide(ref[shard:, :])


def plane_steps(
    tokens,
    doc_lengths,
    query_weight,
    query_bias,
    key_weight,
    value_weight,
    value_bias,
    out_weight,
    out_bias,
    first_gain,
    first_shift,
    inner_weight,
    inner_bias,
    outer_weight,
    outer_bias,
    second_gain,
    second_shift,
    cotangent,
):
    ctx, own = lax.axis_index("ctx"), lax.axis_index("wt")
    core, y, group = ctx & 1, ctx >> 2, ctx & 3
    rows, dim = tokens.shape[2], tokens.shape[3]
    shard = query_weight.shape[0]
    hidden = outer_weight.shape[0]
    half = hidden // 2
    count = 2 * rows

    mine = jnp.concatenate([pick(tokens[:, 0], y), flip(pick(tokens[:, 0], 1 - y), 4)])
    other = flip(mine, 2)
    far = flip(jnp.concatenate([mine, other]), 1)

    vector_list = (
        query_bias,
        value_bias,
        out_bias,
        first_gain,
        first_shift,
        outer_bias,
        second_gain,
        second_shift,
        *[inner_bias[at : at + shard] for at in range(0, 4 * shard, shard)],
    )
    line = lax.broadcasted_iota(jnp.int32, (16, shard), 0)
    vec = jnp.zeros((16, shard), BF)
    for index, value in enumerate(vector_list):
        vec = jnp.where(line == index, value[None, :], vec)
    heads_own, heads_send, w2_send, inner_half, outer_half = run(
        prepare_kernel,
        [
            ((shard, 3 * shard), BF),
            ((shard // 2 + 16, 3 * shard), BF),
            ((shard // 4 * 3 + half // 4, dim), BF),
            ((shard, 4 * half), BF),
            ((half, dim), BF),
        ],
        (query_weight, key_weight, value_weight, out_weight, inner_weight, outer_weight, vec),
    )
    got = [turn(heads_send, step) for step in (1, 2, 3)]
    gone = [flip(value, 4) for value in got]
    pieces = []
    for step in (1, 2, 3):
        piece = turn(w2_send, step)
        pieces += [piece] + [flip(piece, bits) for bits in (2, 4, 6)]

    at = shard // 2
    rel = jnp.stack([vec] + [value[at:, :shard] for value in got])
    vectors = wide(lax.dynamic_slice_in_dim(jnp.concatenate([rel, rel]), (4 - own) % 4, 4))
    mine_b = pick(vectors, group)
    heads_bias = jnp.concatenate([mine_b[0], jnp.zeros_like(mine_b[0]), mine_b[1]])[None]
    inner_b = pick(vectors[:, 8:12].reshape(4, 2, half), core, 1).reshape(1, 4 * half)
    vectors = jnp.swapaxes(vectors[:, :8], 0, 1).reshape(8, dim)

    lengths = pick(doc_lengths[:, 0], y)
    starts = jnp.cumsum(lengths) - lengths
    total = 8 * rows
    positions = jnp.arange(total, dtype=jnp.int32)
    seg = jnp.sum((starts[None, :] <= positions[:, None]).astype(jnp.int32), axis=-1) - 1
    segs = (seg[:, None], seg[None, :])
    first = jnp.arange(4, dtype=jnp.int32)[:, None] * (2 * CHUNK)
    low = jnp.max(jnp.where(starts[None, :] <= first, starts[None, :], 0), axis=-1) // CHUNK
    ends = jnp.where(starts[None, :] >= first + 2 * CHUNK, starts[None, :], total)
    bounds = jnp.stack([low, (jnp.min(ends, axis=-1) - 1) // CHUNK - low + 1])

    qkv, m0, m1, logsum0, heads_weight = run(
        attend_near_kernel,
        [
            ((9, total, HEAD_DIM), BF),
            ((count, shard), BF),
            ((count, shard), BF),
            ((2 * count, 128), F32),
            ((dim, 3 * shard), BF),
        ],
        (mine, other, far, heads_own, *got, *gone, heads_bias, *segs),
        [pltpu.VMEM((3, 2 * count, HEAD_DIM), BF)],
    )
    m2, m3, logsum1 = run(
        attend_far_kernel,
        [((count, shard), BF), ((count, shard), BF), ((2 * count, 128), F32)],
        (qkv, *segs),
        [pltpu.VMEM((3, 2 * count, HEAD_DIM), BF)],
    )
    mixed = [m0, flip(m1, 1), flip(m2, 2), flip(m3, 3)]

    first_sum, first_low, out_full = run(
        project_kernel,
        [((count, dim), F32), ((count, dim), BF), ((dim, dim), BF)],
        (*mixed, mine, out_weight, vectors, *pieces),
    )
    first_far = flip(first_low, 1)
    keep, send, inner, active, wi_full, wo2_full = run(
        forward_kernel,
        [
            ((count, dim), F32),
            ((count, dim), F32),
            ((2 * count, 4 * half), F32),
            ((2 * count, 4 * half), BF),
            ((dim, 4 * half), BF),
            ((4 * half, dim), BF),
        ],
        (first_low, first_far, inner_half, outer_half, inner_b, *pieces),
    )
    cot = pick(cotangent[:, 0], y), flip(pick(cotangent[:, 0], 1 - y), 4)
    out0, out1, dsecond, douter, sums2 = run(
        turnaround_kernel,
        [
            ((rows, dim), BF),
            ((rows, dim), BF),
            ((count, dim), F32),
            ((count, dim), BF),
            ((8, dim), F32),
        ],
        (first_sum, keep, flip(send, 1), vectors, *cot),
    )
    output = pair(out0, flip(out1, 4), y)

    douter_far = flip(douter, 1)
    keep, send, dinner, sums3 = run(
        backward_kernel,
        [
            ((count, dim), F32),
            ((count, dim), F32),
            ((2 * count, 4 * half), BF),
            ((8, dim), F32),
        ],
        (douter, douter_far, inner, wi_full, wo2_full),
    )
    dfirst_sum, dbranch, d0, d1, d2, d3, sums1 = run(
        branch_kernel,
        [((count, dim), F32), ((count, dim), BF)] + [((count, shard), BF)] * 4 + [((8, dim), F32)],
        (first_sum, dsecond, keep, flip(send, 1), vectors, out_full),
    )
    dmixed = [d0, flip(d1, 1), flip(d2, 2), flip(d3, 3)]

    ak, az, bk, bz = run(
        weights_kernel,
        [((dim // 2, 4 * half), BF)] * 2 + [((2 * half, dim), BF)] * 2,
        (first_low, first_far, douter, douter_far, dinner, active),
        [pltpu.VMEM((dim, 4 * half), BF), pltpu.VMEM((4 * half, dim), BF)],
    )
    ar, br = flip(az, 2), flip(bz, 4)
    ck, cz = run(
        out_weight_kernel,
        [((dim + 32, dim // 2), BF)] * 2,
        (*mixed, dbranch, sums1, sums2, sums3),
        [pltpu.VMEM((dim, dim), BF)],
    )
    ck, cz = run(out_split_kernel, [((dim // 2 + 32, dim // 2), BF)] * 2, (ck, flip(cz, 1)))
    cr = flip(cz, 2)

    h0, h1, h2, h3, keep, send = run(
        attend_back_kernel,
        [((shard + 16, 3 * shard), F32)]
        + [((shard + 16, 3 * shard), BF)] * 3
        + [((2 * count, dim), F32), ((2 * count, dim), BF)],
        (qkv, logsum0, logsum1, *segs, *dmixed, mine, other, far, heads_weight),
        [
            pltpu.VMEM((4 * count, 3 * shard), BF),
            pltpu.VMEM((3, 4 * count, HEAD_DIM), BF),
            pltpu.VMEM((3, 4 * count, HEAD_DIM), F32),
            pltpu.VMEM((3, 4 * count, HEAD_DIM), F32),
            pltpu.VMEM((dim, 3 * shard), F32),
            pltpu.VMEM((3, total, HEAD_DIM), BF),
            pltpu.VMEM((total, 128), F32),
            pltpu.VMEM((total, 3 * shard), BF),
        ],
        scalars=(bounds,),
    )

    c2k, c2z = run(reduce_out_kernel, [((dim // 4 + 32, dim // 2), BF)] * 2, (ck, cr))
    reduced = run(
        reduce_kernel,
        ([((dim // 4, 2 * half), BF)] * 2 + [((half, dim // 2), BF)] * 2) * 2,
        (ak, ar, bk, br),
    )
    plane = []
    for lane in range(2):
        a2k, a2z, b2k, b2z = reduced[4 * lane : 4 * lane + 4]
        last = [a2k, flip(a2z, 4), b2k, flip(b2z, 2)]
        size = shard // 4 * 2
        if lane == 1:
            last += [c2k, flip(c2z, 4)]
            size = shard // 4 * 3
        p0, p1, p2, p3 = run(owners_kernel, [((size, dim), F32)] + [((size, dim), BF)] * 3, last)
        turned = [turn(p, step) for step, p in ((1, p1), (2, p2), (3, p3))]
        (piece,) = run(total_kernel, [((size, dim), BF)], (p0, *turned))
        near = [piece] + [flip(piece, bits) for bits in (2, 4, 6)]
        plane += near + [flip(p, 1) for p in near]
    dinner_w, douter_w, dout_w, small = run(
        finish_kernel,
        [((shard, 8 * half), F32), ((hidden, dim), F32), ((shard, dim), F32), ((16, dim), F32)],
        plane,
    )
    dinner_b = pick(small[6:10].reshape(2, 4, half), own, 1).reshape(hidden)
    small = lax.dynamic_slice_in_dim(small[:6], own * shard, shard, 1)

    (heads,) = run(
        total_kernel, [((shard + 16, 3 * shard), BF)], (h0, turn(h1, 1), turn(h2, 2), turn(h3, 3))
    )
    (heads,) = run(total_kernel, [((shard + 16, 3 * shard), BF)], (heads, flip(heads, 4)))
    dquery_w, dkey_w, dvalue_w, heads_b = run(
        heads_kernel,
        [((shard, dim), F32)] * 3 + [((16, 3 * shard), F32)],
        (heads, flip(heads, 1), flip(heads, 2), flip(heads, 3)),
    )

    near_t, far_t = run(
        merge_kernel, [((count, dim), F32), ((count, dim), BF)], (keep, flip(send, 1), dfirst_sum)
    )
    dtokens = near_t + wide(flip(far_t, 2))
    tokens_grad = pair(dtokens[:rows], wide(flip(short(dtokens[rows:]), 4)), y)

    return (
        output[:, None],
        tokens_grad[:, None],
        dquery_w,
        heads_b[0, :shard],
        dkey_w,
        dvalue_w,
        heads_b[0, 2 * shard :],
        dout_w,
        small[0],
        small[1],
        small[2],
        dinner_w,
        dinner_b,
        douter_w,
        small[3],
        small[4],
        small[5],
    )


def plane_device(*args):
    return plane_steps(*args)


def solution(mesh):
    placed = (
        P(None, "wt", "ctx", None),
        P(None, "wt", None),
        P("wt", None),
        P("wt"),
        P("wt", None),
        P("wt", None),
        P("wt"),
        P("wt", None),
        P("wt"),
        P("wt"),
        P("wt"),
        P("wt", None),
        P("wt"),
        P("wt", None),
        P("wt"),
        P("wt"),
        P("wt"),
        P(None, "wt", "ctx", None),
    )
    fits = mesh.shape["ctx"] == 8 and mesh.shape["wt"] == 4
    return jax.shard_map(
        plane_device if fits else general_device,
        mesh=mesh,
        in_specs=placed,
        out_specs=(
            P(None, "wt", "ctx", None),
            P(None, "wt", "ctx", None),
            P("wt", None),
            P("wt"),
            P("wt", None),
            P("wt", None),
            P("wt"),
            P("wt", None),
            P("wt"),
            P("wt"),
            P("wt"),
            P("wt", None),
            P("wt"),
            P("wt", None),
            P("wt"),
            P("wt"),
            P("wt"),
        ),
        check_vma=False,
    )
```

profile of v0, /device:TPU:0, one launch (start us, length us, event | category | flops | bytes accessed | tf_op | source)
XLA Modules:
  0.0 350.5 jit_solution(15465411300258374255)
XLA Ops:
  3.2 3.5 %shard_map.305 = (bf16[192,576]{1,0:T(8,128)(2,1)}, bf16[112,576]{1,0:T(8,128)(2,1)}, bf16[240,768]{1,0:T(8,128)(2,1)}, bf16[192,1536]{1,0:T(8,128)(2,1)}, bf16[384,768]{1,0:T(8,128)(2,1)}) custom-call(bf16[192,768]{1,0:T(8,128)(2,1)} %wq.1, bf16[192,768]{1,0:T(8,128)(2,1)} %wk.1, bf16[192,768]{1,0:T(8,128)(2,1)} %wv.1, bf16[192,768]{1,0:T(8,128)(2,1)} %wo.3, ...), custom_call_target="tpu_custom_call" | custom-call | tf_op jit(solution)/shard_map/pallas_call | solution.py:566
  6.7 5.1 %collective-permute-start.3 = (bf16[112,576]{1,0:T(8,128)(2,1)}, bf16[112,576]{1,0:T(8,128)(2,1)S(1)}, u32[]{:S(2)}, u32[]{:S(2)}) collective-permute-start(bf16[112,576]{1,0:T(8,128)(2,1)} %get-tuple-element.98), channel_id=1, source_target_pairs={{0,3},{1,0},{2,1},{3,2},{4,7},{5,4},{6,5},{7,6},{8,11},{9,8},{10,9... | collective-permute-start | bytes 387080 | tf_op jit(solution)/shard_map/ppermute | solution.py:508
  12.8 2.8 collective-permute-start.12
  18.5 6.4 %collective-permute-done.4.g2 = bf16[112,576]{1,0:T(8,128)(2,1)S(1)} collective-permute-done((bf16[112,576]{1,0:T(8,128)(2,1)}, bf16[112,576]{1,0:T(8,128)(2,1)S(1)}, u32[]{:S(2)}, u32[]{:S(2)}) %collective-permute-start.4) | collective-permute-done | bytes 129056 | tf_op jit(solution)/shard_map/ppermute | solution.py:508
  24.9 1.5 collective-permute-start
  26.5 4.1 %collective-permute-done = bf16[128,768]{1,0:T(8,128)(2,1)S(1)} collective-permute-done((bf16[128,768]{1,0:T(8,128)(2,1)S(1)}, bf16[128,768]{1,0:T(8,128)(2,1)S(1)}, u32[]{:S(2)}, u32[]{:S(2)}) %collective-permute-start) | collective-permute-done | bytes 196640 | tf_op jit(solution)/shard_map/ppermute | solution.py:504
  30.6 1.5 collective-permute-start.6
  32.2 1.5 collective-permute-start.1
  33.8 2.6 collective-permute-done.6.h1
  36.4 1.5 collective-permute-start.7
  37.9 3.2 collective-permute-done.1.other
  41.5 1.5 collective-permute-start.13
  43.0 1.9 collective-permute-start.14
  44.9 4.0 %collective-permute-done.8.h3 = bf16[112,576]{1,0:T(8,128)(2,1)S(1)} collective-permute-done((bf16[112,576]{1,0:T(8,128)(2,1)S(1)}, bf16[112,576]{1,0:T(8,128)(2,1)S(1)}, u32[]{:S(2)}, u32[]{:S(2)}) %collective-permute-start.8) | collective-permute-done | bytes 129056 | tf_op jit(solution)/shard_map/ppermute | solution.py:504
  50.3 5.5 %collective-permute-done.16.refs_4_ = bf16[240,768]{1,0:T(8,128)(2,1)S(1)} collective-permute-done((bf16[240,768]{1,0:T(8,128)(2,1)}, bf16[240,768]{1,0:T(8,128)(2,1)S(1)}, u32[]{:S(2)}, u32[]{:S(2)}) %collective-permute-start.16) | collective-permute-done | bytes 368672 | tf_op jit(solution)/shard_map/ppermute | solution.py:508
  58.7 1.5 collective-permute-start.18
  60.4 1.6 collective-permute-start.19
  63.3 4.7 %collective-permute-done.17.refs_5_ = bf16[240,768]{1,0:T(8,128)(2,1)S(1)} collective-permute-done((bf16[240,768]{1,0:T(8,128)(2,1)S(1)}, bf16[240,768]{1,0:T(8,128)(2,1)S(1)}, u32[]{:S(2)}, u32[]{:S(2)}) %collective-permute-start.17) | collective-permute-done | bytes 368672 | tf_op jit(solution)/shard_map/ppermute | solution.py:504
  68.0 1.5 collective-permute-start.22
  71.8 10.4 %shard_map.306 = (bf16[9,1024,64]{2,1,0:T(8,128)(2,1)}, bf16[256,192]{1,0:T(8,128)(2,1)}, bf16[256,192]{1,0:T(8,128)(2,1)}, f32[512,128]{1,0:T(8,128)}, bf16[768,576]{1,0:T(8,128)(2,1)}) custom-call(bf16[256,768]{1,0:T(8,128)(2,1)} %copy-done, bf16[256,768]{1,0:T(8,128)(2,1)} %copy-done.1, bf16[512,768]{1,0:T(8,128)(2,1)} %copy-done.2, ...), custom_call_target="tpu_custom_call" | custom-call | tf_op jit(solution)/shard_map/pallas_call | solution.py:566
  82.2 7.9 %shard_map.307 = (bf16[256,192]{1,0:T(8,128)(2,1)}, bf16[256,192]{1,0:T(8,128)(2,1)}, f32[512,128]{1,0:T(8,128)}) custom-call(bf16[9,1024,64]{2,1,0:T(8,128)(2,1)} %get-tuple-element.101.qkv, s32[1024,1]{1,0:T(8,128)} %copy.45.seg_col, s32[1,1024]{1,0:T(1,128)} %bitcast.75), custom_call_target="tpu_custom_call" | custom-call | tf_op jit(solution)/shard_map/pallas_call | solution.py:566
  90.7 1.6 collective-permute-start.9
  93.3 3.4 collective-permute-done.10.m2
  97.4 4.7 %shard_map.308 = (f32[256,768]{1,0:T(8,128)}, bf16[256,768]{1,0:T(8,128)(2,1)}, bf16[768,768]{1,0:T(8,128)(2,1)}) custom-call(bf16[256,192]{1,0:T(8,128)(2,1)} %get-tuple-element.99.m0, bf16[256,192]{1,0:T(8,128)(2,1)} %copy-done.20, bf16[256,192]{1,0:T(8,128)(2,1)} %copy-done.18, bf16[256,192]{1,0:T(8,128)(2,1)} %copy-done.19, bf16[256,768]{1,0:T(8,128)(2,1)} %copy-done, ...), custom_call_target="tpu_custom_call" | custom-call | tf_op jit(solution)/shard_map/pallas_call | solution.py:566
  105.6 9.8 %shard_map.309 = (f32[256,768]{1,0:T(8,128)}, f32[256,768]{1,0:T(8,128)}, f32[512,1536]{1,0:T(8,128)}, bf16[512,1536]{1,0:T(8,128)(2,1)}, bf16[768,1536]{1,0:T(8,128)(2,1)}, /*index=5*/bf16[1536,768]{1,0:T(8,128)(2,1)}) custom-call(bf16[256,768]{1,0:T(8,128)(2,1)} %get-tuple-element.106.near.first0, bf16[256,768]{1,0:T(8,128)(2,1)} %copy-done.4, ...), custom_call_target="tpu_custom_call" | custom-call | tf_op jit(solution)/shard_map/pallas_call | solution.py:566
  116.6 1.5 collective-permute-start.26
  118.1 5.4 %collective-permute-done.26.cot1 = bf16[128,768]{1,0:T(8,128)(2,1)S(1)} collective-permute-done((bf16[128,768]{1,0:T(8,128)(2,1)S(1)}, bf16[128,768]{1,0:T(8,128)(2,1)S(1)}, u32[]{:S(2)}, u32[]{:S(2)}) %collective-permute-start.26) | collective-permute-done | bytes 196640 | tf_op jit(solution)/shard_map/ppermute | solution.py:504
  124.4 3.7 %shard_map.310 = (bf16[128,768]{1,0:T(8,128)(2,1)}, bf16[128,768]{1,0:T(8,128)(2,1)}, f32[256,768]{1,0:T(8,128)}, bf16[256,768]{1,0:T(8,128)(2,1)}, f32[8,768]{1,0:T(8,128)}) custom-call(f32[256,768]{1,0:T(8,128)} %get-tuple-element.105.first_sum, f32[256,768]{1,0:T(8,128)} %get-tuple-element.109.keep, f32[256,768]{1,0:T(8,128)} %copy-done.16, ...), custom_call_target="tpu_custom_call" | custom-call | tf_op jit(solution)/shard_map/pallas_call | solution.py:566
  128.2 1.9 collective-permute-done.28.far.douter1
  130.9 7.9 %shard_map.311 = (f32[256,768]{1,0:T(8,128)}, f32[256,768]{1,0:T(8,128)}, bf16[512,1536]{1,0:T(8,128)(2,1)}, f32[8,768]{1,0:T(8,128)}) custom-call(bf16[256,768]{1,0:T(8,128)(2,1)} %get-tuple-element.116.near.douter0, bf16[256,768]{1,0:T(8,128)(2,1)} %copy-done.3, f32[512,1536]{1,0:T(8,128)} %get-tuple-element.117.inner, ...), custom_call_target="tpu_custom_call" | custom-call | tf_op jit(solution)/shard_map/pallas_call | solution.py:566
  138.9 7.3 %shard_map.318 = (bf16[384,1536]{1,0:T(8,128)(2,1)}, bf16[384,1536]{1,0:T(8,128)(2,1)}, bf16[768,768]{1,0:T(8,128)(2,1)}, bf16[768,768]{1,0:T(8,128)(2,1)}) custom-call(bf16[256,768]{1,0:T(8,128)(2,1)} %get-tuple-element.106.near.first0, bf16[256,768]{1,0:T(8,128)(2,1)} %copy-done.4, bf16[256,768]{1,0:T(8,128)(2,1)} %get-tuple-element.116.near.douter0, ...), custom_call_target="tpu_custom_call" | custom-call | tf_op jit(solution)/shard_map/pallas_call | solution.py:566
  146.8 1.5 collective-permute-start.44
  149.4 4.4 %shard_map.312 = (f32[256,768]{1,0:T(8,128)}, bf16[256,768]{1,0:T(8,128)(2,1)}, bf16[256,192]{1,0:T(8,128)(2,1)}, bf16[256,192]{1,0:T(8,128)(2,1)}, bf16[256,192...) custom-call(f32[256,768]{1,0:T(8,128)} %get-tuple-element.105.first_sum, ...), custom_call_target="tpu_custom_call" | custom-call | tf_op jit(solution)/shard_map/pallas_call | solution.py:566
  153.8 3.0 shard_map.322
  159.3 18.7 %collective-permute-done.31.p2 = bf16[256,192]{1,0:T(8,128)(2,1)S(1)} collective-permute-done((bf16[256,192]{1,0:T(8,128)(2,1)}, bf16[256,192]{1,0:T(8,128)(2,1)S(1)}, u32[]{:S(2)}, u32[]{:S(2)}) %collective-permute-start.31) | collective-permute-done | bytes 98336 | tf_op jit(solution)/shard_map/ppermute | solution.py:504
  178.0 1.7 collective-permute-done.32.p3
  180.3 21.0 %shard_map.313 = (f32[208,576]{1,0:T(8,128)}, bf16[208,576]{1,0:T(8,128)(2,1)}, bf16[208,576]{1,0:T(8,128)(2,1)}, bf16[208,576]{1,0:T(8,128)(2,1)}, f32[512,768]{1,0:T(8,128)}, /*index=5*/bf16[512,768]{1,0:T(8,128)(2,1)}) custom-call(s32[2,4]{1,0:T(2,128)} %pad_add_fusion.bounds, bf16[9,1024,64]{2,1,0:T(8,128)(2,1)} %get-tuple-element.101.qkv, ...), custom_call_target="tpu_custom_call" | custom-call | tf_op jit(solution)/shard_map/pallas_call | solution.py:566
  201.3 3.8 %collective-permute-start.36 = (bf16[208,576]{1,0:T(8,128)(2,1)}, bf16[208,576]{1,0:T(8,128)(2,1)S(1)}, u32[]{:S(2)}, u32[]{:S(2)}) collective-permute-start(bf16[208,576]{1,0:T(8,128)(2,1)} %get-tuple-element.134), channel_id=1, source_target_pairs={{0,3},{1,0},{2,1},{3,2},{4,7},{5,4},{6,5},{7,6},{8,11},{9,8},{10,9... | collective-permute-start | bytes 718856 | tf_op jit(solution)/shard_map/ppermute | solution.py:508
  205.0 9.9 %collective-permute-start.37 = (bf16[208,576]{1,0:T(8,128)(2,1)}, bf16[208,576]{1,0:T(8,128)(2,1)S(1)}, u32[]{:S(2)}, u32[]{:S(2)}) collective-permute-start(bf16[208,576]{1,0:T(8,128)(2,1)} %get-tuple-element.135), channel_id=1, source_target_pairs={{0,2},{1,3},{2,0},{3,1},{4,6},{5,7},{6,4},{7,5},{8,10},{9,11},{10,... | collective-permute-start | bytes 718856 | tf_op jit(solution)/shard_map/ppermute | solution.py:508
  214.9 4.7 %collective-permute-done.36.refs_0_ = bf16[208,576]{1,0:T(8,128)(2,1)S(1)} collective-permute-done((bf16[208,576]{1,0:T(8,128)(2,1)}, bf16[208,576]{1,0:T(8,128)(2,1)S(1)}, u32[]{:S(2)}, u32[]{:S(2)}) %collective-permute-start.36) | collective-permute-done | bytes 239648 | tf_op jit(solution)/shard_map/ppermute | solution.py:508
  219.6 3.2 collective-permute-start.38
  222.9 16.2 %collective-permute-done.37.refs_1_ = bf16[208,576]{1,0:T(8,128)(2,1)S(1)} collective-permute-done((bf16[208,576]{1,0:T(8,128)(2,1)}, bf16[208,576]{1,0:T(8,128)(2,1)S(1)}, u32[]{:S(2)}, u32[]{:S(2)}) %collective-permute-start.37) | collective-permute-done | bytes 239648 | tf_op jit(solution)/shard_map/ppermute | solution.py:508
  239.8 2.1 shard_map.315.mine
  244.3 4.1 %shard_map.319 = (bf16[192,768]{1,0:T(8,128)(2,1)}, bf16[192,768]{1,0:T(8,128)(2,1)}, bf16[384,384]{1,0:T(8,128)(2,1)}, bf16[384,384]{1,0:T(8,128)(2,1)}, bf16[1...) custom-call(bf16[384,1536]{1,0:T(8,128)(2,1)} %get-tuple-element.143.ak, ...), custom_call_target="tpu_custom_call" | custom-call | tf_op jit(solution)/shard_map/pallas_call | solution.py:566
  251.0 2.2 shard_map.323
  254.7 1.8 shard_map.316.s0
  256.5 5.5 %collective-permute-done.27 = bf16[128,768]{1,0:T(8,128)(2,1)} collective-permute-done((bf16[128,768]{1,0:T(8,128)(2,1)}, bf16[128,768]{1,0:T(8,128)(2,1)}, u32[]{:S(2)}, u32[]{:S(2)}) %collective-permute-start.27) | collective-permute-done | bytes 196640 | tf_op jit(solution)/shard_map/ppermute | solution.py:504
  263.9 2.2 shard_map.320
  266.2 5.4 %collective-permute-done.41.s2 = bf16[208,576]{1,0:T(8,128)(2,1)S(1)} collective-permute-done((bf16[208,576]{1,0:T(8,128)(2,1)}, bf16[208,576]{1,0:T(8,128)(2,1)S(1)}, u32[]{:S(2)}, u32[]{:S(2)}) %collective-permute-start.41) | collective-permute-done | bytes 239648 | tf_op jit(solution)/shard_map/ppermute | solution.py:504
  271.6 4.7 %collective-permute-done.42.s3 = bf16[208,576]{1,0:T(8,128)(2,1)S(1)} collective-permute-done((bf16[208,576]{1,0:T(8,128)(2,1)}, bf16[208,576]{1,0:T(8,128)(2,1)S(1)}, u32[]{:S(2)}, u32[]{:S(2)}) %collective-permute-start.42) | collective-permute-done | bytes 239648 | tf_op jit(solution)/shard_map/ppermute | solution.py:504
  278.1 1.9 shard_map.324
  281.0 3.0 shard_map.314
  286.0 1.8 maximum_select_fusion.1
  287.9 3.2 shard_map.317
  291.0 1.8 collective-permute-done.49.refs_2_
  293.5 1.9 shard_map.321.refs_0_
  298.1 2.4 shard_map.325
  302.9 1.7 collective-permute-start.52
  306.7 16.4 %collective-permute-done.63.refs_1_ = bf16[144,768]{1,0:T(8,128)(2,1)S(1)} collective-permute-done((bf16[144,768]{1,0:T(8,128)(2,1)}, bf16[144,768]{1,0:T(8,128)(2,1)S(1)}, u32[]{:S(2)}, u32[]{:S(2)}) %collective-permute-start.63) | collective-permute-done | bytes 221216 | tf_op jit(solution)/shard_map/ppermute | solution.py:508
  324.3 2.0 shard_map.326.refs_8_
  328.1 1.8 collective-permute-start.67
  331.0 3.9 %collective-permute-done.65.refs_9_ = bf16[144,768]{1,0:T(8,128)(2,1)S(1)} collective-permute-done((bf16[144,768]{1,0:T(8,128)(2,1)}, bf16[144,768]{1,0:T(8,128)(2,1)S(1)}, u32[]{:S(2)}, u32[]{:S(2)}) %collective-permute-start.65) | collective-permute-done | bytes 221216 | tf_op jit(solution)/shard_map/ppermute | solution.py:504
  334.9 5.0 %collective-permute-done.66.refs_10_ = bf16[144,768]{1,0:T(8,128)(2,1)S(1)} collective-permute-done((bf16[144,768]{1,0:T(8,128)(2,1)}, bf16[144,768]{1,0:T(8,128)(2,1)S(1)}, u32[]{:S(2)}, u32[]{:S(2)}) %collective-permute-start.66) | collective-permute-done | bytes 221216 | tf_op jit(solution)/shard_map/ppermute | solution.py:504
  343.0 4.6 %shard_map.327 = (f32[192,3072]{1,0:T(8,128)}, f32[768,768]{1,0:T(8,128)}, f32[192,768]{1,0:T(8,128)}, f32[16,768]{1,0:T(8,128)}) custom-call(bf16[96,768]{1,0:T(8,128)(2,1)} %shard_map.321.refs_0_, bf16[96,768]{1,0:T(8,128)(2,1)} %copy-done.52, bf16[96,768]{1,0:T(8,128)(2,1)} %collective-permute-done.51.refs_2_, bf16[96,768]{1,0:T(8,128)(2,1)} %copy-done.53, ...), custom_call_target="tpu_custom_call" | custom-call | tf_op jit(solution)/shard_map/pallas_call | solution.py:566
  (313 shorter events, 59.7 us)
Async XLA Ops:
  6.7 11.7 %collective-permute-start.3 = (bf16[112,576]{1,0:T(8,128)(2,1)}, bf16[112,576]{1,0:T(8,128)(2,1)S(1)}, u32[]{:S(2)}, u32[]{:S(2)}) collective-permute-start(bf16[112,576]{1,0:T(8,128)(2,1)} %get-tuple-element.98), channel_id=1, source_target_pairs={{0,3},{1,0},{2,1},{3,2},{4,7},{5,4},{6,5},{7,6},{8,11},{9,8},{10,9... | collective-permute-start | bytes 387080 | tf_op jit(solution)/shard_map/ppermute | solution.py:508
  11.8 13.1 %collective-permute-start.4 = (bf16[112,576]{1,0:T(8,128)(2,1)}, bf16[112,576]{1,0:T(8,128)(2,1)S(1)}, u32[]{:S(2)}, u32[]{:S(2)}) collective-permute-start(bf16[112,576]{1,0:T(8,128)(2,1)} %get-tuple-element.98), channel_id=1, source_target_pairs={{0,2},{1,3},{2,0},{3,1},{4,6},{5,7},{6,4},{7,5},{8,10},{9,11},{10,... | collective-permute-start | bytes 387080 | tf_op jit(solution)/shard_map/ppermute | solution.py:508
  11.8 20.3 %collective-permute-start.5 = (bf16[112,576]{1,0:T(8,128)(2,1)}, bf16[112,576]{1,0:T(8,128)(2,1)S(1)}, u32[]{:S(2)}, u32[]{:S(2)}) collective-permute-start(bf16[112,576]{1,0:T(8,128)(2,1)} %get-tuple-element.98), channel_id=1, source_target_pairs={{0,1},{1,2},{2,3},{3,0},{4,5},{5,6},{6,7},{7,4},{8,9},{9,10},{10,1... | collective-permute-start | bytes 387080 | tf_op jit(solution)/shard_map/ppermute | solution.py:508
  12.8 28.6 %collective-permute-start.12 = (bf16[240,768]{1,0:T(8,128)(2,1)}, bf16[240,768]{1,0:T(8,128)(2,1)S(1)}, u32[]{:S(2)}, u32[]{:S(2)}) collective-permute-start(bf16[240,768]{1,0:T(8,128)(2,1)} %get-tuple-element.104), channel_id=1, source_target_pairs={{0,3},{1,0},{2,1},{3,2},{4,7},{5,4},{6,5},{7,6},{8,11},{9,8},{10,9... | collective-permute-start | bytes 1105928 | tf_op jit(solution)/shard_map/ppermute | solution.py:508
  15.6 40.2 %collective-permute-start.16 = (bf16[240,768]{1,0:T(8,128)(2,1)}, bf16[240,768]{1,0:T(8,128)(2,1)S(1)}, u32[]{:S(2)}, u32[]{:S(2)}) collective-permute-start(bf16[240,768]{1,0:T(8,128)(2,1)} %get-tuple-element.104), channel_id=1, source_target_pairs={{0,2},{1,3},{2,0},{3,1},{4,6},{5,7},{6,4},{7,5},{8,10},{9,11},{10,... | collective-permute-start | bytes 1105928 | tf_op jit(solution)/shard_map/ppermute | solution.py:508
  18.4 38.1 %collective-permute-start.20 = (bf16[240,768]{1,0:T(8,128)(2,1)}, bf16[240,768]{1,0:T(8,128)(2,1)S(1)}, u32[]{:S(2)}, u32[]{:S(2)}) collective-permute-start(bf16[240,768]{1,0:T(8,128)(2,1)} %get-tuple-element.104), channel_id=1, source_target_pairs={{0,1},{1,2},{2,3},{3,0},{4,5},{5,6},{6,7},{7,4},{8,9},{9,10},{10,1... | collective-permute-start | bytes 1105928 | tf_op jit(solution)/shard_map/ppermute | solution.py:508
  32.2 9.0 %collective-permute-start.1 = (bf16[256,768]{1,0:T(8,128)(2,1)S(1)}, bf16[256,768]{1,0:T(8,128)(2,1)S(1)}, u32[]{:S(2)}, u32[]{:S(2)}) collective-permute-start(bf16[256,768]{1,0:T(8,128)(2,1)S(1)} %pad_maximum_fusion.1.mine), channel_id=1, source_target_pairs={{0,8},{4,12},{8,0},{12,4},{16,24},{20,28},{24,16},{28,20},{1,9},{5... | collective-permute-start | bytes 1179656 | tf_op jit(solution)/shard_map/ppermute | solution.py:504
  36.4 6.6 %collective-permute-start.7 = (bf16[112,576]{1,0:T(8,128)(2,1)S(1)}, bf16[112,576]{1,0:T(8,128)(2,1)S(1)}, u32[]{:S(2)}, u32[]{:S(2)}) collective-permute-start(bf16[112,576]{1,0:T(8,128)(2,1)S(1)} %collective-permute-done.4.g2), channel_id=1, source_target_pairs={{0,16},{4,20},{8,24},{12,28},{16,0},{20,4},{24,8},{28,12},{1,17},{... | collective-permute-start | bytes 387080 | tf_op jit(solution)/shard_map/ppermute | solution.py:504
  41.2 7.8 %collective-permute-start.8 = (bf16[112,576]{1,0:T(8,128)(2,1)S(1)}, bf16[112,576]{1,0:T(8,128)(2,1)S(1)}, u32[]{:S(2)}, u32[]{:S(2)}) collective-permute-start(bf16[112,576]{1,0:T(8,128)(2,1)S(1)} %collective-permute-done.5.g3), channel_id=1, source_target_pairs={{0,16},{4,20},{8,24},{12,28},{16,0},{20,4},{24,8},{28,12},{1,17},{... | collective-permute-start | bytes 387080 | tf_op jit(solution)/shard_map/ppermute | solution.py:504
  41.5 17.3 %collective-permute-start.13 = (bf16[240,768]{1,0:T(8,128)(2,1)S(1)}, bf16[240,768]{1,0:T(8,128)(2,1)S(1)}, u32[]{:S(2)}, u32[]{:S(2)}) collective-permute-start(bf16[240,768]{1,0:T(8,128)(2,1)S(1)} %collective-permute-done.12.refs_0_), channel_id=1, source_target_pairs={{0,8},{4,12},{8,0},{12,4},{16,24},{20,28},{24,16},{28,20},{1,9},{5... | collective-permute-start | bytes 1105928 | tf_op jit(solution)/shard_map/ppermute | solution.py:504
  43.0 17.3 %collective-permute-start.14 = (bf16[240,768]{1,0:T(8,128)(2,1)S(1)}, bf16[240,768]{1,0:T(8,128)(2,1)S(1)}, u32[]{:S(2)}, u32[]{:S(2)}) collective-permute-start(bf16[240,768]{1,0:T(8,128)(2,1)S(1)} %collective-permute-done.12.refs_0_), channel_id=1, source_target_pairs={{0,16},{4,20},{8,24},{12,28},{16,0},{20,4},{24,8},{28,12},{1,17},{... | collective-permute-start | bytes 1105928 | tf_op jit(solution)/shard_map/ppermute | solution.py:504
  48.9 13.1 %collective-permute-start.15 = (bf16[240,768]{1,0:T(8,128)(2,1)S(1)}, bf16[240,768]{1,0:T(8,128)(2,1)S(1)}, u32[]{:S(2)}, u32[]{:S(2)}) collective-permute-start(bf16[240,768]{1,0:T(8,128)(2,1)S(1)} %collective-permute-done.12.refs_0_), channel_id=1, source_target_pairs={{0,24},{4,28},{8,16},{12,20},{16,8},{20,12},{24,0},{28,4},{1,25},{... | collective-permute-start | bytes 1105928 | tf_op jit(solution)/shard_map/ppermute | solution.py:504
  55.8 13.7 %collective-permute-start.2 = (bf16[512,768]{1,0:T(8,128)(2,1)S(1)}, bf16[512,768]{1,0:T(8,128)(2,1)S(1)}, u32[]{:S(2)}, u32[]{:S(2)}) collective-permute-start(bf16[512,768]{1,0:T(8,128)(2,1)S(1)} %pad_maximum_fusion), channel_id=1, source_target_pairs={{0,4},{4,0},{8,12},{12,8},{16,20},{20,16},{24,28},{28,24},{1,5},{5... | collective-permute-start | bytes 2359304 | tf_op jit(solution)/shard_map/ppermute | solution.py:504
  56.5 11.5 %collective-permute-start.17 = (bf16[240,768]{1,0:T(8,128)(2,1)S(1)}, bf16[240,768]{1,0:T(8,128)(2,1)S(1)}, u32[]{:S(2)}, u32[]{:S(2)}) collective-permute-start(bf16[240,768]{1,0:T(8,128)(2,1)S(1)} %collective-permute-done.16.refs_4_), channel_id=1, source_target_pairs={{0,8},{4,12},{8,0},{12,4},{16,24},{20,28},{24,16},{28,20},{1,9},{5... | collective-permute-start | bytes 1105928 | tf_op jit(solution)/shard_map/ppermute | solution.py:504
  58.7 31.4 %collective-permute-start.18 = (bf16[240,768]{1,0:T(8,128)(2,1)S(1)}, bf16[240,768]{1,0:T(8,128)(2,1)}, u32[]{:S(2)}, u32[]{:S(2)}) collective-permute-start(bf16[240,768]{1,0:T(8,128)(2,1)S(1)} %collective-permute-done.16.refs_4_), channel_id=1, source_target_pairs={{0,16},{4,20},{8,24},{12,28},{16,0},{20,4},{24,8},{28,12},{1,17},{... | collective-permute-start | bytes 1105928 | tf_op jit(solution)/shard_map/ppermute | solution.py:504
  60.4 30.3 %collective-permute-start.19 = (bf16[240,768]{1,0:T(8,128)(2,1)S(1)}, bf16[240,768]{1,0:T(8,128)(2,1)}, u32[]{:S(2)}, u32[]{:S(2)}) collective-permute-start(bf16[240,768]{1,0:T(8,128)(2,1)S(1)} %collective-permute-done.16.refs_4_), channel_id=1, source_target_pairs={{0,24},{4,28},{8,16},{12,20},{16,8},{20,12},{24,0},{28,4},{1,25},{... | collective-permute-start | bytes 1105928 | tf_op jit(solution)/shard_map/ppermute | solution.py:504
  62.0 28.6 %collective-permute-start.21 = (bf16[240,768]{1,0:T(8,128)(2,1)S(1)}, bf16[240,768]{1,0:T(8,128)(2,1)}, u32[]{:S(2)}, u32[]{:S(2)}) collective-permute-start(bf16[240,768]{1,0:T(8,128)(2,1)S(1)} %collective-permute-done.20.refs_8_), channel_id=1, source_target_pairs={{0,8},{4,12},{8,0},{12,4},{16,24},{20,28},{24,16},{28,20},{1,9},{5... | collective-permute-start | bytes 1105928 | tf_op jit(solution)/shard_map/ppermute | solution.py:504
  68.0 25.2 %collective-permute-start.22 = (bf16[240,768]{1,0:T(8,128)(2,1)S(1)}, bf16[240,768]{1,0:T(8,128)(2,1)}, u32[]{:S(2)}, u32[]{:S(2)}) collective-permute-start(bf16[240,768]{1,0:T(8,128)(2,1)S(1)} %collective-permute-done.20.refs_8_), channel_id=1, source_target_pairs={{0,16},{4,20},{8,24},{12,28},{16,0},{20,4},{24,8},{28,12},{1,17},{... | collective-permute-start | bytes 1105928 | tf_op jit(solution)/shard_map/ppermute | solution.py:504
  69.5 23.7 %collective-permute-start.23 = (bf16[240,768]{1,0:T(8,128)(2,1)S(1)}, bf16[240,768]{1,0:T(8,128)(2,1)}, u32[]{:S(2)}, u32[]{:S(2)}) collective-permute-start(bf16[240,768]{1,0:T(8,128)(2,1)S(1)} %collective-permute-done.20.refs_8_), channel_id=1, source_target_pairs={{0,24},{4,28},{8,16},{12,20},{16,8},{20,12},{24,0},{28,4},{1,25},{... | collective-permute-start | bytes 1105928 | tf_op jit(solution)/shard_map/ppermute | solution.py:504
  90.1 6.6 %collective-permute-start.10 = (bf16[256,192]{1,0:T(8,128)(2,1)}, bf16[256,192]{1,0:T(8,128)(2,1)S(1)}, u32[]{:S(2)}, u32[]{:S(2)}) collective-permute-start(bf16[256,192]{1,0:T(8,128)(2,1)} %get-tuple-element.102), channel_id=1, source_target_pairs={{0,8},{4,12},{8,0},{12,4},{16,24},{20,28},{24,16},{28,20},{1,9},{5... | collective-permute-start | bytes 294920 | tf_op jit(solution)/shard_map/ppermute | solution.py:504
  90.7 6.0 %collective-permute-start.11 = (bf16[256,192]{1,0:T(8,128)(2,1)}, bf16[256,192]{1,0:T(8,128)(2,1)S(1)}, u32[]{:S(2)}, u32[]{:S(2)}) collective-permute-start(bf16[256,192]{1,0:T(8,128)(2,1)} %get-tuple-element.103), channel_id=1, source_target_pairs={{0,12},{4,8},{8,4},{12,0},{16,28},{20,24},{24,20},{28,16},{1,13},{... | collective-permute-start | bytes 294920 | tf_op jit(solution)/shard_map/ppermute | solution.py:504
  90.7 6.0 %collective-permute-start.9 = (bf16[256,192]{1,0:T(8,128)(2,1)S(1)}, bf16[256,192]{1,0:T(8,128)(2,1)S(1)}, u32[]{:S(2)}, u32[]{:S(2)}) collective-permute-start(bf16[256,192]{1,0:T(8,128)(2,1)S(1)} %copy-done.76), channel_id=1, source_target_pairs={{0,4},{4,0},{8,12},{12,8},{16,20},{20,16},{24,28},{28,24},{1,5},{5... | collective-permute-start | bytes 294920 | tf_op jit(solution)/shard_map/ppermute | solution.py:504
  115.4 8.1 %collective-permute-start.25 = (f32[256,768]{1,0:T(8,128)}, f32[256,768]{1,0:T(8,128)S(1)}, u32[]{:S(2)}, u32[]{:S(2)}) collective-permute-start(f32[256,768]{1,0:T(8,128)} %get-tuple-element.110), channel_id=1, source_target_pairs={{0,4},{4,0},{8,12},{12,8},{16,20},{20,16},{24,28},{28,24},{1,5},{5... | collective-permute-start | bytes 2359304 | tf_op jit(solution)/shard_map/ppermute | solution.py:504
  116.6 6.9 %collective-permute-start.26 = (bf16[128,768]{1,0:T(8,128)(2,1)S(1)}, bf16[128,768]{1,0:T(8,128)(2,1)S(1)}, u32[]{:S(2)}, u32[]{:S(2)}) collective-permute-start(bf16[128,768]{1,0:T(8,128)(2,1)S(1)} %get-tuple-element.179), channel_id=1, source_target_pairs={{0,16},{4,20},{8,24},{12,28},{16,0},{20,4},{24,8},{28,12},{1,17},{... | collective-permute-start | bytes 589832 | tf_op jit(solution)/shard_map/ppermute | solution.py:504
  138.7 9.8 %collective-permute-start.29 = (f32[256,768]{1,0:T(8,128)}, f32[256,768]{1,0:T(8,128)S(1)}, u32[]{:S(2)}, u32[]{:S(2)}) collective-permute-start(f32[256,768]{1,0:T(8,128)} %get-tuple-element.121), channel_id=1, source_target_pairs={{0,4},{4,0},{8,12},{12,8},{16,20},{20,16},{24,28},{28,24},{1,5},{5... | collective-permute-start | bytes 2359304 | tf_op jit(solution)/shard_map/ppermute | solution.py:504
  146.1 96.7 %collective-permute-start.43 = (bf16[384,1536]{1,0:T(8,128)(2,1)}, bf16[384,1536]{1,0:T(8,128)(2,1)S(1)}, u32[]{:S(2)}, u32[]{:S(2)}) collective-permute-start(bf16[384,1536]{1,0:T(8,128)(2,1)} %get-tuple-element.144), channel_id=1, source_target_pairs={{0,8},{4,12},{8,0},{12,4},{16,24},{20,28},{24,16},{28,20},{1,9},{5... | collective-permute-start | bytes 3538952 | tf_op jit(solution)/shard_map/ppermute | solution.py:504
  146.8 96.1 %collective-permute-start.44 = (bf16[768,768]{1,0:T(8,128)(2,1)}, bf16[768,768]{1,0:T(8,128)(2,1)S(1)}, u32[]{:S(2)}, u32[]{:S(2)}) collective-permute-start(bf16[768,768]{1,0:T(8,128)(2,1)} %get-tuple-element.146), channel_id=1, source_target_pairs={{0,16},{4,20},{8,24},{12,28},{16,0},{20,4},{24,8},{28,12},{1,17},{... | collective-permute-start | bytes 3538952 | tf_op jit(solution)/shard_map/ppermute | solution.py:504
  156.8 93.3 %collective-permute-start.59 = (bf16[800,384]{1,0:T(8,128)(2,1)}, bf16[800,384]{1,0:T(8,128)(2,1)}, u32[]{:S(2)}, u32[]{:S(2)}) collective-permute-start(bf16[800,384]{1,0:T(8,128)(2,1)} %get-tuple-element.164), channel_id=1, source_target_pairs={{0,4},{4,0},{8,12},{12,8},{16,20},{20,16},{24,28},{28,24},{1,5},{5... | collective-permute-start | bytes 1843208 | tf_op jit(solution)/shard_map/ppermute | solution.py:504
  157.3 20.7 %collective-permute-start.31 = (bf16[256,192]{1,0:T(8,128)(2,1)}, bf16[256,192]{1,0:T(8,128)(2,1)S(1)}, u32[]{:S(2)}, u32[]{:S(2)}) collective-permute-start(bf16[256,192]{1,0:T(8,128)(2,1)} %get-tuple-element.125), channel_id=1, source_target_pairs={{0,8},{4,12},{8,0},{12,4},{16,24},{20,28},{24,16},{28,20},{1,9},{5... | collective-permute-start | bytes 294920 | tf_op jit(solution)/shard_map/ppermute | solution.py:504
  158.7 21.0 %collective-permute-start.32 = (bf16[256,192]{1,0:T(8,128)(2,1)}, bf16[256,192]{1,0:T(8,128)(2,1)S(1)}, u32[]{:S(2)}, u32[]{:S(2)}) collective-permute-start(bf16[256,192]{1,0:T(8,128)(2,1)} %get-tuple-element.126), channel_id=1, source_target_pairs={{0,12},{4,8},{8,4},{12,0},{16,28},{20,24},{24,20},{28,16},{1,13},{... | collective-permute-start | bytes 294920 | tf_op jit(solution)/shard_map/ppermute | solution.py:504
  201.3 18.3 %collective-permute-start.36 = (bf16[208,576]{1,0:T(8,128)(2,1)}, bf16[208,576]{1,0:T(8,128)(2,1)S(1)}, u32[]{:S(2)}, u32[]{:S(2)}) collective-permute-start(bf16[208,576]{1,0:T(8,128)(2,1)} %get-tuple-element.134), channel_id=1, source_target_pairs={{0,3},{1,0},{2,1},{3,2},{4,7},{5,4},{6,5},{7,6},{8,11},{9,8},{10,9... | collective-permute-start | bytes 718856 | tf_op jit(solution)/shard_map/ppermute | solution.py:508
  205.0 34.1 %collective-permute-start.37 = (bf16[208,576]{1,0:T(8,128)(2,1)}, bf16[208,576]{1,0:T(8,128)(2,1)S(1)}, u32[]{:S(2)}, u32[]{:S(2)}) collective-permute-start(bf16[208,576]{1,0:T(8,128)(2,1)} %get-tuple-element.135), channel_id=1, source_target_pairs={{0,2},{1,3},{2,0},{3,1},{4,6},{5,7},{6,4},{7,5},{8,10},{9,11},{10,... | collective-permute-start | bytes 718856 | tf_op jit(solution)/shard_map/ppermute | solution.py:508
  219.6 20.2 %collective-permute-start.38 = (bf16[208,576]{1,0:T(8,128)(2,1)}, bf16[208,576]{1,0:T(8,128)(2,1)}, u32[]{:S(2)}, u32[]{:S(2)}) collective-permute-start(bf16[208,576]{1,0:T(8,128)(2,1)} %get-tuple-element.136), channel_id=1, source_target_pairs={{0,1},{1,2},{2,3},{3,0},{4,5},{5,6},{6,7},{7,4},{8,9},{9,10},{10,1... | collective-permute-start | bytes 718856 | tf_op jit(solution)/shard_map/ppermute | solution.py:508
  239.8 40.2 %collective-permute-start.33 = (bf16[512,768]{1,0:T(8,128)(2,1)}, bf16[512,768]{1,0:T(8,128)(2,1)S(1)}, u32[]{:S(2)}, u32[]{:S(2)}) collective-permute-start(bf16[512,768]{1,0:T(8,128)(2,1)} %get-tuple-element.129), channel_id=1, source_target_pairs={{0,4},{4,0},{8,12},{12,8},{16,20},{20,16},{24,28},{28,24},{1,5},{5... | collective-permute-start | bytes 2359304 | tf_op jit(solution)/shard_map/ppermute | solution.py:504
  241.9 11.4 %collective-permute-start.39 = (bf16[208,576]{1,0:T(8,128)(2,1)}, bf16[208,576]{1,0:T(8,128)(2,1)S(1)}, u32[]{:S(2)}, u32[]{:S(2)}) collective-permute-start(bf16[208,576]{1,0:T(8,128)(2,1)} %shard_map.315.mine), channel_id=1, source_target_pairs={{0,16},{4,20},{8,24},{12,28},{16,0},{20,4},{24,8},{28,12},{1,17},{... | collective-permute-start | bytes 718856 | tf_op jit(solution)/shard_map/ppermute | solution.py:504
  248.4 13.7 %collective-permute-start.45 = (bf16[192,768]{1,0:T(8,128)(2,1)}, bf16[192,768]{1,0:T(8,128)(2,1)S(1)}, u32[]{:S(2)}, u32[]{:S(2)}) collective-permute-start(bf16[192,768]{1,0:T(8,128)(2,1)} %get-tuple-element.148), channel_id=1, source_target_pairs={{0,16},{4,20},{8,24},{12,28},{16,0},{20,4},{24,8},{28,12},{1,17},{... | collective-permute-start | bytes 884744 | tf_op jit(solution)/shard_map/ppermute | solution.py:504
  249.5 13.3 %collective-permute-start.46 = (bf16[384,384]{1,0:T(8,128)(2,1)}, bf16[384,384]{1,0:T(8,128)(2,1)S(1)}, u32[]{:S(2)}, u32[]{:S(2)}) collective-permute-start(bf16[384,384]{1,0:T(8,128)(2,1)} %get-tuple-element.150), channel_id=1, source_target_pairs={{0,8},{4,12},{8,0},{12,4},{16,24},{20,28},{24,16},{28,20},{1,9},{5... | collective-permute-start | bytes 884744 | tf_op jit(solution)/shard_map/ppermute | solution.py:504
  250.1 11.9 %collective-permute-start.27 = (bf16[128,768]{1,0:T(8,128)(2,1)}, bf16[128,768]{1,0:T(8,128)(2,1)}, u32[]{:S(2)}, u32[]{:S(2)}) collective-permute-start(bf16[128,768]{1,0:T(8,128)(2,1)} %get-tuple-element.112), channel_id=1, source_target_pairs={{0,16},{4,20},{8,24},{12,28},{16,0},{20,4},{24,8},{28,12},{1,17},{... | collective-permute-start | bytes 589832 | tf_op jit(solution)/shard_map/ppermute | solution.py:504
  253.3 24.0 %collective-permute-start.60 = (bf16[416,384]{1,0:T(8,128)(2,1)}, bf16[416,384]{1,0:T(8,128)(2,1)S(1)}, u32[]{:S(2)}, u32[]{:S(2)}) collective-permute-start(bf16[416,384]{1,0:T(8,128)(2,1)} %get-tuple-element.166), channel_id=1, source_target_pairs={{0,8},{4,12},{8,0},{12,4},{16,24},{20,28},{24,16},{28,20},{1,9},{5... | collective-permute-start | bytes 958472 | tf_op jit(solution)/shard_map/ppermute | solution.py:504
  262.0 9.5 %collective-permute-start.41 = (bf16[208,576]{1,0:T(8,128)(2,1)}, bf16[208,576]{1,0:T(8,128)(2,1)S(1)}, u32[]{:S(2)}, u32[]{:S(2)}) collective-permute-start(bf16[208,576]{1,0:T(8,128)(2,1)} %shard_map.316.s0), channel_id=1, source_target_pairs={{0,8},{4,12},{8,0},{12,4},{16,24},{20,28},{24,16},{28,20},{1,9},{5... | collective-permute-start | bytes 718856 | tf_op jit(solution)/shard_map/ppermute | solution.py:504
  262.8 13.5 %collective-permute-start.42 = (bf16[208,576]{1,0:T(8,128)(2,1)}, bf16[208,576]{1,0:T(8,128)(2,1)S(1)}, u32[]{:S(2)}, u32[]{:S(2)}) collective-permute-start(bf16[208,576]{1,0:T(8,128)(2,1)} %shard_map.316.s0), channel_id=1, source_target_pairs={{0,12},{4,8},{8,4},{12,0},{16,28},{20,24},{24,20},{28,16},{1,13},{... | collective-permute-start | bytes 718856 | tf_op jit(solution)/shard_map/ppermute | solution.py:504
  266.1 17.9 %collective-permute-start.47 = (bf16[96,768]{1,0:T(8,128)(2,1)}, bf16[96,768]{1,0:T(8,128)(2,1)S(1)}, u32[]{:S(2)}, u32[]{:S(2)}) collective-permute-start(bf16[96,768]{1,0:T(8,128)(2,1)} %get-tuple-element.152), channel_id=1, source_target_pairs={{0,3},{1,0},{2,1},{3,2},{4,7},{5,4},{6,5},{7,6},{8,11},{9,8},{10,9... | collective-permute-start | bytes 442376 | tf_op jit(solution)/shard_map/ppermute | solution.py:508
  271.6 13.8 %collective-permute-start.48 = (bf16[96,768]{1,0:T(8,128)(2,1)}, bf16[96,768]{1,0:T(8,128)(2,1)S(1)}, u32[]{:S(2)}, u32[]{:S(2)}) collective-permute-start(bf16[96,768]{1,0:T(8,128)(2,1)} %get-tuple-element.153), channel_id=1, source_target_pairs={{0,2},{1,3},{2,0},{3,1},{4,6},{5,7},{6,4},{7,5},{8,10},{9,11},{10,... | collective-permute-start | bytes 442376 | tf_op jit(solution)/shard_map/ppermute | solution.py:508
  276.3 20.1 %collective-permute-start.57 = (bf16[192,768]{1,0:T(8,128)(2,1)}, bf16[192,768]{1,0:T(8,128)(2,1)S(1)}, u32[]{:S(2)}, u32[]{:S(2)}) collective-permute-start(bf16[192,768]{1,0:T(8,128)(2,1)} %get-tuple-element.156), channel_id=1, source_target_pairs={{0,16},{4,20},{8,24},{12,28},{16,0},{20,4},{24,8},{28,12},{1,17},{... | collective-permute-start | bytes 884744 | tf_op jit(solution)/shard_map/ppermute | solution.py:504
  277.3 20.0 %collective-permute-start.58 = (bf16[384,384]{1,0:T(8,128)(2,1)}, bf16[384,384]{1,0:T(8,128)(2,1)S(1)}, u32[]{:S(2)}, u32[]{:S(2)}) collective-permute-start(bf16[384,384]{1,0:T(8,128)(2,1)} %get-tuple-element.158), channel_id=1, source_target_pairs={{0,8},{4,12},{8,0},{12,4},{16,24},{20,28},{24,16},{28,20},{1,9},{5... | collective-permute-start | bytes 884744 | tf_op jit(solution)/shard_map/ppermute | solution.py:504
  280.0 17.3 %collective-permute-start.61 = (bf16[224,384]{1,0:T(8,128)(2,1)}, bf16[224,384]{1,0:T(8,128)(2,1)S(1)}, u32[]{:S(2)}, u32[]{:S(2)}) collective-permute-start(bf16[224,384]{1,0:T(8,128)(2,1)} %get-tuple-element.168), channel_id=1, source_target_pairs={{0,16},{4,20},{8,24},{12,28},{16,0},{20,4},{24,8},{28,12},{1,17},{... | collective-permute-start | bytes 516104 | tf_op jit(solution)/shard_map/ppermute | solution.py:504
  284.0 21.2 %collective-permute-start.34 = (bf16[256,768]{1,0:T(8,128)(2,1)}, bf16[256,768]{1,0:T(8,128)(2,1)S(1)}, u32[]{:S(2)}, u32[]{:S(2)}) collective-permute-start(bf16[256,768]{1,0:T(8,128)(2,1)} %get-tuple-element.132), channel_id=1, source_target_pairs={{0,8},{4,12},{8,0},{12,4},{16,24},{20,28},{24,16},{28,20},{1,9},{5... | collective-permute-start | bytes 1179656 | tf_op jit(solution)/shard_map/ppermute | solution.py:504
  285.4 7.5 %collective-permute-start.49 = (bf16[96,768]{1,0:T(8,128)(2,1)}, bf16[96,768]{1,0:T(8,128)(2,1)S(1)}, u32[]{:S(2)}, u32[]{:S(2)}) collective-permute-start(bf16[96,768]{1,0:T(8,128)(2,1)} %get-tuple-element.154), channel_id=1, source_target_pairs={{0,1},{1,2},{2,3},{3,0},{4,5},{5,6},{6,7},{7,4},{8,9},{9,10},{10,1... | collective-permute-start | bytes 442376 | tf_op jit(solution)/shard_map/ppermute | solution.py:508
  295.4 9.3 %collective-permute-start.50 = (bf16[96,768]{1,0:T(8,128)(2,1)}, bf16[96,768]{1,0:T(8,128)(2,1)S(1)}, u32[]{:S(2)}, u32[]{:S(2)}) collective-permute-start(bf16[96,768]{1,0:T(8,128)(2,1)} %shard_map.321.refs_0_), channel_id=1, source_target_pairs={{0,8},{4,12},{8,0},{12,4},{16,24},{20,28},{24,16},{28,20},{1,9},{5... | collective-permute-start | bytes 442376 | tf_op jit(solution)/shard_map/ppermute | solution.py:504
  296.4 8.3 %collective-permute-start.51 = (bf16[96,768]{1,0:T(8,128)(2,1)}, bf16[96,768]{1,0:T(8,128)(2,1)}, u32[]{:S(2)}, u32[]{:S(2)}) collective-permute-start(bf16[96,768]{1,0:T(8,128)(2,1)} %shard_map.321.refs_0_), channel_id=1, source_target_pairs={{0,16},{4,20},{8,24},{12,28},{16,0},{20,4},{24,8},{28,12},{1,17},{... | collective-permute-start | bytes 442376 | tf_op jit(solution)/shard_map/ppermute | solution.py:504
  300.4 6.1 %collective-permute-start.62 = (bf16[144,768]{1,0:T(8,128)(2,1)}, bf16[144,768]{1,0:T(8,128)(2,1)S(1)}, u32[]{:S(2)}, u32[]{:S(2)}) collective-permute-start(bf16[144,768]{1,0:T(8,128)(2,1)} %get-tuple-element.170), channel_id=1, source_target_pairs={{0,3},{1,0},{2,1},{3,2},{4,7},{5,4},{6,5},{7,6},{8,11},{9,8},{10,9... | collective-permute-start | bytes 663560 | tf_op jit(solution)/shard_map/ppermute | solution.py:508
  302.9 23.4 %collective-permute-start.52 = (bf16[96,768]{1,0:T(8,128)(2,1)}, bf16[96,768]{1,0:T(8,128)(2,1)S(1)}, u32[]{:S(2)}, u32[]{:S(2)}) collective-permute-start(bf16[96,768]{1,0:T(8,128)(2,1)} %shard_map.321.refs_0_), channel_id=1, source_target_pairs={{0,24},{4,28},{8,16},{12,20},{16,8},{20,12},{24,0},{28,4},{1,25},{... | collective-permute-start | bytes 442376 | tf_op jit(solution)/shard_map/ppermute | solution.py:504
  304.6 22.5 %collective-permute-start.53 = (bf16[96,768]{1,0:T(8,128)(2,1)}, bf16[96,768]{1,0:T(8,128)(2,1)S(1)}, u32[]{:S(2)}, u32[]{:S(2)}) collective-permute-start(bf16[96,768]{1,0:T(8,128)(2,1)} %shard_map.321.refs_0_), channel_id=1, source_target_pairs={{0,4},{4,0},{8,12},{12,8},{16,20},{20,16},{24,28},{28,24},{1,5},{5... | collective-permute-start | bytes 442376 | tf_op jit(solution)/shard_map/ppermute | solution.py:504
  304.7 23.5 %collective-permute-start.54 = (bf16[96,768]{1,0:T(8,128)(2,1)S(1)}, bf16[96,768]{1,0:T(8,128)(2,1)}, u32[]{:S(2)}, u32[]{:S(2)}) collective-permute-start(bf16[96,768]{1,0:T(8,128)(2,1)S(1)} %collective-permute-done.50.refs_1_), channel_id=1, source_target_pairs={{0,4},{4,0},{8,12},{12,8},{16,20},{20,16},{24,28},{28,24},{1,5},{5... | collective-permute-start | bytes 442376 | tf_op jit(solution)/shard_map/ppermute | solution.py:504
  305.2 18.0 %collective-permute-start.63 = (bf16[144,768]{1,0:T(8,128)(2,1)}, bf16[144,768]{1,0:T(8,128)(2,1)S(1)}, u32[]{:S(2)}, u32[]{:S(2)}) collective-permute-start(bf16[144,768]{1,0:T(8,128)(2,1)} %get-tuple-element.171), channel_id=1, source_target_pairs={{0,2},{1,3},{2,0},{3,1},{4,6},{5,7},{6,4},{7,5},{8,10},{9,11},{10,... | collective-permute-start | bytes 663560 | tf_op jit(solution)/shard_map/ppermute | solution.py:508
  306.6 16.6 %collective-permute-start.64 = (bf16[144,768]{1,0:T(8,128)(2,1)}, bf16[144,768]{1,0:T(8,128)(2,1)S(1)}, u32[]{:S(2)}, u32[]{:S(2)}) collective-permute-start(bf16[144,768]{1,0:T(8,128)(2,1)} %get-tuple-element.172), channel_id=1, source_target_pairs={{0,1},{1,2},{2,3},{3,0},{4,5},{5,6},{6,7},{7,4},{8,9},{9,10},{10,1... | collective-permute-start | bytes 663560 | tf_op jit(solution)/shard_map/ppermute | solution.py:508
  323.2 6.8 %collective-permute-start.55 = (bf16[96,768]{1,0:T(8,128)(2,1)}, bf16[96,768]{1,0:T(8,128)(2,1)S(1)}, u32[]{:S(2)}, u32[]{:S(2)}) collective-permute-start(bf16[96,768]{1,0:T(8,128)(2,1)} %collective-permute-done.51.refs_2_), channel_id=1, source_target_pairs={{0,4},{4,0},{8,12},{12,8},{16,20},{20,16},{24,28},{28,24},{1,5},{5... | collective-permute-start | bytes 442376 | tf_op jit(solution)/shard_map/ppermute | solution.py:504
  323.2 7.8 %collective-permute-start.35 = (bf16[128,768]{1,0:T(8,128)(2,1)S(1)}, bf16[128,768]{1,0:T(8,128)(2,1)S(1)}, u32[]{:S(2)}, u32[]{:S(2)}) collective-permute-start(bf16[128,768]{1,0:T(8,128)(2,1)S(1)} %slice.120), channel_id=1, source_target_pairs={{0,16},{4,20},{8,24},{12,28},{16,0},{20,4},{24,8},{28,12},{1,17},{... | collective-permute-start | bytes 589832 | tf_op jit(solution)/shard_map/ppermute | solution.py:504
  326.4 8.6 %collective-permute-start.65 = (bf16[144,768]{1,0:T(8,128)(2,1)}, bf16[144,768]{1,0:T(8,128)(2,1)S(1)}, u32[]{:S(2)}, u32[]{:S(2)}) collective-permute-start(bf16[144,768]{1,0:T(8,128)(2,1)} %shard_map.326.refs_8_), channel_id=1, source_target_pairs={{0,8},{4,12},{8,0},{12,4},{16,24},{20,28},{24,16},{28,20},{1,9},{5... | collective-permute-start | bytes 663560 | tf_op jit(solution)/shard_map/ppermute | solution.py:504
  327.1 12.8 %collective-permute-start.66 = (bf16[144,768]{1,0:T(8,128)(2,1)}, bf16[144,768]{1,0:T(8,128)(2,1)S(1)}, u32[]{:S(2)}, u32[]{:S(2)}) collective-permute-start(bf16[144,768]{1,0:T(8,128)(2,1)} %shard_map.326.refs_8_), channel_id=1, source_target_pairs={{0,16},{4,20},{8,24},{12,28},{16,0},{20,4},{24,8},{28,12},{1,17},{... | collective-permute-start | bytes 663560 | tf_op jit(solution)/shard_map/ppermute | solution.py:504
  328.1 11.9 %collective-permute-start.67 = (bf16[144,768]{1,0:T(8,128)(2,1)}, bf16[144,768]{1,0:T(8,128)(2,1)S(1)}, u32[]{:S(2)}, u32[]{:S(2)}) collective-permute-start(bf16[144,768]{1,0:T(8,128)(2,1)} %shard_map.326.refs_8_), channel_id=1, source_target_pairs={{0,24},{4,28},{8,16},{12,20},{16,8},{20,12},{24,0},{28,4},{1,25},{... | collective-permute-start | bytes 663560 | tf_op jit(solution)/shard_map/ppermute | solution.py:504
  330.0 11.5 %collective-permute-start.56 = (bf16[96,768]{1,0:T(8,128)(2,1)S(1)}, bf16[96,768]{1,0:T(8,128)(2,1)S(1)}, u32[]{:S(2)}, u32[]{:S(2)}) collective-permute-start(bf16[96,768]{1,0:T(8,128)(2,1)S(1)} %collective-permute-done.52.refs_3_), channel_id=1, source_target_pairs={{0,4},{4,0},{8,12},{12,8},{16,20},{20,16},{24,28},{28,24},{1,5},{5... | collective-permute-start | bytes 442376 | tf_op jit(solution)/shard_map/ppermute | solution.py:504
  331.0 10.4 %collective-permute-start.68 = (bf16[144,768]{1,0:T(8,128)(2,1)}, bf16[144,768]{1,0:T(8,128)(2,1)S(1)}, u32[]{:S(2)}, u32[]{:S(2)}) collective-permute-start(bf16[144,768]{1,0:T(8,128)(2,1)} %shard_map.326.refs_8_), channel_id=1, source_target_pairs={{0,4},{4,0},{8,12},{12,8},{16,20},{20,16},{24,28},{28,24},{1,5},{5... | collective-permute-start | bytes 663560 | tf_op jit(solution)/shard_map/ppermute | solution.py:504
  334.9 6.6 %collective-permute-start.69 = (bf16[144,768]{1,0:T(8,128)(2,1)S(1)}, bf16[144,768]{1,0:T(8,128)(2,1)S(1)}, u32[]{:S(2)}, u32[]{:S(2)}) collective-permute-start(bf16[144,768]{1,0:T(8,128)(2,1)S(1)} %collective-permute-done.65.refs_9_), channel_id=1, source_target_pairs={{0,4},{4,0},{8,12},{12,8},{16,20},{20,16},{24,28},{28,24},{1,5},{5... | collective-permute-start | bytes 663560 | tf_op jit(solution)/shard_map/ppermute | solution.py:504
  (85 other events, 861.8 us)
where the time goes:
time: 351 us; the launch traced here: 350 us
  waiting for transfers between devices  130 us (37%)
  Pallas kernels  115 us (33%)
  starting transfers between devices  77.4 us (22%)
  local copies, waits for them, and re-layouts  21.4 us (6%)
  other arithmetic  5.81 us (2%)
    pallas_call x23, Pallas kernels, run(): pl.pallas_call(kernel, out_shape=shapes, in_specs=[pl.BlockSpec(memory_sp...  115 us
    ppermute x57, waiting for transfers between devices, flip(): return lax.ppermute(value, 'ctx', [(i, i ^ bits) for i in range(8)])  77 us
    ppermute x15, waiting for transfers between devices, turn(): return lax.ppermute(value, 'wt', [(i, (i - step) % 4) for i in range(4)])  52.5 us
    ppermute x57, starting transfers between devices, flip(): return lax.ppermute(value, 'ctx', [(i, i ^ bits) for i in range(8)])  49.2 us
    ppermute x15, starting transfers between devices, turn(): return lax.ppermute(value, 'wt', [(i, (i - step) % 4) for i in range(4)])  28.2 us
    unnamed x159, local copies, waits for them, and re-layouts  11.7 us
  transfers between devices with their start and end apart: 72, of which 27 were waited for; matrix products, arithmetic and copies ran while one was open for 3% of the time, Pallas kernels for 23%

commit v1 on v0

--- a/solution.py
+++ b/solution.py
@@ -555,22 +555,28 @@
     return root * (grad - mean - normed * along)
 
 
-def gelu_slope(inner):
+def gelu_parts(inner):
+    rise = 0.5 * (1.0 + lax.erf(inner * ROOT_HALF))
     bell = jnp.exp(-0.5 * inner * inner) * (1.0 / math.sqrt(2.0 * math.pi))
-    return 0.5 * (1.0 + lax.erf(inner * ROOT_HALF)) + inner * bell
-
-
-def run(kernel, outs, args, scratch=(), scalars=()):
+    return inner * rise, rise + inner * bell
+
+
+def run(kernel, outs, args, scratch=(), scalars=(), specs=None, out_specs=None):
     shapes = tuple(jax.ShapeDtypeStruct(shape, dtype) for shape, dtype in outs)
-    spaces = [pltpu.SMEM] * len(scalars) + [pltpu.VMEM] * len(args)
+    whole = pl.BlockSpec(memory_space=pltpu.VMEM)
+    in_specs = [pl.BlockSpec(memory_space=pltpu.SMEM)] * len(scalars)
+    in_specs += [whole] * len(args) if specs is None else specs
     return pl.pallas_call(
         kernel,
         out_shape=shapes,
-        in_specs=[pl.BlockSpec(memory_space=space) for space in spaces],
+        in_specs=in_specs,
+        out_specs=tuple([whole] * len(outs) if out_specs is None else out_specs),
         scratch_shapes=list(scratch),
     )(*scalars, *args)
 
 
+WHOLE = pl.BlockSpec(memory_space=pltpu.VMEM)
+LEFT = pl.BlockSpec(memory_space=pl.ANY)
 BF = jnp.bfloat16
 F32 = jnp.float32
 
@@ -584,10 +590,10 @@
     return pl.ds(pl.multiple_of(start, 16), count)
 
 
-def prepare_kernel(wq, wk, wv, wo, wi, wo2, vec, heads_own, heads_send, w2_send, inner_half, outer_half):
-    core, quarter, group, _ = where_am_i()
+def prepare_heads_kernel(wq, wk, wv, vec, heads_own, heads_send):
+    _, quarter, group, _ = where_am_i()
     shard, dim = wq.shape
-    width, half = dim // 4, wo2.shape[0] // 2
+    width = dim // 4
     for index in range(4):
 
         @pl.when(group == index)
@@ -597,6 +603,16 @@
                     :, index * width : (index + 1) * width
                 ]
 
+    part = shard // 2
+    heads_send[0:part, :] = heads_own[some_rows((quarter >> 1) * part, part), :]
+    heads_send[part:, 0:width] = vec[...]
+    heads_send[part:, width:] = jnp.zeros((16, 2 * width), BF)
+
+
+def prepare_kernel(wo, wi, wo2, w2_send, inner_half, outer_half):
+    core, quarter, _, _ = where_am_i()
+    shard, dim = wo.shape
+    half = wo2.shape[0] // 2
     for index in range(2):
 
         @pl.when(core == index)
@@ -606,10 +622,6 @@
                 inner_half[:, block * half : (block + 1) * half] = wi[:, at : at + half]
             outer_half[...] = wo2[index * half : (index + 1) * half, :]
 
-    part = shard // 2
-    heads_send[0:part, :] = heads_own[some_rows((quarter >> 1) * part, part), :]
-    heads_send[part:, 0:width] = vec[...]
-    heads_send[part:, width:] = jnp.zeros((16, 2 * width), BF)
     part = shard // 4
     rows = some_rows(quarter * part, part)
     w2_send[0:part, :] = inner_half[rows, 0:dim]
@@ -716,52 +728,86 @@
     attend_rows(qkv, seg_col, seg_row, 1, (m2, m3), logsum, mixed)
 
 
-def project_kernel(m0, m1, m2, m3, mine, wo, vec, *refs):
-    pieces, (first_sum, first_low, out_full) = refs[:12], refs[12:]
+def project_kernel(m0, m1, m2, m3, mine, vec, wo, *refs):
+    pieces, (first_sum, first_low, out_full, sems) = refs[:12], refs[12:]
     _, quarter, group, own = where_am_i()
     shard = wo.shape[0]
     part = shard // 4
-    out_full[some_rows(own * shard, shard), :] = wo[...]
+    copies = [(wo, out_full.at[some_rows(own * shard, shard), :])]
     for index, piece in enumerate(pieces):
         at = ((own + 1 + index // 4) & 3) * shard + part * (quarter ^ (index % 4))
-        out_full[some_rows(at, part), :] = piece[piece.shape[0] - part :, :]
+        rows = piece.shape[0]
+        copies.append((piece.at[rows - part : rows, :], out_full.at[some_rows(at, part), :]))
+    copies = [
+        pltpu.make_async_copy(source, target, sems.at[index])
+        for index, (source, target) in enumerate(copies)
+    ]
+    for copy in copies:
+        copy.start()
     total = wide(mine[...]) + vec[2:3, :]
+    for copy in copies:
+        copy.wait()
     for code, ref in enumerate((m0, m1, m2, m3)):
         total += dot(ref[...], out_full[some_rows((group ^ code) * shard, shard), :])
     first_sum[...] = total
     first_low[...] = short(norm_parts(total)[0] * vec[3:4, :] + vec[4:5, :])
 
 
-def forward_kernel(near, far, inner_half, outer_half, bias, *refs):
-    pieces, (keep, send, inner, active, wi_full, wo2_full) = refs[:12], refs[12:]
+def forward_kernel(near, far, bias, inner_half, outer_half, *refs):
+    pieces, (keep, send, slope, active, wi_full, wo2_full, wi, wo2, sems) = refs[:12], refs[12:]
     _, quarter, _, own = where_am_i()
     shard, half = inner_half.shape[0], outer_half.shape[0]
     dim = keep.shape[1]
     part, step = shard // 4, half // 4
-    wi_full[some_rows(own * shard, shard), :] = inner_half[...]
-    wo2_full[some_rows(own * half, half), :] = outer_half[...]
+    first = [(inner_half, wi.at[some_rows(own * shard, shard), :])]
+    second = [(outer_half, wo2.at[some_rows(own * half, half), :])]
     for index, piece in enumerate(pieces):
         row, spot = (own + 1 + index // 4) & 3, quarter ^ (index % 4)
         rows = some_rows(row * shard + part * spot, part)
-        wi_full[rows, 0:dim] = piece[0:part, :]
-        wi_full[rows, dim:] = piece[part : 2 * part, :]
-        wo2_full[some_rows(row * half + step * spot, step), :] = piece[
-            2 * part : 2 * part + step, :
-        ]
+        for side in range(2):
+            first.append(
+                (
+                    piece.at[side * part : (side + 1) * part, :],
+                    wi.at[rows, side * dim : (side + 1) * dim],
+                )
+            )
+        rows = some_rows(row * half + step * spot, step)
+        second.append((piece.at[2 * part : 2 * part + step, :], wo2.at[rows, :]))
+    copies = [
+        pltpu.make_async_copy(source, target, sems.at[index])
+        for index, (source, target) in enumerate(first + second)
+    ]
+    for copy in copies:
+        copy.start()
+    for copy in copies[: len(first)]:
+        copy.wait()
+    back = [
+        pltpu.make_async_copy(wi, wi_full, sems.at[len(copies)]),
+        pltpu.make_async_copy(wo2, wo2_full, sems.at[len(copies) + 1]),
+    ]
+    back[0].start()
     count = near.shape[0]
     chunk = 512
+    waiting = True
     for index, (source, out) in enumerate(((far, send), (near, keep))):
         at = (1 - index) * count
         total = None
-        for lane in range(0, inner.shape[1], chunk):
+        for lane in range(0, slope.shape[1], chunk):
             lanes = slice(lane, lane + chunk)
-            value = dot(source[...], wi_full[:, lanes]) + bias[:, lanes]
-            inner[at : at + count, lanes] = value
-            low = short(gelu(value))
+            value, rate = gelu_parts(dot(source[...], wi[:, lanes]) + bias[:, lanes])
+            low = short(value)
+            slope[at : at + count, lanes] = short(rate)
             active[at : at + count, lanes] = low
-            added = dot(low, wo2_full[lanes, :])
+            if waiting:
+                for copy in copies[len(first) :]:
+                    copy.wait()
+                back[1].start()
+                waiting = False
+            added = dot(low, wo2[lanes, :])
             total = added if total is None else total + added
         out[...] = total
+    for copy in back:
+        copy.wait()
 
 
 def turnaround_kernel(first_sum, keep, got, vec, cot0, cot1, out0, out1, dsecond, douter, sums):
@@ -782,18 +828,24 @@
     sums[3:, :] = jnp.zeros_like(sums[3:, :])
 
 
-def backward_kernel(near, far, inner, wi_full, wo2_full, keep, send, dinner, sums):
+def backward_kernel(near, far, slope, wo2, wi_full, keep, send, dinner, sums, wi, sem):
+    copy = pltpu.make_async_copy(wi_full, wi, sem)
+    copy.start()
     count, dim = near.shape
     chunk = 512
+    waiting = True
     for index, (source, out) in enumerate(((far, send), (near, keep))):
         at = (1 - index) * count
         total = None
-        for lane in range(0, inner.shape[1], chunk):
+        for lane in range(0, slope.shape[1], chunk):
             lanes = slice(lane, lane + chunk)
-            slope = gelu_slope(inner[at : at + count, lanes])
-            low = short(dot_back(source[...], wo2_full[lanes, :]) * slope)
+            rate = wide(slope[at : at + count, lanes])
+            low = short(dot_back(source[...], wo2[lanes, :]) * rate)
             dinner[at : at + count, lanes] = low
-            added = dot_back(low, wi_full[:, lanes])
+            if waiting:
+                copy.wait()
+                waiting = False
+            added = dot_back(low, wi[:, lanes])
             total = added if total is None else total + added
         out[...] = total
     total = jnp.sum(wide(dinner[...]), axis=0, keepdims=True)
@@ -974,8 +1026,8 @@
 
 
 def attend_back_kernel(
-    bounds, qkv, logsum0, logsum1, seg_col, seg_row, p0, p1, p2, p3, mine, other, far, weight,
-    h0, h1, h2, h3, keep, send, grads, dqueries, dkeys, dvalues, dweight, dmixed, logsum, whole,
+    bounds, qkv, logsum0, logsum1, seg_col, seg_row, p0, p1, p2, p3, mine, other, far,
+    h0, h1, h2, h3, grads, dqueries, dkeys, dvalues, dweight, dmixed, logsum, whole,
 ):
     _, quarter, _, own = where_am_i()
     ctx = lax.axis_index("ctx")
@@ -1048,6 +1100,10 @@
         take = pl.ds(pl.multiple_of(((own - index) & 3) * width, 16), width)
         out[0:width, :] = dweight[take, :].astype(out.dtype)
         out[width:, :] = tail.astype(out.dtype)
+
+
+def tokens_kernel(grads, weight, keep, send):
+    rows = keep.shape[0]
     keep[...] = dot_back(grads[:rows], weight[...])
     send[...] = short(dot_back(grads[rows:], weight[...]))
 
@@ -1125,16 +1181,15 @@
     vec = jnp.zeros((16, shard), BF)
     for index, value in enumerate(vector_list):
         vec = jnp.where(line == index, value[None, :], vec)
-    heads_own, heads_send, w2_send, inner_half, outer_half = run(
+    heads_own, heads_send = run(
+        prepare_heads_kernel,
+        [((shard, 3 * shard), BF), ((shard // 2 + 16, 3 * shard), BF)],
+        (query_weight, key_weight, value_weight, vec),
+    )
+    w2_send, inner_half, outer_half = run(
         prepare_kernel,
-        [
-            ((shard, 3 * shard), BF),
-            ((shard // 2 + 16, 3 * shard), BF),
-            ((shard // 4 * 3 + half // 4, dim), BF),
-            ((shard, 4 * half), BF),
-            ((half, dim), BF),
-        ],
-        (query_weight, key_weight, value_weight, out_weight, inner_weight, outer_weight, vec),
+        [((shard // 4 * 3 + half // 4, dim), BF), ((shard, 4 * half), BF), ((half, dim), BF)],
+        (out_weight, inner_weight, outer_weight),
     )
     got = [turn(heads_send, step) for step in (1, 2, 3)]
     gone = [flip(value, 4) for value in got]
@@ -1185,20 +1240,29 @@
     first_sum, first_low, out_full = run(
         project_kernel,
         [((count, dim), F32), ((count, dim), BF), ((dim, dim), BF)],
-        (*mixed, mine, out_weight, vectors, *pieces),
+        (*mixed, mine, vectors, out_weight, *pieces),
+        [pltpu.SemaphoreType.DMA((13,))],
+        specs=[WHOLE] * 6 + [LEFT] * 13,
     )
     first_far = flip(first_low, 1)
-    keep, send, inner, active, wi_full, wo2_full = run(
+    keep, send, slope, active, wi_full, wo2_full = run(
         forward_kernel,
         [
             ((count, dim), F32),
             ((count, dim), F32),
-            ((2 * count, 4 * half), F32),
+            ((2 * count, 4 * half), BF),
             ((2 * count, 4 * half), BF),
             ((dim, 4 * half), BF),
             ((4 * half, dim), BF),
         ],
-        (first_low, first_far, inner_half, outer_half, inner_b, *pieces),
+        (first_low, first_far, inner_b, inner_half, outer_half, *pieces),
+        [
+            pltpu.VMEM((dim, 4 * half), BF),
+            pltpu.VMEM((4 * half, dim), BF),
+            pltpu.SemaphoreType.DMA((40,)),
+        ],
+        specs=[WHOLE] * 3 + [LEFT] * 14,
+        out_specs=[WHOLE] * 4 + [LEFT] * 2,
     )
     cot = pick(cotangent[:, 0], y), flip(pick(cotangent[:, 0], 1 - y), 4)
     out0, out1, dsecond, douter, sums2 = run(
@@ -1223,7 +1287,9 @@
             ((2 * count, 4 * half), BF),
             ((8, dim), F32),
         ],
-        (douter, douter_far, inner, wi_full, wo2_full),
+        (douter, douter_far, slope, wo2_full, wi_full),
+        [pltpu.VMEM((dim, 4 * half), BF), pltpu.SemaphoreType.DMA],
+        specs=[WHOLE] * 4 + [LEFT],
     )
     dfirst_sum, dbranch, d0, d1, d2, d3, sums1 = run(
         branch_kernel,
@@ -1248,14 +1314,13 @@
     ck, cz = run(out_split_kernel, [((dim // 2 + 32, dim // 2), BF)] * 2, (ck, flip(cz, 1)))
     cr = flip(cz, 2)
 
-    h0, h1, h2, h3, keep, send = run(
+    h0, h1, h2, h3, grads = run(
         attend_back_kernel,
         [((shard + 16, 3 * shard), F32)]
         + [((shard + 16, 3 * shard), BF)] * 3
-        + [((2 * count, dim), F32), ((2 * count, dim), BF)],
-        (qkv, logsum0, logsum1, *segs, *dmixed, mine, other, far, heads_weight),
+        + [((4 * count, 3 * shard), BF)],
+        (qkv, logsum0, logsum1, *segs, *dmixed, mine, other, far),
         [
-            pltpu.VMEM((4 * count, 3 * shard), BF),
             pltpu.VMEM((3, 4 * count, HEAD_DIM), BF),
             pltpu.VMEM((3, 4 * count, HEAD_DIM), F32),
             pltpu.VMEM((3, 4 * count, HEAD_DIM), F32),
@@ -1265,6 +1330,9 @@
             pltpu.VMEM((total, 3 * shard), BF),
         ],
         scalars=(bounds,),
+    )
+    keep, send = run(
+        tokens_kernel, [((2 * count, dim), F32), ((2 * count, dim), BF)], (grads, heads_weight)
     )
 
     c2k, c2z = run(reduce_out_kernel, [((dim // 4 + 32, dim // 2), BF)] * 2, (ck, cr))

time: 351 us -> 348 us (level)
  waiting for transfers between devices: 130 us -> 123 us
    ppermute x15, waiting for transfers between devices: 52.5 us -> 45.6 us  [turn(): return lax.ppermute(value, 'wt', [(i, (i - step) % 4) for i in range(4)])]
    pallas_call x23 -> x25, Pallas kernels: 115 us -> 118 us  [run(): pl.pallas_call(kernel, out_shape=shapes, in_specs=in_specs, out_specs=tup...]
  transfers between devices with their start and end apart: 72 -> 72, of which waited for: 27 -> 27; matrix products, arithmetic and copies ran while one was open for 3% -> 3% of each run, Pallas kernels for 23% -> 25%
where the time goes in v1:
time: 348 us; the launch traced here: 347 us
  waiting for transfers between devices  123 us (35%)
  Pallas kernels  118 us (34%)
  starting transfers between devices  77.5 us (22%)
  local copies, waits for them, and re-layouts  21.4 us (6%)
  other arithmetic  5.81 us (2%)
    pallas_call x25, Pallas kernels, run(): pl.pallas_call(kernel, out_shape=shapes, in_specs=in_specs, out_specs=tup...  118 us
    ppermute x57, waiting for transfers between devices, flip(): return lax.ppermute(value, 'ctx', [(i, i ^ bits) for i in range(8)])  77.1 us
    ppermute x57, starting transfers between devices, flip(): return lax.ppermute(value, 'ctx', [(i, i ^ bits) for i in range(8)])  49.3 us
    ppermute x15, waiting for transfers between devices, turn(): return lax.ppermute(value, 'wt', [(i, (i - step) % 4) for i in range(4)])  45.6 us
    ppermute x15, starting transfers between devices, turn(): return lax.ppermute(value, 'wt', [(i, (i - step) % 4) for i in range(4)])  28.2 us
    unnamed x159, local copies, waits for them, and re-layouts  11.8 us
  transfers between devices with their start and end apart: 72, of which 27 were waited for; matrix products, arithmetic and copies ran while one was open for 3% of the time, Pallas kernels for 25%

profile of v1, /device:TPU:0, one launch (start us, length us, event | category | flops | bytes accessed | tf_op | source)
XLA Modules:
  0.0 347.0 jit_solution(16562994985210962201)
XLA Ops:
  3.2 2.0 shard_map.305
  5.2 5.1 %collective-permute-start.3 = (bf16[112,576]{1,0:T(8,128)(2,1)}, bf16[112,576]{1,0:T(8,128)(2,1)S(1)}, u32[]{:S(2)}, u32[]{:S(2)}) collective-permute-start(bf16[112,576]{1,0:T(8,128)(2,1)} %get-tuple-element.99), channel_id=1, source_target_pairs={{0,3},{1,0},{2,1},{3,2},{4,7},{5,4},{6,5},{7,6},{8,11},{9,8},{10,9... | collective-permute-start | bytes 387080 | tf_op jit(solution)/shard_map/ppermute | solution.py:508
  11.3 3.0 shard_map.308
  14.3 2.8 collective-permute-start.12
  20.0 3.5 collective-permute-done.4.g2
  23.4 1.5 collective-permute-start
  24.9 4.1 %collective-permute-done = bf16[128,768]{1,0:T(8,128)(2,1)S(1)} collective-permute-done((bf16[128,768]{1,0:T(8,128)(2,1)S(1)}, bf16[128,768]{1,0:T(8,128)(2,1)S(1)}, u32[]{:S(2)}, u32[]{:S(2)}) %collective-permute-start) | collective-permute-done | bytes 196640 | tf_op jit(solution)/shard_map/ppermute | solution.py:504
  29.1 1.5 collective-permute-start.6
  30.7 1.6 collective-permute-start.1
  32.3 2.6 collective-permute-done.6.h1
  34.9 1.5 collective-permute-start.7
  36.4 3.2 collective-permute-done.1.other
  39.9 1.6 collective-permute-start.13
  41.5 1.9 collective-permute-start.14
  43.4 4.0 %collective-permute-done.8.h3 = bf16[112,576]{1,0:T(8,128)(2,1)S(1)} collective-permute-done((bf16[112,576]{1,0:T(8,128)(2,1)S(1)}, bf16[112,576]{1,0:T(8,128)(2,1)S(1)}, u32[]{:S(2)}, u32[]{:S(2)}) %collective-permute-start.8) | collective-permute-done | bytes 129056 | tf_op jit(solution)/shard_map/ppermute | solution.py:504
  48.8 5.5 %collective-permute-done.16.refs_4_ = bf16[240,768]{1,0:T(8,128)(2,1)S(1)} collective-permute-done((bf16[240,768]{1,0:T(8,128)(2,1)}, bf16[240,768]{1,0:T(8,128)(2,1)S(1)}, u32[]{:S(2)}, u32[]{:S(2)}) %collective-permute-start.16) | collective-permute-done | bytes 368672 | tf_op jit(solution)/shard_map/ppermute | solution.py:508
  57.2 1.5 collective-permute-start.18
  58.9 1.7 collective-permute-start.19
  61.8 4.7 %collective-permute-done.17.refs_5_ = bf16[240,768]{1,0:T(8,128)(2,1)S(1)} collective-permute-done((bf16[240,768]{1,0:T(8,128)(2,1)S(1)}, bf16[240,768]{1,0:T(8,128)(2,1)S(1)}, u32[]{:S(2)}, u32[]{:S(2)}) %collective-permute-start.17) | collective-permute-done | bytes 368672 | tf_op jit(solution)/shard_map/ppermute | solution.py:504
  70.3 10.4 %shard_map.306 = (bf16[9,1024,64]{2,1,0:T(8,128)(2,1)}, bf16[256,192]{1,0:T(8,128)(2,1)}, bf16[256,192]{1,0:T(8,128)(2,1)}, f32[512,128]{1,0:T(8,128)}, bf16[768,576]{1,0:T(8,128)(2,1)}) custom-call(bf16[256,768]{1,0:T(8,128)(2,1)} %copy-done, bf16[256,768]{1,0:T(8,128)(2,1)} %copy-done.1, bf16[512,768]{1,0:T(8,128)(2,1)} %copy-done.2, ...), custom_call_target="tpu_custom_call" | custom-call | tf_op jit(solution)/shard_map/pallas_call | solution.py:569
  80.7 7.9 %shard_map.307 = (bf16[256,192]{1,0:T(8,128)(2,1)}, bf16[256,192]{1,0:T(8,128)(2,1)}, f32[512,128]{1,0:T(8,128)}) custom-call(bf16[9,1024,64]{2,1,0:T(8,128)(2,1)} %get-tuple-element.102.qkv, s32[1024,1]{1,0:T(8,128)} %copy.45.seg_col, s32[1,1024]{1,0:T(1,128)} %bitcast.75), custom_call_target="tpu_custom_call" | custom-call | tf_op jit(solution)/shard_map/pallas_call | solution.py:569
  89.2 1.6 collective-permute-start.9
  91.8 3.4 collective-permute-done.10.m2
  95.9 4.7 %shard_map.309 = (f32[256,768]{1,0:T(8,128)}, bf16[256,768]{1,0:T(8,128)(2,1)}, bf16[768,768]{1,0:T(8,128)(2,1)}) custom-call(bf16[256,192]{1,0:T(8,128)(2,1)} %get-tuple-element.100.m0, bf16[256,192]{1,0:T(8,128)(2,1)} %copy-done.20, bf16[256,192]{1,0:T(8,128)(2,1)} %copy-done.18, bf16[256,192]{1,0:T(8,128)(2,1)} %copy-done.19, bf16[256,768]{1,0:T(8,128)(2,1)} %copy-done, ...), custom_call_target="tpu_custom_call" | custom-call | tf_op jit(solution)/shard_map/pallas_call | solution.py:569
  104.2 9.1 %shard_map.310 = (f32[256,768]{1,0:T(8,128)}, f32[256,768]{1,0:T(8,128)}, bf16[512,1536]{1,0:T(8,128)(2,1)}, bf16[512,1536]{1,0:T(8,128)(2,1)}, bf16[768,1536]{1,0:T(8,128)(2,1)}, /*index=5*/bf16[1536,768]{1,0:T(8,128)(2,1)}) custom-call(bf16[256,768]{1,0:T(8,128)(2,1)} %get-tuple-element.107.near.first0, bf16[256,768]{1,0:T(8,128)(2,1)} %copy-done.3, ...), custom_call_target="tpu_custom_call" | custom-call | tf_op jit(solution)/shard_map/pallas_call | solution.py:569
  116.0 5.4 %collective-permute-done.26.cot1 = bf16[128,768]{1,0:T(8,128)(2,1)S(1)} collective-permute-done((bf16[128,768]{1,0:T(8,128)(2,1)S(1)}, bf16[128,768]{1,0:T(8,128)(2,1)S(1)}, u32[]{:S(2)}, u32[]{:S(2)}) %collective-permute-start.26) | collective-permute-done | bytes 196640 | tf_op jit(solution)/shard_map/ppermute | solution.py:504
  122.4 3.7 %shard_map.311 = (bf16[128,768]{1,0:T(8,128)(2,1)}, bf16[128,768]{1,0:T(8,128)(2,1)}, f32[256,768]{1,0:T(8,128)}, bf16[256,768]{1,0:T(8,128)(2,1)}, f32[8,768]{1,0:T(8,128)}) custom-call(f32[256,768]{1,0:T(8,128)} %get-tuple-element.106.first_sum, f32[256,768]{1,0:T(8,128)} %get-tuple-element.110.keep, f32[256,768]{1,0:T(8,128)} %copy-done.16, ...), custom_call_target="tpu_custom_call" | custom-call | tf_op jit(solution)/shard_map/pallas_call | solution.py:569
  126.2 1.9 collective-permute-done.28.far.douter1
  128.8 8.1 %shard_map.312 = (f32[256,768]{1,0:T(8,128)}, f32[256,768]{1,0:T(8,128)}, bf16[512,1536]{1,0:T(8,128)(2,1)}, f32[8,768]{1,0:T(8,128)}) custom-call(bf16[256,768]{1,0:T(8,128)(2,1)} %get-tuple-element.117.near.douter0, bf16[256,768]{1,0:T(8,128)(2,1)} %copy-done.4, bf16[512,1536]{1,0:T(8,128)(2,1)} %get-tuple-element.118.slope, ...), custom_call_target="tpu_custom_call" | custom-call | tf_op jit(solution)/shard_map/pallas_call | solution.py:569
  137.2 7.3 %shard_map.320 = (bf16[384,1536]{1,0:T(8,128)(2,1)}, bf16[384,1536]{1,0:T(8,128)(2,1)}, bf16[768,768]{1,0:T(8,128)(2,1)}, bf16[768,768]{1,0:T(8,128)(2,1)}) custom-call(bf16[256,768]{1,0:T(8,128)(2,1)} %get-tuple-element.107.near.first0, bf16[256,768]{1,0:T(8,128)(2,1)} %copy-done.3, bf16[256,768]{1,0:T(8,128)(2,1)} %get-tuple-element.117.near.douter0, ...), custom_call_target="tpu_custom_call" | custom-call | tf_op jit(solution)/shard_map/pallas_call | solution.py:569
  145.1 1.5 collective-permute-start.44
  147.7 4.4 %shard_map.313 = (f32[256,768]{1,0:T(8,128)}, bf16[256,768]{1,0:T(8,128)(2,1)}, bf16[256,192]{1,0:T(8,128)(2,1)}, bf16[256,192]{1,0:T(8,128)(2,1)}, bf16[256,192...) custom-call(f32[256,768]{1,0:T(8,128)} %get-tuple-element.106.first_sum, ...), custom_call_target="tpu_custom_call" | custom-call | tf_op jit(solution)/shard_map/pallas_call | solution.py:569
  152.1 3.0 shard_map.324
  157.6 18.7 %collective-permute-done.31.p2 = bf16[256,192]{1,0:T(8,128)(2,1)S(1)} collective-permute-done((bf16[256,192]{1,0:T(8,128)(2,1)}, bf16[256,192]{1,0:T(8,128)(2,1)S(1)}, u32[]{:S(2)}, u32[]{:S(2)}) %collective-permute-start.31) | collective-permute-done | bytes 98336 | tf_op jit(solution)/shard_map/ppermute | solution.py:504
  176.3 1.6 collective-permute-done.32.p3
  178.6 19.2 %shard_map.314 = (f32[208,576]{1,0:T(8,128)}, bf16[208,576]{1,0:T(8,128)(2,1)}, bf16[208,576]{1,0:T(8,128)(2,1)}, bf16[208,576]{1,0:T(8,128)(2,1)}, bf16[1024,576]{1,0:T(8,128)(2,1)}) custom-call(s32[2,4]{1,0:T(2,128)} %pad_add_fusion.bounds, bf16[9,1024,64]{2,1,0:T(8,128)(2,1)} %get-tuple-element.102.qkv, f32[512,128]{1,0:T(8,128)} %get-tuple-element.114.logsum0, ...), custom_call_target="tpu_custom_call" | custom-call | tf_op jit(solution)/shard_map/pallas_call | solution.py:569
  197.8 3.7 %collective-permute-start.36 = (bf16[208,576]{1,0:T(8,128)(2,1)}, bf16[208,576]{1,0:T(8,128)(2,1)S(1)}, u32[]{:S(2)}, u32[]{:S(2)}) collective-permute-start(bf16[208,576]{1,0:T(8,128)(2,1)} %get-tuple-element.136), channel_id=1, source_target_pairs={{0,3},{1,0},{2,1},{3,2},{4,7},{5,4},{6,5},{7,6},{8,11},{9,8},{10,9... | collective-permute-start | bytes 718856 | tf_op jit(solution)/shard_map/ppermute | solution.py:508
  201.5 9.9 %collective-permute-start.37 = (bf16[208,576]{1,0:T(8,128)(2,1)}, bf16[208,576]{1,0:T(8,128)(2,1)S(1)}, u32[]{:S(2)}, u32[]{:S(2)}) collective-permute-start(bf16[208,576]{1,0:T(8,128)(2,1)} %get-tuple-element.137), channel_id=1, source_target_pairs={{0,2},{1,3},{2,0},{3,1},{4,6},{5,7},{6,4},{7,5},{8,10},{9,11},{10,... | collective-permute-start | bytes 718856 | tf_op jit(solution)/shard_map/ppermute | solution.py:508
  211.4 4.7 %collective-permute-done.36.refs_0_ = bf16[208,576]{1,0:T(8,128)(2,1)S(1)} collective-permute-done((bf16[208,576]{1,0:T(8,128)(2,1)}, bf16[208,576]{1,0:T(8,128)(2,1)S(1)}, u32[]{:S(2)}, u32[]{:S(2)}) %collective-permute-start.36) | collective-permute-done | bytes 239648 | tf_op jit(solution)/shard_map/ppermute | solution.py:508
  216.1 3.2 collective-permute-start.38
  219.4 4.0 %shard_map.315 = (f32[512,768]{1,0:T(8,128)}, bf16[512,768]{1,0:T(8,128)(2,1)}) custom-call(bf16[1024,576]{1,0:T(8,128)(2,1)} %get-tuple-element.128.grads, bf16[768,576]{1,0:T(8,128)(2,1)} %get-tuple-element.129.weight), custom_call_target="tpu_custom_call" | custom-call | tf_op jit(solution)/shard_map/pallas_call | solution.py:569
  223.4 12.3 %collective-permute-done.37.refs_1_ = bf16[208,576]{1,0:T(8,128)(2,1)S(1)} collective-permute-done((bf16[208,576]{1,0:T(8,128)(2,1)}, bf16[208,576]{1,0:T(8,128)(2,1)S(1)}, u32[]{:S(2)}, u32[]{:S(2)}) %collective-permute-start.37) | collective-permute-done | bytes 239648 | tf_op jit(solution)/shard_map/ppermute | solution.py:508
  236.3 2.1 shard_map.317.mine
  240.8 4.1 %shard_map.321 = (bf16[192,768]{1,0:T(8,128)(2,1)}, bf16[192,768]{1,0:T(8,128)(2,1)}, bf16[384,384]{1,0:T(8,128)(2,1)}, bf16[384,384]{1,0:T(8,128)(2,1)}, bf16[1...) custom-call(bf16[384,1536]{1,0:T(8,128)(2,1)} %get-tuple-element.145.ak, ...), custom_call_target="tpu_custom_call" | custom-call | tf_op jit(solution)/shard_map/pallas_call | solution.py:569
  247.6 2.2 shard_map.325
  251.2 1.8 shard_map.318.s0
  253.0 5.5 %collective-permute-done.27 = bf16[128,768]{1,0:T(8,128)(2,1)} collective-permute-done((bf16[128,768]{1,0:T(8,128)(2,1)}, bf16[128,768]{1,0:T(8,128)(2,1)}, u32[]{:S(2)}, u32[]{:S(2)}) %collective-permute-start.27) | collective-permute-done | bytes 196640 | tf_op jit(solution)/shard_map/ppermute | solution.py:504
  260.4 2.2 shard_map.322
  262.6 5.4 %collective-permute-done.41.s2 = bf16[208,576]{1,0:T(8,128)(2,1)S(1)} collective-permute-done((bf16[208,576]{1,0:T(8,128)(2,1)}, bf16[208,576]{1,0:T(8,128)(2,1)S(1)}, u32[]{:S(2)}, u32[]{:S(2)}) %collective-permute-start.41) | collective-permute-done | bytes 239648 | tf_op jit(solution)/shard_map/ppermute | solution.py:504
  268.1 4.7 %collective-permute-done.42.s3 = bf16[208,576]{1,0:T(8,128)(2,1)S(1)} collective-permute-done((bf16[208,576]{1,0:T(8,128)(2,1)}, bf16[208,576]{1,0:T(8,128)(2,1)S(1)}, u32[]{:S(2)}, u32[]{:S(2)}) %collective-permute-start.42) | collective-permute-done | bytes 239648 | tf_op jit(solution)/shard_map/ppermute | solution.py:504
  274.6 1.9 shard_map.326
  277.5 3.0 shard_map.316
  282.5 1.8 maximum_select_fusion.1
  284.4 3.2 shard_map.319
  287.6 1.8 collective-permute-done.49.refs_2_
  290.0 1.9 shard_map.323.refs_0_
  294.6 2.4 shard_map.327
  299.4 1.8 collective-permute-start.52
  303.2 16.5 %collective-permute-done.63.refs_1_ = bf16[144,768]{1,0:T(8,128)(2,1)S(1)} collective-permute-done((bf16[144,768]{1,0:T(8,128)(2,1)}, bf16[144,768]{1,0:T(8,128)(2,1)S(1)}, u32[]{:S(2)}, u32[]{:S(2)}) %collective-permute-start.63) | collective-permute-done | bytes 221216 | tf_op jit(solution)/shard_map/ppermute | solution.py:508
  320.8 2.0 shard_map.328.refs_8_
  324.6 1.8 collective-permute-start.67
  327.6 3.8 %collective-permute-done.65.refs_9_ = bf16[144,768]{1,0:T(8,128)(2,1)S(1)} collective-permute-done((bf16[144,768]{1,0:T(8,128)(2,1)}, bf16[144,768]{1,0:T(8,128)(2,1)S(1)}, u32[]{:S(2)}, u32[]{:S(2)}) %collective-permute-start.65) | collective-permute-done | bytes 221216 | tf_op jit(solution)/shard_map/ppermute | solution.py:504
  331.4 5.1 %collective-permute-done.66.refs_10_ = bf16[144,768]{1,0:T(8,128)(2,1)S(1)} collective-permute-done((bf16[144,768]{1,0:T(8,128)(2,1)}, bf16[144,768]{1,0:T(8,128)(2,1)S(1)}, u32[]{:S(2)}, u32[]{:S(2)}) %collective-permute-start.66) | collective-permute-done | bytes 221216 | tf_op jit(solution)/shard_map/ppermute | solution.py:504
  339.6 4.6 %shard_map.329 = (f32[192,3072]{1,0:T(8,128)}, f32[768,768]{1,0:T(8,128)}, f32[192,768]{1,0:T(8,128)}, f32[16,768]{1,0:T(8,128)}) custom-call(bf16[96,768]{1,0:T(8,128)(2,1)} %shard_map.323.refs_0_, bf16[96,768]{1,0:T(8,128)(2,1)} %copy-done.52, bf16[96,768]{1,0:T(8,128)(2,1)} %collective-permute-done.51.refs_2_, bf16[96,768]{1,0:T(8,128)(2,1)} %copy-done.53, ...), custom_call_target="tpu_custom_call" | custom-call | tf_op jit(solution)/shard_map/pallas_call | solution.py:569
  (315 shorter events, 62.8 us)
Async XLA Ops:
  5.2 14.6 %collective-permute-start.3 = (bf16[112,576]{1,0:T(8,128)(2,1)}, bf16[112,576]{1,0:T(8,128)(2,1)S(1)}, u32[]{:S(2)}, u32[]{:S(2)}) collective-permute-start(bf16[112,576]{1,0:T(8,128)(2,1)} %get-tuple-element.99), channel_id=1, source_target_pairs={{0,3},{1,0},{2,1},{3,2},{4,7},{5,4},{6,5},{7,6},{8,11},{9,8},{10,9... | collective-permute-start | bytes 387080 | tf_op jit(solution)/shard_map/ppermute | solution.py:508
  10.3 13.1 %collective-permute-start.4 = (bf16[112,576]{1,0:T(8,128)(2,1)}, bf16[112,576]{1,0:T(8,128)(2,1)S(1)}, u32[]{:S(2)}, u32[]{:S(2)}) collective-permute-start(bf16[112,576]{1,0:T(8,128)(2,1)} %get-tuple-element.99), channel_id=1, source_target_pairs={{0,2},{1,3},{2,0},{3,1},{4,6},{5,7},{6,4},{7,5},{8,10},{9,11},{10,... | collective-permute-start | bytes 387080 | tf_op jit(solution)/shard_map/ppermute | solution.py:508
  10.3 20.3 %collective-permute-start.5 = (bf16[112,576]{1,0:T(8,128)(2,1)}, bf16[112,576]{1,0:T(8,128)(2,1)S(1)}, u32[]{:S(2)}, u32[]{:S(2)}) collective-permute-start(bf16[112,576]{1,0:T(8,128)(2,1)} %get-tuple-element.99), channel_id=1, source_target_pairs={{0,1},{1,2},{2,3},{3,0},{4,5},{5,6},{6,7},{7,4},{8,9},{9,10},{10,1... | collective-permute-start | bytes 387080 | tf_op jit(solution)/shard_map/ppermute | solution.py:508
  14.3 25.6 %collective-permute-start.12 = (bf16[240,768]{1,0:T(8,128)(2,1)}, bf16[240,768]{1,0:T(8,128)(2,1)S(1)}, u32[]{:S(2)}, u32[]{:S(2)}) collective-permute-start(bf16[240,768]{1,0:T(8,128)(2,1)} %get-tuple-element.105), channel_id=1, source_target_pairs={{0,3},{1,0},{2,1},{3,2},{4,7},{5,4},{6,5},{7,6},{8,11},{9,8},{10,9... | collective-permute-start | bytes 1105928 | tf_op jit(solution)/shard_map/ppermute | solution.py:508
  17.1 37.2 %collective-permute-start.16 = (bf16[240,768]{1,0:T(8,128)(2,1)}, bf16[240,768]{1,0:T(8,128)(2,1)S(1)}, u32[]{:S(2)}, u32[]{:S(2)}) collective-permute-start(bf16[240,768]{1,0:T(8,128)(2,1)} %get-tuple-element.105), channel_id=1, source_target_pairs={{0,2},{1,3},{2,0},{3,1},{4,6},{5,7},{6,4},{7,5},{8,10},{9,11},{10,... | collective-permute-start | bytes 1105928 | tf_op jit(solution)/shard_map/ppermute | solution.py:508
  19.9 35.2 %collective-permute-start.20 = (bf16[240,768]{1,0:T(8,128)(2,1)}, bf16[240,768]{1,0:T(8,128)(2,1)S(1)}, u32[]{:S(2)}, u32[]{:S(2)}) collective-permute-start(bf16[240,768]{1,0:T(8,128)(2,1)} %get-tuple-element.105), channel_id=1, source_target_pairs={{0,1},{1,2},{2,3},{3,0},{4,5},{5,6},{6,7},{7,4},{8,9},{9,10},{10,1... | collective-permute-start | bytes 1105928 | tf_op jit(solution)/shard_map/ppermute | solution.py:508
  30.7 9.0 %collective-permute-start.1 = (bf16[256,768]{1,0:T(8,128)(2,1)S(1)}, bf16[256,768]{1,0:T(8,128)(2,1)S(1)}, u32[]{:S(2)}, u32[]{:S(2)}) collective-permute-start(bf16[256,768]{1,0:T(8,128)(2,1)S(1)} %pad_maximum_fusion.1.mine), channel_id=1, source_target_pairs={{0,8},{4,12},{8,0},{12,4},{16,24},{20,28},{24,16},{28,20},{1,9},{5... | collective-permute-start | bytes 1179656 | tf_op jit(solution)/shard_map/ppermute | solution.py:504
  34.9 6.6 %collective-permute-start.7 = (bf16[112,576]{1,0:T(8,128)(2,1)S(1)}, bf16[112,576]{1,0:T(8,128)(2,1)S(1)}, u32[]{:S(2)}, u32[]{:S(2)}) collective-permute-start(bf16[112,576]{1,0:T(8,128)(2,1)S(1)} %collective-permute-done.4.g2), channel_id=1, source_target_pairs={{0,16},{4,20},{8,24},{12,28},{16,0},{20,4},{24,8},{28,12},{1,17},{... | collective-permute-start | bytes 387080 | tf_op jit(solution)/shard_map/ppermute | solution.py:504
  39.6 7.8 %collective-permute-start.8 = (bf16[112,576]{1,0:T(8,128)(2,1)S(1)}, bf16[112,576]{1,0:T(8,128)(2,1)S(1)}, u32[]{:S(2)}, u32[]{:S(2)}) collective-permute-start(bf16[112,576]{1,0:T(8,128)(2,1)S(1)} %collective-permute-done.5.g3), channel_id=1, source_target_pairs={{0,16},{4,20},{8,24},{12,28},{16,0},{20,4},{24,8},{28,12},{1,17},{... | collective-permute-start | bytes 387080 | tf_op jit(solution)/shard_map/ppermute | solution.py:504
  39.9 17.3 %collective-permute-start.13 = (bf16[240,768]{1,0:T(8,128)(2,1)S(1)}, bf16[240,768]{1,0:T(8,128)(2,1)S(1)}, u32[]{:S(2)}, u32[]{:S(2)}) collective-permute-start(bf16[240,768]{1,0:T(8,128)(2,1)S(1)} %collective-permute-done.12.refs_0_), channel_id=1, source_target_pairs={{0,8},{4,12},{8,0},{12,4},{16,24},{20,28},{24,16},{28,20},{1,9},{5... | collective-permute-start | bytes 1105928 | tf_op jit(solution)/shard_map/ppermute | solution.py:504
  41.5 17.3 %collective-permute-start.14 = (bf16[240,768]{1,0:T(8,128)(2,1)S(1)}, bf16[240,768]{1,0:T(8,128)(2,1)S(1)}, u32[]{:S(2)}, u32[]{:S(2)}) collective-permute-start(bf16[240,768]{1,0:T(8,128)(2,1)S(1)} %collective-permute-done.12.refs_0_), channel_id=1, source_target_pairs={{0,16},{4,20},{8,24},{12,28},{16,0},{20,4},{24,8},{28,12},{1,17},{... | collective-permute-start | bytes 1105928 | tf_op jit(solution)/shard_map/ppermute | solution.py:504
  47.4 13.1 %collective-permute-start.15 = (bf16[240,768]{1,0:T(8,128)(2,1)S(1)}, bf16[240,768]{1,0:T(8,128)(2,1)S(1)}, u32[]{:S(2)}, u32[]{:S(2)}) collective-permute-start(bf16[240,768]{1,0:T(8,128)(2,1)S(1)} %collective-permute-done.12.refs_0_), channel_id=1, source_target_pairs={{0,24},{4,28},{8,16},{12,20},{16,8},{20,12},{24,0},{28,4},{1,25},{... | collective-permute-start | bytes 1105928 | tf_op jit(solution)/shard_map/ppermute | solution.py:504
  54.3 13.7 %collective-permute-start.2 = (bf16[512,768]{1,0:T(8,128)(2,1)S(1)}, bf16[512,768]{1,0:T(8,128)(2,1)S(1)}, u32[]{:S(2)}, u32[]{:S(2)}) collective-permute-start(bf16[512,768]{1,0:T(8,128)(2,1)S(1)} %pad_maximum_fusion), channel_id=1, source_target_pairs={{0,4},{4,0},{8,12},{12,8},{16,20},{20,16},{24,28},{28,24},{1,5},{5... | collective-permute-start | bytes 2359304 | tf_op jit(solution)/shard_map/ppermute | solution.py:504
  55.0 11.5 %collective-permute-start.17 = (bf16[240,768]{1,0:T(8,128)(2,1)S(1)}, bf16[240,768]{1,0:T(8,128)(2,1)S(1)}, u32[]{:S(2)}, u32[]{:S(2)}) collective-permute-start(bf16[240,768]{1,0:T(8,128)(2,1)S(1)} %collective-permute-done.16.refs_4_), channel_id=1, source_target_pairs={{0,8},{4,12},{8,0},{12,4},{16,24},{20,28},{24,16},{28,20},{1,9},{5... | collective-permute-start | bytes 1105928 | tf_op jit(solution)/shard_map/ppermute | solution.py:504
  57.2 31.4 %collective-permute-start.18 = (bf16[240,768]{1,0:T(8,128)(2,1)S(1)}, bf16[240,768]{1,0:T(8,128)(2,1)}, u32[]{:S(2)}, u32[]{:S(2)}) collective-permute-start(bf16[240,768]{1,0:T(8,128)(2,1)S(1)} %collective-permute-done.16.refs_4_), channel_id=1, source_target_pairs={{0,16},{4,20},{8,24},{12,28},{16,0},{20,4},{24,8},{28,12},{1,17},{... | collective-permute-start | bytes 1105928 | tf_op jit(solution)/shard_map/ppermute | solution.py:504
  58.9 30.3 %collective-permute-start.19 = (bf16[240,768]{1,0:T(8,128)(2,1)S(1)}, bf16[240,768]{1,0:T(8,128)(2,1)}, u32[]{:S(2)}, u32[]{:S(2)}) collective-permute-start(bf16[240,768]{1,0:T(8,128)(2,1)S(1)} %collective-permute-done.16.refs_4_), channel_id=1, source_target_pairs={{0,24},{4,28},{8,16},{12,20},{16,8},{20,12},{24,0},{28,4},{1,25},{... | collective-permute-start | bytes 1105928 | tf_op jit(solution)/shard_map/ppermute | solution.py:504
  60.5 28.6 %collective-permute-start.21 = (bf16[240,768]{1,0:T(8,128)(2,1)S(1)}, bf16[240,768]{1,0:T(8,128)(2,1)}, u32[]{:S(2)}, u32[]{:S(2)}) collective-permute-start(bf16[240,768]{1,0:T(8,128)(2,1)S(1)} %collective-permute-done.20.refs_8_), channel_id=1, source_target_pairs={{0,8},{4,12},{8,0},{12,4},{16,24},{20,28},{24,16},{28,20},{1,9},{5... | collective-permute-start | bytes 1105928 | tf_op jit(solution)/shard_map/ppermute | solution.py:504
  66.5 25.3 %collective-permute-start.22 = (bf16[240,768]{1,0:T(8,128)(2,1)S(1)}, bf16[240,768]{1,0:T(8,128)(2,1)}, u32[]{:S(2)}, u32[]{:S(2)}) collective-permute-start(bf16[240,768]{1,0:T(8,128)(2,1)S(1)} %collective-permute-done.20.refs_8_), channel_id=1, source_target_pairs={{0,16},{4,20},{8,24},{12,28},{16,0},{20,4},{24,8},{28,12},{1,17},{... | collective-permute-start | bytes 1105928 | tf_op jit(solution)/shard_map/ppermute | solution.py:504
  68.0 23.7 %collective-permute-start.23 = (bf16[240,768]{1,0:T(8,128)(2,1)S(1)}, bf16[240,768]{1,0:T(8,128)(2,1)}, u32[]{:S(2)}, u32[]{:S(2)}) collective-permute-start(bf16[240,768]{1,0:T(8,128)(2,1)S(1)} %collective-permute-done.20.refs_8_), channel_id=1, source_target_pairs={{0,24},{4,28},{8,16},{12,20},{16,8},{20,12},{24,0},{28,4},{1,25},{... | collective-permute-start | bytes 1105928 | tf_op jit(solution)/shard_map/ppermute | solution.py:504
  88.6 6.5 %collective-permute-start.10 = (bf16[256,192]{1,0:T(8,128)(2,1)}, bf16[256,192]{1,0:T(8,128)(2,1)S(1)}, u32[]{:S(2)}, u32[]{:S(2)}) collective-permute-start(bf16[256,192]{1,0:T(8,128)(2,1)} %get-tuple-element.103), channel_id=1, source_target_pairs={{0,8},{4,12},{8,0},{12,4},{16,24},{20,28},{24,16},{28,20},{1,9},{5... | collective-permute-start | bytes 294920 | tf_op jit(solution)/shard_map/ppermute | solution.py:504
  89.2 6.0 %collective-permute-start.11 = (bf16[256,192]{1,0:T(8,128)(2,1)}, bf16[256,192]{1,0:T(8,128)(2,1)S(1)}, u32[]{:S(2)}, u32[]{:S(2)}) collective-permute-start(bf16[256,192]{1,0:T(8,128)(2,1)} %get-tuple-element.104), channel_id=1, source_target_pairs={{0,12},{4,8},{8,4},{12,0},{16,28},{20,24},{24,20},{28,16},{1,13},{... | collective-permute-start | bytes 294920 | tf_op jit(solution)/shard_map/ppermute | solution.py:504
  89.2 6.0 %collective-permute-start.9 = (bf16[256,192]{1,0:T(8,128)(2,1)S(1)}, bf16[256,192]{1,0:T(8,128)(2,1)S(1)}, u32[]{:S(2)}, u32[]{:S(2)}) collective-permute-start(bf16[256,192]{1,0:T(8,128)(2,1)S(1)} %copy-done.76), channel_id=1, source_target_pairs={{0,4},{4,0},{8,12},{12,8},{16,20},{20,16},{24,28},{28,24},{1,5},{5... | collective-permute-start | bytes 294920 | tf_op jit(solution)/shard_map/ppermute | solution.py:504
  113.3 8.1 %collective-permute-start.25 = (f32[256,768]{1,0:T(8,128)}, f32[256,768]{1,0:T(8,128)S(1)}, u32[]{:S(2)}, u32[]{:S(2)}) collective-permute-start(f32[256,768]{1,0:T(8,128)} %get-tuple-element.111), channel_id=1, source_target_pairs={{0,4},{4,0},{8,12},{12,8},{16,20},{20,16},{24,28},{28,24},{1,5},{5... | collective-permute-start | bytes 2359304 | tf_op jit(solution)/shard_map/ppermute | solution.py:504
  114.5 6.9 %collective-permute-start.26 = (bf16[128,768]{1,0:T(8,128)(2,1)S(1)}, bf16[128,768]{1,0:T(8,128)(2,1)S(1)}, u32[]{:S(2)}, u32[]{:S(2)}) collective-permute-start(bf16[128,768]{1,0:T(8,128)(2,1)S(1)} %get-tuple-element.181), channel_id=1, source_target_pairs={{0,16},{4,20},{8,24},{12,28},{16,0},{20,4},{24,8},{28,12},{1,17},{... | collective-permute-start | bytes 589832 | tf_op jit(solution)/shard_map/ppermute | solution.py:504
  137.0 9.9 %collective-permute-start.29 = (f32[256,768]{1,0:T(8,128)}, f32[256,768]{1,0:T(8,128)S(1)}, u32[]{:S(2)}, u32[]{:S(2)}) collective-permute-start(f32[256,768]{1,0:T(8,128)} %get-tuple-element.122), channel_id=1, source_target_pairs={{0,4},{4,0},{8,12},{12,8},{16,20},{20,16},{24,28},{28,24},{1,5},{5... | collective-permute-start | bytes 2359304 | tf_op jit(solution)/shard_map/ppermute | solution.py:504
  144.4 94.9 %collective-permute-start.43 = (bf16[384,1536]{1,0:T(8,128)(2,1)}, bf16[384,1536]{1,0:T(8,128)(2,1)S(1)}, u32[]{:S(2)}, u32[]{:S(2)}) collective-permute-start(bf16[384,1536]{1,0:T(8,128)(2,1)} %get-tuple-element.146), channel_id=1, source_target_pairs={{0,8},{4,12},{8,0},{12,4},{16,24},{20,28},{24,16},{28,20},{1,9},{5... | collective-permute-start | bytes 3538952 | tf_op jit(solution)/shard_map/ppermute | solution.py:504
  145.1 94.3 %collective-permute-start.44 = (bf16[768,768]{1,0:T(8,128)(2,1)}, bf16[768,768]{1,0:T(8,128)(2,1)S(1)}, u32[]{:S(2)}, u32[]{:S(2)}) collective-permute-start(bf16[768,768]{1,0:T(8,128)(2,1)} %get-tuple-element.148), channel_id=1, source_target_pairs={{0,16},{4,20},{8,24},{12,28},{16,0},{20,4},{24,8},{28,12},{1,17},{... | collective-permute-start | bytes 3538952 | tf_op jit(solution)/shard_map/ppermute | solution.py:504
  155.1 91.6 %collective-permute-start.59 = (bf16[800,384]{1,0:T(8,128)(2,1)}, bf16[800,384]{1,0:T(8,128)(2,1)}, u32[]{:S(2)}, u32[]{:S(2)}) collective-permute-start(bf16[800,384]{1,0:T(8,128)(2,1)} %get-tuple-element.166), channel_id=1, source_target_pairs={{0,4},{4,0},{8,12},{12,8},{16,20},{20,16},{24,28},{28,24},{1,5},{5... | collective-permute-start | bytes 1843208 | tf_op jit(solution)/shard_map/ppermute | solution.py:504
  155.6 20.7 %collective-permute-start.31 = (bf16[256,192]{1,0:T(8,128)(2,1)}, bf16[256,192]{1,0:T(8,128)(2,1)S(1)}, u32[]{:S(2)}, u32[]{:S(2)}) collective-permute-start(bf16[256,192]{1,0:T(8,128)(2,1)} %get-tuple-element.126), channel_id=1, source_target_pairs={{0,8},{4,12},{8,0},{12,4},{16,24},{20,28},{24,16},{28,20},{1,9},{5... | collective-permute-start | bytes 294920 | tf_op jit(solution)/shard_map/ppermute | solution.py:504
  157.0 21.0 %collective-permute-start.32 = (bf16[256,192]{1,0:T(8,128)(2,1)}, bf16[256,192]{1,0:T(8,128)(2,1)S(1)}, u32[]{:S(2)}, u32[]{:S(2)}) collective-permute-start(bf16[256,192]{1,0:T(8,128)(2,1)} %get-tuple-element.127), channel_id=1, source_target_pairs={{0,12},{4,8},{8,4},{12,0},{16,28},{20,24},{24,20},{28,16},{1,13},{... | collective-permute-start | bytes 294920 | tf_op jit(solution)/shard_map/ppermute | solution.py:504
  197.8 18.3 %collective-permute-start.36 = (bf16[208,576]{1,0:T(8,128)(2,1)}, bf16[208,576]{1,0:T(8,128)(2,1)S(1)}, u32[]{:S(2)}, u32[]{:S(2)}) collective-permute-start(bf16[208,576]{1,0:T(8,128)(2,1)} %get-tuple-element.136), channel_id=1, source_target_pairs={{0,3},{1,0},{2,1},{3,2},{4,7},{5,4},{6,5},{7,6},{8,11},{9,8},{10,9... | collective-permute-start | bytes 718856 | tf_op jit(solution)/shard_map/ppermute | solution.py:508
  201.5 34.1 %collective-permute-start.37 = (bf16[208,576]{1,0:T(8,128)(2,1)}, bf16[208,576]{1,0:T(8,128)(2,1)S(1)}, u32[]{:S(2)}, u32[]{:S(2)}) collective-permute-start(bf16[208,576]{1,0:T(8,128)(2,1)} %get-tuple-element.137), channel_id=1, source_target_pairs={{0,2},{1,3},{2,0},{3,1},{4,6},{5,7},{6,4},{7,5},{8,10},{9,11},{10,... | collective-permute-start | bytes 718856 | tf_op jit(solution)/shard_map/ppermute | solution.py:508
  216.1 20.2 %collective-permute-start.38 = (bf16[208,576]{1,0:T(8,128)(2,1)}, bf16[208,576]{1,0:T(8,128)(2,1)}, u32[]{:S(2)}, u32[]{:S(2)}) collective-permute-start(bf16[208,576]{1,0:T(8,128)(2,1)} %get-tuple-element.138), channel_id=1, source_target_pairs={{0,1},{1,2},{2,3},{3,0},{4,5},{5,6},{6,7},{7,4},{8,9},{9,10},{10,1... | collective-permute-start | bytes 718856 | tf_op jit(solution)/shard_map/ppermute | solution.py:508
  236.3 40.1 %collective-permute-start.33 = (bf16[512,768]{1,0:T(8,128)(2,1)}, bf16[512,768]{1,0:T(8,128)(2,1)S(1)}, u32[]{:S(2)}, u32[]{:S(2)}) collective-permute-start(bf16[512,768]{1,0:T(8,128)(2,1)} %get-tuple-element.131), channel_id=1, source_target_pairs={{0,4},{4,0},{8,12},{12,8},{16,20},{20,16},{24,28},{28,24},{1,5},{5... | collective-permute-start | bytes 2359304 | tf_op jit(solution)/shard_map/ppermute | solution.py:504
  238.4 11.4 %collective-permute-start.39 = (bf16[208,576]{1,0:T(8,128)(2,1)}, bf16[208,576]{1,0:T(8,128)(2,1)S(1)}, u32[]{:S(2)}, u32[]{:S(2)}) collective-permute-start(bf16[208,576]{1,0:T(8,128)(2,1)} %shard_map.317.mine), channel_id=1, source_target_pairs={{0,16},{4,20},{8,24},{12,28},{16,0},{20,4},{24,8},{28,12},{1,17},{... | collective-permute-start | bytes 718856 | tf_op jit(solution)/shard_map/ppermute | solution.py:504
  244.9 13.7 %collective-permute-start.45 = (bf16[192,768]{1,0:T(8,128)(2,1)}, bf16[192,768]{1,0:T(8,128)(2,1)S(1)}, u32[]{:S(2)}, u32[]{:S(2)}) collective-permute-start(bf16[192,768]{1,0:T(8,128)(2,1)} %get-tuple-element.150), channel_id=1, source_target_pairs={{0,16},{4,20},{8,24},{12,28},{16,0},{20,4},{24,8},{28,12},{1,17},{... | collective-permute-start | bytes 884744 | tf_op jit(solution)/shard_map/ppermute | solution.py:504
  246.0 13.3 %collective-permute-start.46 = (bf16[384,384]{1,0:T(8,128)(2,1)}, bf16[384,384]{1,0:T(8,128)(2,1)S(1)}, u32[]{:S(2)}, u32[]{:S(2)}) collective-permute-start(bf16[384,384]{1,0:T(8,128)(2,1)} %get-tuple-element.152), channel_id=1, source_target_pairs={{0,8},{4,12},{8,0},{12,4},{16,24},{20,28},{24,16},{28,20},{1,9},{5... | collective-permute-start | bytes 884744 | tf_op jit(solution)/shard_map/ppermute | solution.py:504
  246.7 11.9 %collective-permute-start.27 = (bf16[128,768]{1,0:T(8,128)(2,1)}, bf16[128,768]{1,0:T(8,128)(2,1)}, u32[]{:S(2)}, u32[]{:S(2)}) collective-permute-start(bf16[128,768]{1,0:T(8,128)(2,1)} %get-tuple-element.113), channel_id=1, source_target_pairs={{0,16},{4,20},{8,24},{12,28},{16,0},{20,4},{24,8},{28,12},{1,17},{... | collective-permute-start | bytes 589832 | tf_op jit(solution)/shard_map/ppermute | solution.py:504
  249.8 24.0 %collective-permute-start.60 = (bf16[416,384]{1,0:T(8,128)(2,1)}, bf16[416,384]{1,0:T(8,128)(2,1)S(1)}, u32[]{:S(2)}, u32[]{:S(2)}) collective-permute-start(bf16[416,384]{1,0:T(8,128)(2,1)} %get-tuple-element.168), channel_id=1, source_target_pairs={{0,8},{4,12},{8,0},{12,4},{16,24},{20,28},{24,16},{28,20},{1,9},{5... | collective-permute-start | bytes 958472 | tf_op jit(solution)/shard_map/ppermute | solution.py:504
  258.5 9.5 %collective-permute-start.41 = (bf16[208,576]{1,0:T(8,128)(2,1)}, bf16[208,576]{1,0:T(8,128)(2,1)S(1)}, u32[]{:S(2)}, u32[]{:S(2)}) collective-permute-start(bf16[208,576]{1,0:T(8,128)(2,1)} %shard_map.318.s0), channel_id=1, source_target_pairs={{0,8},{4,12},{8,0},{12,4},{16,24},{20,28},{24,16},{28,20},{1,9},{5... | collective-permute-start | bytes 718856 | tf_op jit(solution)/shard_map/ppermute | solution.py:504
  259.3 13.5 %collective-permute-start.42 = (bf16[208,576]{1,0:T(8,128)(2,1)}, bf16[208,576]{1,0:T(8,128)(2,1)S(1)}, u32[]{:S(2)}, u32[]{:S(2)}) collective-permute-start(bf16[208,576]{1,0:T(8,128)(2,1)} %shard_map.318.s0), channel_id=1, source_target_pairs={{0,12},{4,8},{8,4},{12,0},{16,28},{20,24},{24,20},{28,16},{1,13},{... | collective-permute-start | bytes 718856 | tf_op jit(solution)/shard_map/ppermute | solution.py:504
  262.6 17.9 %collective-permute-start.47 = (bf16[96,768]{1,0:T(8,128)(2,1)}, bf16[96,768]{1,0:T(8,128)(2,1)S(1)}, u32[]{:S(2)}, u32[]{:S(2)}) collective-permute-start(bf16[96,768]{1,0:T(8,128)(2,1)} %get-tuple-element.154), channel_id=1, source_target_pairs={{0,3},{1,0},{2,1},{3,2},{4,7},{5,4},{6,5},{7,6},{8,11},{9,8},{10,9... | collective-permute-start | bytes 442376 | tf_op jit(solution)/shard_map/ppermute | solution.py:508
  268.1 13.8 %collective-permute-start.48 = (bf16[96,768]{1,0:T(8,128)(2,1)}, bf16[96,768]{1,0:T(8,128)(2,1)S(1)}, u32[]{:S(2)}, u32[]{:S(2)}) collective-permute-start(bf16[96,768]{1,0:T(8,128)(2,1)} %get-tuple-element.155), channel_id=1, source_target_pairs={{0,2},{1,3},{2,0},{3,1},{4,6},{5,7},{6,4},{7,5},{8,10},{9,11},{10,... | collective-permute-start | bytes 442376 | tf_op jit(solution)/shard_map/ppermute | solution.py:508
  272.8 20.0 %collective-permute-start.57 = (bf16[192,768]{1,0:T(8,128)(2,1)}, bf16[192,768]{1,0:T(8,128)(2,1)S(1)}, u32[]{:S(2)}, u32[]{:S(2)}) collective-permute-start(bf16[192,768]{1,0:T(8,128)(2,1)} %get-tuple-element.158), channel_id=1, source_target_pairs={{0,16},{4,20},{8,24},{12,28},{16,0},{20,4},{24,8},{28,12},{1,17},{... | collective-permute-start | bytes 884744 | tf_op jit(solution)/shard_map/ppermute | solution.py:504
  273.8 20.0 %collective-permute-start.58 = (bf16[384,384]{1,0:T(8,128)(2,1)}, bf16[384,384]{1,0:T(8,128)(2,1)S(1)}, u32[]{:S(2)}, u32[]{:S(2)}) collective-permute-start(bf16[384,384]{1,0:T(8,128)(2,1)} %get-tuple-element.160), channel_id=1, source_target_pairs={{0,8},{4,12},{8,0},{12,4},{16,24},{20,28},{24,16},{28,20},{1,9},{5... | collective-permute-start | bytes 884744 | tf_op jit(solution)/shard_map/ppermute | solution.py:504
  276.5 17.3 %collective-permute-start.61 = (bf16[224,384]{1,0:T(8,128)(2,1)}, bf16[224,384]{1,0:T(8,128)(2,1)S(1)}, u32[]{:S(2)}, u32[]{:S(2)}) collective-permute-start(bf16[224,384]{1,0:T(8,128)(2,1)} %get-tuple-element.170), channel_id=1, source_target_pairs={{0,16},{4,20},{8,24},{12,28},{16,0},{20,4},{24,8},{28,12},{1,17},{... | collective-permute-start | bytes 516104 | tf_op jit(solution)/shard_map/ppermute | solution.py:504
  280.5 21.2 %collective-permute-start.34 = (bf16[256,768]{1,0:T(8,128)(2,1)}, bf16[256,768]{1,0:T(8,128)(2,1)S(1)}, u32[]{:S(2)}, u32[]{:S(2)}) collective-permute-start(bf16[256,768]{1,0:T(8,128)(2,1)} %get-tuple-element.134), channel_id=1, source_target_pairs={{0,8},{4,12},{8,0},{12,4},{16,24},{20,28},{24,16},{28,20},{1,9},{5... | collective-permute-start | bytes 1179656 | tf_op jit(solution)/shard_map/ppermute | solution.py:504
  281.9 7.4 %collective-permute-start.49 = (bf16[96,768]{1,0:T(8,128)(2,1)}, bf16[96,768]{1,0:T(8,128)(2,1)S(1)}, u32[]{:S(2)}, u32[]{:S(2)}) collective-permute-start(bf16[96,768]{1,0:T(8,128)(2,1)} %get-tuple-element.156), channel_id=1, source_target_pairs={{0,1},{1,2},{2,3},{3,0},{4,5},{5,6},{6,7},{7,4},{8,9},{9,10},{10,1... | collective-permute-start | bytes 442376 | tf_op jit(solution)/shard_map/ppermute | solution.py:508
  291.8 9.3 %collective-permute-start.50 = (bf16[96,768]{1,0:T(8,128)(2,1)}, bf16[96,768]{1,0:T(8,128)(2,1)S(1)}, u32[]{:S(2)}, u32[]{:S(2)}) collective-permute-start(bf16[96,768]{1,0:T(8,128)(2,1)} %shard_map.323.refs_0_), channel_id=1, source_target_pairs={{0,8},{4,12},{8,0},{12,4},{16,24},{20,28},{24,16},{28,20},{1,9},{5... | collective-permute-start | bytes 442376 | tf_op jit(solution)/shard_map/ppermute | solution.py:504
  292.8 8.3 %collective-permute-start.51 = (bf16[96,768]{1,0:T(8,128)(2,1)}, bf16[96,768]{1,0:T(8,128)(2,1)}, u32[]{:S(2)}, u32[]{:S(2)}) collective-permute-start(bf16[96,768]{1,0:T(8,128)(2,1)} %shard_map.323.refs_0_), channel_id=1, source_target_pairs={{0,16},{4,20},{8,24},{12,28},{16,0},{20,4},{24,8},{28,12},{1,17},{... | collective-permute-start | bytes 442376 | tf_op jit(solution)/shard_map/ppermute | solution.py:504
  296.9 6.1 %collective-permute-start.62 = (bf16[144,768]{1,0:T(8,128)(2,1)}, bf16[144,768]{1,0:T(8,128)(2,1)S(1)}, u32[]{:S(2)}, u32[]{:S(2)}) collective-permute-start(bf16[144,768]{1,0:T(8,128)(2,1)} %get-tuple-element.172), channel_id=1, source_target_pairs={{0,3},{1,0},{2,1},{3,2},{4,7},{5,4},{6,5},{7,6},{8,11},{9,8},{10,9... | collective-permute-start | bytes 663560 | tf_op jit(solution)/shard_map/ppermute | solution.py:508
  299.4 23.4 %collective-permute-start.52 = (bf16[96,768]{1,0:T(8,128)(2,1)}, bf16[96,768]{1,0:T(8,128)(2,1)S(1)}, u32[]{:S(2)}, u32[]{:S(2)}) collective-permute-start(bf16[96,768]{1,0:T(8,128)(2,1)} %shard_map.323.refs_0_), channel_id=1, source_target_pairs={{0,24},{4,28},{8,16},{12,20},{16,8},{20,12},{24,0},{28,4},{1,25},{... | collective-permute-start | bytes 442376 | tf_op jit(solution)/shard_map/ppermute | solution.py:504
  301.2 22.4 %collective-permute-start.53 = (bf16[96,768]{1,0:T(8,128)(2,1)}, bf16[96,768]{1,0:T(8,128)(2,1)S(1)}, u32[]{:S(2)}, u32[]{:S(2)}) collective-permute-start(bf16[96,768]{1,0:T(8,128)(2,1)} %shard_map.323.refs_0_), channel_id=1, source_target_pairs={{0,4},{4,0},{8,12},{12,8},{16,20},{20,16},{24,28},{28,24},{1,5},{5... | collective-permute-start | bytes 442376 | tf_op jit(solution)/shard_map/ppermute | solution.py:504
  301.2 23.4 %collective-permute-start.54 = (bf16[96,768]{1,0:T(8,128)(2,1)S(1)}, bf16[96,768]{1,0:T(8,128)(2,1)}, u32[]{:S(2)}, u32[]{:S(2)}) collective-permute-start(bf16[96,768]{1,0:T(8,128)(2,1)S(1)} %collective-permute-done.50.refs_1_), channel_id=1, source_target_pairs={{0,4},{4,0},{8,12},{12,8},{16,20},{20,16},{24,28},{28,24},{1,5},{5... | collective-permute-start | bytes 442376 | tf_op jit(solution)/shard_map/ppermute | solution.py:504
  301.7 18.0 %collective-permute-start.63 = (bf16[144,768]{1,0:T(8,128)(2,1)}, bf16[144,768]{1,0:T(8,128)(2,1)S(1)}, u32[]{:S(2)}, u32[]{:S(2)}) collective-permute-start(bf16[144,768]{1,0:T(8,128)(2,1)} %get-tuple-element.173), channel_id=1, source_target_pairs={{0,2},{1,3},{2,0},{3,1},{4,6},{5,7},{6,4},{7,5},{8,10},{9,11},{10,... | collective-permute-start | bytes 663560 | tf_op jit(solution)/shard_map/ppermute | solution.py:508
  303.1 16.6 %collective-permute-start.64 = (bf16[144,768]{1,0:T(8,128)(2,1)}, bf16[144,768]{1,0:T(8,128)(2,1)S(1)}, u32[]{:S(2)}, u32[]{:S(2)}) collective-permute-start(bf16[144,768]{1,0:T(8,128)(2,1)} %get-tuple-element.174), channel_id=1, source_target_pairs={{0,1},{1,2},{2,3},{3,0},{4,5},{5,6},{6,7},{7,4},{8,9},{9,10},{10,1... | collective-permute-start | bytes 663560 | tf_op jit(solution)/shard_map/ppermute | solution.py:508
  319.7 6.7 %collective-permute-start.55 = (bf16[96,768]{1,0:T(8,128)(2,1)}, bf16[96,768]{1,0:T(8,128)(2,1)S(1)}, u32[]{:S(2)}, u32[]{:S(2)}) collective-permute-start(bf16[96,768]{1,0:T(8,128)(2,1)} %collective-permute-done.51.refs_2_), channel_id=1, source_target_pairs={{0,4},{4,0},{8,12},{12,8},{16,20},{20,16},{24,28},{28,24},{1,5},{5... | collective-permute-start | bytes 442376 | tf_op jit(solution)/shard_map/ppermute | solution.py:504
  319.7 7.8 %collective-permute-start.35 = (bf16[128,768]{1,0:T(8,128)(2,1)S(1)}, bf16[128,768]{1,0:T(8,128)(2,1)S(1)}, u32[]{:S(2)}, u32[]{:S(2)}) collective-permute-start(bf16[128,768]{1,0:T(8,128)(2,1)S(1)} %slice.120), channel_id=1, source_target_pairs={{0,16},{4,20},{8,24},{12,28},{16,0},{20,4},{24,8},{28,12},{1,17},{... | collective-permute-start | bytes 589832 | tf_op jit(solution)/shard_map/ppermute | solution.py:504
  322.8 8.6 %collective-permute-start.65 = (bf16[144,768]{1,0:T(8,128)(2,1)}, bf16[144,768]{1,0:T(8,128)(2,1)S(1)}, u32[]{:S(2)}, u32[]{:S(2)}) collective-permute-start(bf16[144,768]{1,0:T(8,128)(2,1)} %shard_map.328.refs_8_), channel_id=1, source_target_pairs={{0,8},{4,12},{8,0},{12,4},{16,24},{20,28},{24,16},{28,20},{1,9},{5... | collective-permute-start | bytes 663560 | tf_op jit(solution)/shard_map/ppermute | solution.py:504
  323.6 12.9 %collective-permute-start.66 = (bf16[144,768]{1,0:T(8,128)(2,1)}, bf16[144,768]{1,0:T(8,128)(2,1)S(1)}, u32[]{:S(2)}, u32[]{:S(2)}) collective-permute-start(bf16[144,768]{1,0:T(8,128)(2,1)} %shard_map.328.refs_8_), channel_id=1, source_target_pairs={{0,16},{4,20},{8,24},{12,28},{16,0},{20,4},{24,8},{28,12},{1,17},{... | collective-permute-start | bytes 663560 | tf_op jit(solution)/shard_map/ppermute | solution.py:504
  324.6 11.9 %collective-permute-start.67 = (bf16[144,768]{1,0:T(8,128)(2,1)}, bf16[144,768]{1,0:T(8,128)(2,1)S(1)}, u32[]{:S(2)}, u32[]{:S(2)}) collective-permute-start(bf16[144,768]{1,0:T(8,128)(2,1)} %shard_map.328.refs_8_), channel_id=1, source_target_pairs={{0,24},{4,28},{8,16},{12,20},{16,8},{20,12},{24,0},{28,4},{1,25},{... | collective-permute-start | bytes 663560 | tf_op jit(solution)/shard_map/ppermute | solution.py:504
  326.5 11.5 %collective-permute-start.56 = (bf16[96,768]{1,0:T(8,128)(2,1)S(1)}, bf16[96,768]{1,0:T(8,128)(2,1)S(1)}, u32[]{:S(2)}, u32[]{:S(2)}) collective-permute-start(bf16[96,768]{1,0:T(8,128)(2,1)S(1)} %collective-permute-done.52.refs_3_), channel_id=1, source_target_pairs={{0,4},{4,0},{8,12},{12,8},{16,20},{20,16},{24,28},{28,24},{1,5},{5... | collective-permute-start | bytes 442376 | tf_op jit(solution)/shard_map/ppermute | solution.py:504
  327.6 10.4 %collective-permute-start.68 = (bf16[144,768]{1,0:T(8,128)(2,1)}, bf16[144,768]{1,0:T(8,128)(2,1)S(1)}, u32[]{:S(2)}, u32[]{:S(2)}) collective-permute-start(bf16[144,768]{1,0:T(8,128)(2,1)} %shard_map.328.refs_8_), channel_id=1, source_target_pairs={{0,4},{4,0},{8,12},{12,8},{16,20},{20,16},{24,28},{28,24},{1,5},{5... | collective-permute-start | bytes 663560 | tf_op jit(solution)/shard_map/ppermute | solution.py:504
  331.4 6.6 %collective-permute-start.69 = (bf16[144,768]{1,0:T(8,128)(2,1)S(1)}, bf16[144,768]{1,0:T(8,128)(2,1)S(1)}, u32[]{:S(2)}, u32[]{:S(2)}) collective-permute-start(bf16[144,768]{1,0:T(8,128)(2,1)S(1)} %collective-permute-done.65.refs_9_), channel_id=1, source_target_pairs={{0,4},{4,0},{8,12},{12,8},{16,20},{20,16},{24,28},{28,24},{1,5},{5... | collective-permute-start | bytes 663560 | tf_op jit(solution)/shard_map/ppermute | solution.py:504
  (85 other events, 867.9 us)

commit v2 on v1

--- a/solution.py
+++ b/solution.py
@@ -632,7 +632,7 @@
 
 
 CHUNK = 128
-WINDOWS = (4, 6, 8)
+WINDOWS = (3, 5, 6, 8)
 
 
 def chunk_of(ctx, index):
@@ -660,7 +660,6 @@
 
 def attend_rows(qkv, seg_col, seg_row, far, outs, logsum, mixed):
     core, quarter, _, _ = where_am_i()
-    scale = HEAD_DIM ** (-0.5)
     group = qkv.shape[0] // 3
 
     def step(side, carry):
@@ -670,7 +669,7 @@
         def one_head(head, carry):
             mask = seg_col[rows, :] == seg_row[...]
             scores = dot_back(qkv[head, rows, :], qkv[group + head])
-            scores = jnp.where(mask, scores * scale, NEG)
+            scores = jnp.where(mask, scores, NEG)
             top = jnp.max(scores, axis=-1, keepdims=True)
             expd = jnp.exp(scores - top)
             total = jnp.sum(expd, axis=-1, keepdims=True)
@@ -696,14 +695,34 @@
 
 
 def attend_near_kernel(
-    mine, other, far, heads_own, g1, g2, g3, h1, h2, h3, bias, seg_col, seg_row,
-    qkv, m0, m1, logsum, weight, mixed,
+    mine, other, far, heads_own, g1, g2, g3, h1, h2, h3, vec, seg_col, seg_row,
+    qkv, m0, m1, logsum, weight, vectors, inner_b, mixed, bias,
 ):
-    _, quarter, _, own = where_am_i()
+    core, quarter, group, own = where_am_i()
     ctx = lax.axis_index("ctx")
     shard = heads_own.shape[0]
     part = shard // 2
     y = quarter >> 1
+    bias[:, shard : 2 * shard] = jnp.zeros_like(bias[:, :shard])
+    for index in range(4):
+
+        @pl.when(own == index)
+        def _():
+            for step, ref, at in ((0, vec, 0), (1, g1, part), (2, g2, part), (3, g3, part)):
+                row = (index + step) % 4
+                block = wide(ref[at : at + 16, 0:shard])
+                lane = row * shard
+                vectors[:, lane : lane + shard] = block[0:8]
+                lines = jnp.where(core == 0, block[8:10], block[10:12])
+                for side in range(2):
+                    lane = (2 * row + side) * shard
+                    inner_b[:, lane : lane + shard] = lines[side : side + 1]
+
+                @pl.when(group == row)
+                def _():
+                    bias[:, 0:shard] = block[0:1]
+                    bias[:, 2 * shard :] = block[1:2]
+
     weight[some_rows(own * shard, shard), :] = heads_own[...]
     for step, near_half, far_half in ((1, g1, h1), (2, g2, h2), (3, g3, h3)):
         at = ((own + step) & 3) * shard
@@ -716,10 +735,13 @@
             for half in range(2):
                 at = pl.multiple_of(chunk_of(ctx, index) * CHUNK, CHUNK)
                 for slot in range(qkv.shape[0]):
-                    qkv[slot, pl.ds(at, CHUNK), :] = low[
+                    value = low[
                         half * CHUNK : (half + 1) * CHUNK,
                         slot * HEAD_DIM : (slot + 1) * HEAD_DIM,
                     ]
+                    if slot < qkv.shape[0] // 3:
+                        value = value * jnp.asarray(HEAD_DIM ** (-0.5), BF)
+                    qkv[slot, pl.ds(at, CHUNK), :] = value
                 index += 1
     attend_rows(qkv, seg_col, seg_row, 0, (m0, m1), logsum, mixed)
 
@@ -1063,7 +1085,7 @@
                 sums = jnp.sum(
                     jnp.where(lane == head, logsum[rows, :], 0.0), axis=-1, keepdims=True
                 )
-                scores = jnp.where(mask, dot_back(query, keys) * scale, NEG)
+                scores = jnp.where(mask, dot_back(query, keys), NEG)
                 probs = jnp.exp(scores - sums)
                 dprobs = dot_back(grad, qkv[2 * group + head, window, :])
                 delta = jnp.sum(probs * dprobs, axis=-1, keepdims=True)
@@ -1082,7 +1104,7 @@
     for head in range(group):
         whole[:, head * HEAD_DIM : (head + 1) * HEAD_DIM] = dqueries[head]
         at = width + head * HEAD_DIM
-        whole[:, at : at + HEAD_DIM] = short(dkeys[head] * scale)
+        whole[:, at : at + HEAD_DIM] = short(dkeys[head])
         whole[:, at + width : at + width + HEAD_DIM] = short(dvalues[head])
     for index in range(8):
         grads[index * CHUNK : (index + 1) * CHUNK, :] = whole[
@@ -1155,7 +1177,7 @@
     cotangent,
 ):
     ctx, own = lax.axis_index("ctx"), lax.axis_index("wt")
-    core, y, group = ctx & 1, ctx >> 2, ctx & 3
+    y = ctx >> 2
     rows, dim = tokens.shape[2], tokens.shape[3]
     shard = query_weight.shape[0]
     hidden = outer_weight.shape[0]
@@ -1198,14 +1220,6 @@
         piece = turn(w2_send, step)
         pieces += [piece] + [flip(piece, bits) for bits in (2, 4, 6)]
 
-    at = shard // 2
-    rel = jnp.stack([vec] + [value[at:, :shard] for value in got])
-    vectors = wide(lax.dynamic_slice_in_dim(jnp.concatenate([rel, rel]), (4 - own) % 4, 4))
-    mine_b = pick(vectors, group)
-    heads_bias = jnp.concatenate([mine_b[0], jnp.zeros_like(mine_b[0]), mine_b[1]])[None]
-    inner_b = pick(vectors[:, 8:12].reshape(4, 2, half), core, 1).reshape(1, 4 * half)
-    vectors = jnp.swapaxes(vectors[:, :8], 0, 1).reshape(8, dim)
-
     lengths = pick(doc_lengths[:, 0], y)
     starts = jnp.cumsum(lengths) - lengths
     total = 8 * rows
@@ -1217,7 +1231,7 @@
     ends = jnp.where(starts[None, :] >= first + 2 * CHUNK, starts[None, :], total)
     bounds = jnp.stack([low, (jnp.min(ends, axis=-1) - 1) // CHUNK - low + 1])
 
-    qkv, m0, m1, logsum0, heads_weight = run(
+    qkv, m0, m1, logsum0, heads_weight, vectors, inner_b = run(
         attend_near_kernel,
         [
             ((9, total, HEAD_DIM), BF),
@@ -1225,9 +1239,11 @@
             ((count, shard), BF),
             ((2 * count, 128), F32),
             ((dim, 3 * shard), BF),
+            ((8, dim), F32),
+            ((1, 4 * half), F32),
         ],
-        (mine, other, far, heads_own, *got, *gone, heads_bias, *segs),
-        [pltpu.VMEM((3, 2 * count, HEAD_DIM), BF)],
+        (mine, other, far, heads_own, *got, *gone, vec, *segs),
+        [pltpu.VMEM((3, 2 * count, HEAD_DIM), BF), pltpu.VMEM((1, 3 * shard), F32)],
     )
     m2, m3, logsum1 = run(
         attend_far_kernel,

time: 348 us -> 354 us (1.017)
  starting transfers between devices: 77.5 us -> 84.5 us
    ppermute x15, starting transfers between devices: 28.2 us -> 38.3 us  [turn(): return lax.ppermute(value, 'wt', [(i, (i - step) % 4) for i in range(4)])]
    ppermute x57, waiting for transfers between devices: 77.1 us -> 84.5 us  [flip(): return lax.ppermute(value, 'ctx', [(i, i ^ bits) for i in range(8)])]
    ppermute x15, waiting for transfers between devices: 45.6 us -> 40.6 us  [turn(): return lax.ppermute(value, 'wt', [(i, (i - step) % 4) for i in range(4)])]
    unnamed x159 -> x150, local copies, waits for them, and re-layouts: 11.8 us -> 11.3 us
  transfers between devices with their start and end apart: 72 -> 72, of which waited for: 27 -> 28; matrix products, arithmetic and copies ran while one was open for 3% -> 3% of each run, Pallas kernels for 25% -> 25%
where the time goes in v2:
time: 354 us; the launch traced here: 353 us
  waiting for transfers between devices  125 us (35%)
  Pallas kernels  117 us (33%)
  starting transfers between devices  84.5 us (24%)
  local copies, waits for them, and re-layouts  19.2 us (5%)
  other arithmetic  5.59 us (2%)
    pallas_call x25, Pallas kernels, run(): pl.pallas_call(kernel, out_shape=shapes, in_specs=in_specs, out_specs=tup...  117 us
    ppermute x57, waiting for transfers between devices, flip(): return lax.ppermute(value, 'ctx', [(i, i ^ bits) for i in range(8)])  84.5 us
    ppermute x57, starting transfers between devices, flip(): return lax.ppermute(value, 'ctx', [(i, i ^ bits) for i in range(8)])  46.2 us
    ppermute x15, waiting for transfers between devices, turn(): return lax.ppermute(value, 'wt', [(i, (i - step) % 4) for i in range(4)])  40.6 us
    ppermute x15, starting transfers between devices, turn(): return lax.ppermute(value, 'wt', [(i, (i - step) % 4) for i in range(4)])  38.3 us
    unnamed x150, local copies, waits for them, and re-layouts  11.3 us
  transfers between devices with their start and end apart: 72, of which 28 were waited for; matrix products, arithmetic and copies ran while one was open for 3% of the time, Pallas kernels for 25%

profile of v2, /device:TPU:0, one launch (start us, length us, event | category | flops | bytes accessed | tf_op | source)
XLA Modules:
  0.0 352.8 jit_solution(4994037530768327675)
XLA Ops:
  1.8 3.1 collective-permute-start
  5.9 3.9 %collective-permute-done = bf16[128,768]{1,0:T(8,128)(2,1)S(1)} collective-permute-done((bf16[128,768]{1,0:T(8,128)(2,1)S(1)}, bf16[128,768]{1,0:T(8,128)(2,1)S(1)}, u32[]{:S(2)}, u32[]{:S(2)}) %collective-permute-start) | collective-permute-done | bytes 196640 | tf_op jit(solution)/shard_map/ppermute | solution.py:504
  9.8 1.8 collective-permute-start.1
  12.4 2.0 shard_map.305
  14.4 3.6 %collective-permute-start.3 = (bf16[112,576]{1,0:T(8,128)(2,1)}, bf16[112,576]{1,0:T(8,128)(2,1)S(1)}, u32[]{:S(2)}, u32[]{:S(2)}) collective-permute-start(bf16[112,576]{1,0:T(8,128)(2,1)} %get-tuple-element.101), channel_id=1, source_target_pairs={{0,3},{1,0},{2,1},{3,2},{4,7},{5,4},{6,5},{7,6},{8,11},{9,8},{10,9... | collective-permute-start | bytes 387080 | tf_op jit(solution)/shard_map/ppermute | solution.py:508
  18.0 3.0 shard_map.308
  21.7 2.2 collective-permute-start.16
  24.0 2.0 collective-permute-start.5
  26.0 2.0 collective-permute-done.4.g2
  28.0 1.5 collective-permute-start.6
  30.9 12.3 %collective-permute-done.5.g3 = bf16[112,576]{1,0:T(8,128)(2,1)S(1)} collective-permute-done((bf16[112,576]{1,0:T(8,128)(2,1)S(1)}, bf16[112,576]{1,0:T(8,128)(2,1)S(1)}, u32[]{:S(2)}, u32[]{:S(2)}) %collective-permute-start.5) | collective-permute-done | bytes 129056 | tf_op jit(solution)/shard_map/ppermute | solution.py:508
  43.3 10.5 %collective-permute-start.20 = (bf16[240,768]{1,0:T(8,128)(2,1)S(1)}, bf16[240,768]{1,0:T(8,128)(2,1)S(1)}, u32[]{:S(2)}, u32[]{:S(2)}) collective-permute-start(bf16[240,768]{1,0:T(8,128)(2,1)S(1)} %copy-done.72), channel_id=1, source_target_pairs={{0,1},{1,2},{2,3},{3,0},{4,5},{5,6},{6,7},{7,4},{8,9},{9,10},{10,1... | collective-permute-start | bytes 1105928 | tf_op jit(solution)/shard_map/ppermute | solution.py:508
  53.8 1.5 collective-permute-start.8
  56.0 3.8 %collective-permute-done.8.h3 = bf16[112,576]{1,0:T(8,128)(2,1)} collective-permute-done((bf16[112,576]{1,0:T(8,128)(2,1)S(1)}, bf16[112,576]{1,0:T(8,128)(2,1)}, u32[]{:S(2)}, u32[]{:S(2)}) %collective-permute-start.8) | collective-permute-done | bytes 129056 | tf_op jit(solution)/shard_map/ppermute | solution.py:504
  59.8 1.5 collective-permute-start.14
  63.0 1.5 collective-permute-start.17
  64.8 2.1 collective-permute-done.13.refs_1_
  67.4 11.8 %collective-permute-done.14.refs_2_ = bf16[240,768]{1,0:T(8,128)(2,1)S(1)} collective-permute-done((bf16[240,768]{1,0:T(8,128)(2,1)S(1)}, bf16[240,768]{1,0:T(8,128)(2,1)S(1)}, u32[]{:S(2)}, u32[]{:S(2)}) %collective-permute-start.14) | collective-permute-done | bytes 368672 | tf_op jit(solution)/shard_map/ppermute | solution.py:504
  79.2 1.5 collective-permute-start.19
  80.7 1.5 collective-permute-start.21
  83.4 1.5 collective-permute-start.23
  86.0 10.8 %shard_map.306 = (bf16[9,1024,64]{2,1,0:T(8,128)(2,1)}, bf16[256,192]{1,0:T(8,128)(2,1)}, bf16[256,192]{1,0:T(8,128)(2,1)}, f32[512,128]{1,0:T(8,128)}, bf16[768...) custom-call(bf16[256,768]{1,0:T(8,128)(2,1)} %copy-done, bf16[256,768]{1,0:T(8,128)(2,1)} %copy-done.1, ...), custom_call_target="tpu_custom_call" | custom-call | tf_op jit(solution)/shard_map/pallas_call | solution.py:569
  96.8 7.8 %shard_map.307 = (bf16[256,192]{1,0:T(8,128)(2,1)}, bf16[256,192]{1,0:T(8,128)(2,1)}, f32[512,128]{1,0:T(8,128)}) custom-call(bf16[9,1024,64]{2,1,0:T(8,128)(2,1)} %get-tuple-element.104.qkv, s32[1024,1]{1,0:T(8,128)} %copy.41.seg_col, s32[1,1024]{1,0:T(1,128)} %bitcast.52), custom_call_target="tpu_custom_call" | custom-call | tf_op jit(solution)/shard_map/pallas_call | solution.py:569
  106.7 2.5 collective-permute-done.22.refs_10_
  110.3 1.8 collective-permute-done.11.m3
  112.8 4.7 %shard_map.309 = (f32[256,768]{1,0:T(8,128)}, bf16[256,768]{1,0:T(8,128)(2,1)}, bf16[768,768]{1,0:T(8,128)(2,1)}) custom-call(bf16[256,192]{1,0:T(8,128)(2,1)} %get-tuple-element.102.m0, bf16[256,192]{1,0:T(8,128)(2,1)} %copy-done.19, bf16[256,192]{1,0:T(8,128)(2,1)} %copy-done.17, bf16[256,192]{1,0:T(8,128)(2,1)} %copy-done.18, bf16[256,768]{1,0:T(8,128)(2,1)} %copy-done, ...), custom_call_target="tpu_custom_call" | custom-call | tf_op jit(solution)/shard_map/pallas_call | solution.py:569
  117.9 1.6 collective-permute-done.24.far.first1
  120.3 9.1 %shard_map.310 = (f32[256,768]{1,0:T(8,128)}, f32[256,768]{1,0:T(8,128)}, bf16[512,1536]{1,0:T(8,128)(2,1)}, bf16[512,1536]{1,0:T(8,128)(2,1)}, bf16[768,1536]{1,0:T(8,128)(2,1)}, /*index=5*/bf16[1536,768]{1,0:T(8,128)(2,1)}) custom-call(bf16[256,768]{1,0:T(8,128)(2,1)} %get-tuple-element.110.near.first0, bf16[256,768]{1,0:T(8,128)(2,1)} %copy-done.3, ...), custom_call_target="tpu_custom_call" | custom-call | tf_op jit(solution)/shard_map/pallas_call | solution.py:569
  131.0 6.5 %collective-permute-done.26.cot1 = bf16[128,768]{1,0:T(8,128)(2,1)S(1)} collective-permute-done((bf16[128,768]{1,0:T(8,128)(2,1)S(1)}, bf16[128,768]{1,0:T(8,128)(2,1)S(1)}, u32[]{:S(2)}, u32[]{:S(2)}) %collective-permute-start.26) | collective-permute-done | bytes 196640 | tf_op jit(solution)/shard_map/ppermute | solution.py:504
  138.5 3.7 %shard_map.311 = (bf16[128,768]{1,0:T(8,128)(2,1)}, bf16[128,768]{1,0:T(8,128)(2,1)}, f32[256,768]{1,0:T(8,128)}, bf16[256,768]{1,0:T(8,128)(2,1)}, f32[8,768]{1,0:T(8,128)}) custom-call(f32[256,768]{1,0:T(8,128)} %get-tuple-element.109.first_sum, f32[256,768]{1,0:T(8,128)} %get-tuple-element.114.keep, f32[256,768]{1,0:T(8,128)} %copy-done.15, ...), custom_call_target="tpu_custom_call" | custom-call | tf_op jit(solution)/shard_map/pallas_call | solution.py:569
  142.2 1.9 collective-permute-done.28.far.douter1
  144.9 8.1 %shard_map.312 = (f32[256,768]{1,0:T(8,128)}, f32[256,768]{1,0:T(8,128)}, bf16[512,1536]{1,0:T(8,128)(2,1)}, f32[8,768]{1,0:T(8,128)}) custom-call(bf16[256,768]{1,0:T(8,128)(2,1)} %get-tuple-element.121.near.douter0, bf16[256,768]{1,0:T(8,128)(2,1)} %copy-done.4, bf16[512,1536]{1,0:T(8,128)(2,1)} %get-tuple-element.122.slope, ...), custom_call_target="tpu_custom_call" | custom-call | tf_op jit(solution)/shard_map/pallas_call | solution.py:569
  153.2 7.3 %shard_map.320 = (bf16[384,1536]{1,0:T(8,128)(2,1)}, bf16[384,1536]{1,0:T(8,128)(2,1)}, bf16[768,768]{1,0:T(8,128)(2,1)}, bf16[768,768]{1,0:T(8,128)(2,1)}) custom-call(bf16[256,768]{1,0:T(8,128)(2,1)} %get-tuple-element.110.near.first0, bf16[256,768]{1,0:T(8,128)(2,1)} %copy-done.3, bf16[256,768]{1,0:T(8,128)(2,1)} %get-tuple-element.121.near.douter0, ...), custom_call_target="tpu_custom_call" | custom-call | tf_op jit(solution)/shard_map/pallas_call | solution.py:569
  163.5 4.4 %shard_map.313 = (f32[256,768]{1,0:T(8,128)}, bf16[256,768]{1,0:T(8,128)(2,1)}, bf16[256,192]{1,0:T(8,128)(2,1)}, bf16[256,192]{1,0:T(8,128)(2,1)}, bf16[256,192...) custom-call(f32[256,768]{1,0:T(8,128)} %get-tuple-element.109.first_sum, ...), custom_call_target="tpu_custom_call" | custom-call | tf_op jit(solution)/shard_map/pallas_call | solution.py:569
  167.9 3.0 shard_map.324
  173.3 19.1 %collective-permute-done.31.p2 = bf16[256,192]{1,0:T(8,128)(2,1)S(1)} collective-permute-done((bf16[256,192]{1,0:T(8,128)(2,1)}, bf16[256,192]{1,0:T(8,128)(2,1)S(1)}, u32[]{:S(2)}, u32[]{:S(2)}) %collective-permute-start.31) | collective-permute-done | bytes 98336 | tf_op jit(solution)/shard_map/ppermute | solution.py:504
  192.4 1.6 collective-permute-done.32.p3
  194.6 17.8 %shard_map.314 = (f32[208,576]{1,0:T(8,128)}, bf16[208,576]{1,0:T(8,128)(2,1)}, bf16[208,576]{1,0:T(8,128)(2,1)}, bf16[208,576]{1,0:T(8,128)(2,1)}, bf16[1024,576]{1,0:T(8,128)(2,1)}) custom-call(s32[2,4]{1,0:T(2,128)} %pad_add_fusion.bounds, bf16[9,1024,64]{2,1,0:T(8,128)(2,1)} %get-tuple-element.104.qkv, f32[512,128]{1,0:T(8,128)} %get-tuple-element.118.logsum0, ...), custom_call_target="tpu_custom_call" | custom-call | tf_op jit(solution)/shard_map/pallas_call | solution.py:569
  212.5 4.2 %collective-permute-start.37 = (bf16[208,576]{1,0:T(8,128)(2,1)}, bf16[208,576]{1,0:T(8,128)(2,1)S(1)}, u32[]{:S(2)}, u32[]{:S(2)}) collective-permute-start(bf16[208,576]{1,0:T(8,128)(2,1)} %get-tuple-element.141), channel_id=1, source_target_pairs={{0,2},{1,3},{2,0},{3,1},{4,6},{5,7},{6,4},{7,5},{8,10},{9,11},{10,... | collective-permute-start | bytes 718856 | tf_op jit(solution)/shard_map/ppermute | solution.py:508
  216.7 5.7 %collective-permute-done.36.refs_0_ = bf16[208,576]{1,0:T(8,128)(2,1)S(1)} collective-permute-done((bf16[208,576]{1,0:T(8,128)(2,1)}, bf16[208,576]{1,0:T(8,128)(2,1)S(1)}, u32[]{:S(2)}, u32[]{:S(2)}) %collective-permute-start.36) | collective-permute-done | bytes 239648 | tf_op jit(solution)/shard_map/ppermute | solution.py:508
  222.4 13.7 %collective-permute-start.38 = (bf16[208,576]{1,0:T(8,128)(2,1)}, bf16[208,576]{1,0:T(8,128)(2,1)}, u32[]{:S(2)}, u32[]{:S(2)}) collective-permute-start(bf16[208,576]{1,0:T(8,128)(2,1)} %get-tuple-element.142), channel_id=1, source_target_pairs={{0,1},{1,2},{2,3},{3,0},{4,5},{5,6},{6,7},{7,4},{8,9},{9,10},{10,1... | collective-permute-start | bytes 718856 | tf_op jit(solution)/shard_map/ppermute | solution.py:508
  236.1 4.0 %shard_map.315 = (f32[512,768]{1,0:T(8,128)}, bf16[512,768]{1,0:T(8,128)(2,1)}) custom-call(bf16[1024,576]{1,0:T(8,128)(2,1)} %get-tuple-element.132.grads, bf16[768,576]{1,0:T(8,128)(2,1)} %get-tuple-element.133.weight), custom_call_target="tpu_custom_call" | custom-call | tf_op jit(solution)/shard_map/pallas_call | solution.py:569
  241.4 2.1 shard_map.317.mine
  245.4 4.1 %shard_map.321 = (bf16[192,768]{1,0:T(8,128)(2,1)}, bf16[192,768]{1,0:T(8,128)(2,1)}, bf16[384,384]{1,0:T(8,128)(2,1)}, bf16[384,384]{1,0:T(8,128)(2,1)}, bf16[1...) custom-call(bf16[384,1536]{1,0:T(8,128)(2,1)} %get-tuple-element.149.ak, ...), custom_call_target="tpu_custom_call" | custom-call | tf_op jit(solution)/shard_map/pallas_call | solution.py:569
  249.5 1.5 collective-permute-start.45
  252.9 2.2 shard_map.325
  255.9 1.8 shard_map.318.s0
  257.7 5.5 %collective-permute-done.27 = bf16[128,768]{1,0:T(8,128)(2,1)} collective-permute-done((bf16[128,768]{1,0:T(8,128)(2,1)}, bf16[128,768]{1,0:T(8,128)(2,1)}, u32[]{:S(2)}, u32[]{:S(2)}) %collective-permute-start.27) | collective-permute-done | bytes 196640 | tf_op jit(solution)/shard_map/ppermute | solution.py:504
  265.4 2.2 shard_map.322
  267.6 5.5 %collective-permute-done.41.s2 = bf16[208,576]{1,0:T(8,128)(2,1)S(1)} collective-permute-done((bf16[208,576]{1,0:T(8,128)(2,1)}, bf16[208,576]{1,0:T(8,128)(2,1)S(1)}, u32[]{:S(2)}, u32[]{:S(2)}) %collective-permute-start.41) | collective-permute-done | bytes 239648 | tf_op jit(solution)/shard_map/ppermute | solution.py:504
  273.1 4.8 %collective-permute-done.42.s3 = bf16[208,576]{1,0:T(8,128)(2,1)S(1)} collective-permute-done((bf16[208,576]{1,0:T(8,128)(2,1)}, bf16[208,576]{1,0:T(8,128)(2,1)S(1)}, u32[]{:S(2)}, u32[]{:S(2)}) %collective-permute-start.42) | collective-permute-done | bytes 239648 | tf_op jit(solution)/shard_map/ppermute | solution.py:504
  280.3 1.9 shard_map.326
  283.3 3.0 shard_map.316
  288.3 1.8 maximum_select_fusion.1
  290.2 3.2 shard_map.319
  293.3 1.8 collective-permute-done.49.refs_2_
  295.8 1.9 shard_map.323.refs_0_
  300.6 2.4 shard_map.327
  307.4 1.7 collective-permute-done.62.refs_0_
  309.2 16.2 %collective-permute-done.63.refs_1_ = bf16[144,768]{1,0:T(8,128)(2,1)S(1)} collective-permute-done((bf16[144,768]{1,0:T(8,128)(2,1)}, bf16[144,768]{1,0:T(8,128)(2,1)S(1)}, u32[]{:S(2)}, u32[]{:S(2)}) %collective-permute-start.63) | collective-permute-done | bytes 221216 | tf_op jit(solution)/shard_map/ppermute | solution.py:508
  326.5 2.0 shard_map.328.refs_8_
  333.1 4.0 %collective-permute-done.65.refs_9_ = bf16[144,768]{1,0:T(8,128)(2,1)S(1)} collective-permute-done((bf16[144,768]{1,0:T(8,128)(2,1)}, bf16[144,768]{1,0:T(8,128)(2,1)S(1)}, u32[]{:S(2)}, u32[]{:S(2)}) %collective-permute-start.65) | collective-permute-done | bytes 221216 | tf_op jit(solution)/shard_map/ppermute | solution.py:504
  337.2 5.1 %collective-permute-done.66.refs_10_ = bf16[144,768]{1,0:T(8,128)(2,1)S(1)} collective-permute-done((bf16[144,768]{1,0:T(8,128)(2,1)}, bf16[144,768]{1,0:T(8,128)(2,1)S(1)}, u32[]{:S(2)}, u32[]{:S(2)}) %collective-permute-start.66) | collective-permute-done | bytes 221216 | tf_op jit(solution)/shard_map/ppermute | solution.py:504
  345.3 4.6 %shard_map.329 = (f32[192,3072]{1,0:T(8,128)}, f32[768,768]{1,0:T(8,128)}, f32[192,768]{1,0:T(8,128)}, f32[16,768]{1,0:T(8,128)}) custom-call(bf16[96,768]{1,0:T(8,128)(2,1)} %shard_map.323.refs_0_, bf16[96,768]{1,0:T(8,128)(2,1)} %copy-done.44, bf16[96,768]{1,0:T(8,128)(2,1)} %copy-done.45, bf16[96,768]{1,0:T(8,128)(2,1)} %copy-done.46, ...), custom_call_target="tpu_custom_call" | custom-call | tf_op jit(solution)/shard_map/pallas_call | solution.py:569
  (292 shorter events, 58.1 us)
Async XLA Ops:
  1.8 8.0 %collective-permute-start = (bf16[128,768]{1,0:T(8,128)(2,1)S(1)}, bf16[128,768]{1,0:T(8,128)(2,1)S(1)}, u32[]{:S(2)}, u32[]{:S(2)}) collective-permute-start(bf16[128,768]{1,0:T(8,128)(2,1)S(1)} %get-tuple-element.188), channel_id=1, source_target_pairs={{0,16},{4,20},{8,24},{12,28},{16,0},{20,4},{24,8},{28,12},{1,17},{... | collective-permute-start | bytes 589832 | tf_op jit(solution)/shard_map/ppermute | solution.py:504
  9.8 19.7 %collective-permute-start.1 = (bf16[256,768]{1,0:T(8,128)(2,1)S(1)}, bf16[256,768]{1,0:T(8,128)(2,1)S(1)}, u32[]{:S(2)}, u32[]{:S(2)}) collective-permute-start(bf16[256,768]{1,0:T(8,128)(2,1)S(1)} %pad_maximum_fusion.1.mine), channel_id=1, source_target_pairs={{0,8},{4,12},{8,0},{12,4},{16,24},{20,28},{24,16},{28,20},{1,9},{5... | collective-permute-start | bytes 1179656 | tf_op jit(solution)/shard_map/ppermute | solution.py:504
  14.4 9.6 %collective-permute-start.3 = (bf16[112,576]{1,0:T(8,128)(2,1)}, bf16[112,576]{1,0:T(8,128)(2,1)S(1)}, u32[]{:S(2)}, u32[]{:S(2)}) collective-permute-start(bf16[112,576]{1,0:T(8,128)(2,1)} %get-tuple-element.101), channel_id=1, source_target_pairs={{0,3},{1,0},{2,1},{3,2},{4,7},{5,4},{6,5},{7,6},{8,11},{9,8},{10,9... | collective-permute-start | bytes 387080 | tf_op jit(solution)/shard_map/ppermute | solution.py:508
  18.0 10.0 %collective-permute-start.4 = (bf16[112,576]{1,0:T(8,128)(2,1)}, bf16[112,576]{1,0:T(8,128)(2,1)S(1)}, u32[]{:S(2)}, u32[]{:S(2)}) collective-permute-start(bf16[112,576]{1,0:T(8,128)(2,1)} %get-tuple-element.101), channel_id=1, source_target_pairs={{0,2},{1,3},{2,0},{3,1},{4,6},{5,7},{6,4},{7,5},{8,10},{9,11},{10,... | collective-permute-start | bytes 387080 | tf_op jit(solution)/shard_map/ppermute | solution.py:508
  21.0 34.4 %collective-permute-start.12 = (bf16[240,768]{1,0:T(8,128)(2,1)}, bf16[240,768]{1,0:T(8,128)(2,1)S(1)}, u32[]{:S(2)}, u32[]{:S(2)}) collective-permute-start(bf16[240,768]{1,0:T(8,128)(2,1)} %get-tuple-element.108), channel_id=1, source_target_pairs={{0,3},{1,0},{2,1},{3,2},{4,7},{5,4},{6,5},{7,6},{8,11},{9,8},{10,9... | collective-permute-start | bytes 1105928 | tf_op jit(solution)/shard_map/ppermute | solution.py:508
  21.7 39.8 %collective-permute-start.16 = (bf16[240,768]{1,0:T(8,128)(2,1)}, bf16[240,768]{1,0:T(8,128)(2,1)S(1)}, u32[]{:S(2)}, u32[]{:S(2)}) collective-permute-start(bf16[240,768]{1,0:T(8,128)(2,1)} %get-tuple-element.108), channel_id=1, source_target_pairs={{0,2},{1,3},{2,0},{3,1},{4,6},{5,7},{6,4},{7,5},{8,10},{9,11},{10,... | collective-permute-start | bytes 1105928 | tf_op jit(solution)/shard_map/ppermute | solution.py:508
  24.0 19.3 %collective-permute-start.5 = (bf16[112,576]{1,0:T(8,128)(2,1)S(1)}, bf16[112,576]{1,0:T(8,128)(2,1)S(1)}, u32[]{:S(2)}, u32[]{:S(2)}) collective-permute-start(bf16[112,576]{1,0:T(8,128)(2,1)S(1)} %copy-done.73), channel_id=1, source_target_pairs={{0,1},{1,2},{2,3},{3,0},{4,5},{5,6},{6,7},{7,4},{8,9},{9,10},{10,1... | collective-permute-start | bytes 387080 | tf_op jit(solution)/shard_map/ppermute | solution.py:508
  28.0 15.3 %collective-permute-start.6 = (bf16[112,576]{1,0:T(8,128)(2,1)S(1)}, bf16[112,576]{1,0:T(8,128)(2,1)S(1)}, u32[]{:S(2)}, u32[]{:S(2)}) collective-permute-start(bf16[112,576]{1,0:T(8,128)(2,1)S(1)} %collective-permute-done.3.g1), channel_id=1, source_target_pairs={{0,16},{4,20},{8,24},{12,28},{16,0},{20,4},{24,8},{28,12},{1,17},{... | collective-permute-start | bytes 387080 | tf_op jit(solution)/shard_map/ppermute | solution.py:504
  29.5 24.3 %collective-permute-start.7 = (bf16[112,576]{1,0:T(8,128)(2,1)S(1)}, bf16[112,576]{1,0:T(8,128)(2,1)S(1)}, u32[]{:S(2)}, u32[]{:S(2)}) collective-permute-start(bf16[112,576]{1,0:T(8,128)(2,1)S(1)} %collective-permute-done.4.g2), channel_id=1, source_target_pairs={{0,16},{4,20},{8,24},{12,28},{16,0},{20,4},{24,8},{28,12},{1,17},{... | collective-permute-start | bytes 387080 | tf_op jit(solution)/shard_map/ppermute | solution.py:504
  43.2 40.1 %collective-permute-start.2 = (bf16[512,768]{1,0:T(8,128)(2,1)}, bf16[512,768]{1,0:T(8,128)(2,1)S(1)}, u32[]{:S(2)}, u32[]{:S(2)}) collective-permute-start(bf16[512,768]{1,0:T(8,128)(2,1)} %pad_maximum_fusion), channel_id=1, source_target_pairs={{0,4},{4,0},{8,12},{12,8},{16,20},{20,16},{24,28},{28,24},{1,5},{5... | collective-permute-start | bytes 2359304 | tf_op jit(solution)/shard_map/ppermute | solution.py:504
  43.3 19.7 %collective-permute-start.20 = (bf16[240,768]{1,0:T(8,128)(2,1)S(1)}, bf16[240,768]{1,0:T(8,128)(2,1)S(1)}, u32[]{:S(2)}, u32[]{:S(2)}) collective-permute-start(bf16[240,768]{1,0:T(8,128)(2,1)S(1)} %copy-done.72), channel_id=1, source_target_pairs={{0,1},{1,2},{2,3},{3,0},{4,5},{5,6},{6,7},{7,4},{8,9},{9,10},{10,1... | collective-permute-start | bytes 1105928 | tf_op jit(solution)/shard_map/ppermute | solution.py:508
  55.4 11.5 %collective-permute-start.13 = (bf16[240,768]{1,0:T(8,128)(2,1)S(1)}, bf16[240,768]{1,0:T(8,128)(2,1)S(1)}, u32[]{:S(2)}, u32[]{:S(2)}) collective-permute-start(bf16[240,768]{1,0:T(8,128)(2,1)S(1)} %collective-permute-done.12.refs_0_), channel_id=1, source_target_pairs={{0,8},{4,12},{8,0},{12,4},{16,24},{20,28},{24,16},{28,20},{1,9},{5... | collective-permute-start | bytes 1105928 | tf_op jit(solution)/shard_map/ppermute | solution.py:504
  59.8 19.4 %collective-permute-start.14 = (bf16[240,768]{1,0:T(8,128)(2,1)S(1)}, bf16[240,768]{1,0:T(8,128)(2,1)S(1)}, u32[]{:S(2)}, u32[]{:S(2)}) collective-permute-start(bf16[240,768]{1,0:T(8,128)(2,1)S(1)} %collective-permute-done.12.refs_0_), channel_id=1, source_target_pairs={{0,16},{4,20},{8,24},{12,28},{16,0},{20,4},{24,8},{28,12},{1,17},{... | collective-permute-start | bytes 1105928 | tf_op jit(solution)/shard_map/ppermute | solution.py:504
  61.5 19.1 %collective-permute-start.15 = (bf16[240,768]{1,0:T(8,128)(2,1)S(1)}, bf16[240,768]{1,0:T(8,128)(2,1)S(1)}, u32[]{:S(2)}, u32[]{:S(2)}) collective-permute-start(bf16[240,768]{1,0:T(8,128)(2,1)S(1)} %collective-permute-done.12.refs_0_), channel_id=1, source_target_pairs={{0,24},{4,28},{8,16},{12,20},{16,8},{20,12},{24,0},{28,4},{1,25},{... | collective-permute-start | bytes 1105928 | tf_op jit(solution)/shard_map/ppermute | solution.py:504
  63.0 19.8 %collective-permute-start.17 = (bf16[240,768]{1,0:T(8,128)(2,1)S(1)}, bf16[240,768]{1,0:T(8,128)(2,1)}, u32[]{:S(2)}, u32[]{:S(2)}) collective-permute-start(bf16[240,768]{1,0:T(8,128)(2,1)S(1)} %collective-permute-done.16.refs_4_), channel_id=1, source_target_pairs={{0,8},{4,12},{8,0},{12,4},{16,24},{20,28},{24,16},{28,20},{1,9},{5... | collective-permute-start | bytes 1105928 | tf_op jit(solution)/shard_map/ppermute | solution.py:504
  66.9 37.7 %collective-permute-start.18 = (bf16[240,768]{1,0:T(8,128)(2,1)S(1)}, bf16[240,768]{1,0:T(8,128)(2,1)}, u32[]{:S(2)}, u32[]{:S(2)}) collective-permute-start(bf16[240,768]{1,0:T(8,128)(2,1)S(1)} %collective-permute-done.16.refs_4_), channel_id=1, source_target_pairs={{0,16},{4,20},{8,24},{12,28},{16,0},{20,4},{24,8},{28,12},{1,17},{... | collective-permute-start | bytes 1105928 | tf_op jit(solution)/shard_map/ppermute | solution.py:504
  79.2 26.9 %collective-permute-start.19 = (bf16[240,768]{1,0:T(8,128)(2,1)S(1)}, bf16[240,768]{1,0:T(8,128)(2,1)}, u32[]{:S(2)}, u32[]{:S(2)}) collective-permute-start(bf16[240,768]{1,0:T(8,128)(2,1)S(1)} %collective-permute-done.16.refs_4_), channel_id=1, source_target_pairs={{0,24},{4,28},{8,16},{12,20},{16,8},{20,12},{24,0},{28,4},{1,25},{... | collective-permute-start | bytes 1105928 | tf_op jit(solution)/shard_map/ppermute | solution.py:504
  80.7 25.4 %collective-permute-start.21 = (bf16[240,768]{1,0:T(8,128)(2,1)S(1)}, bf16[240,768]{1,0:T(8,128)(2,1)}, u32[]{:S(2)}, u32[]{:S(2)}) collective-permute-start(bf16[240,768]{1,0:T(8,128)(2,1)S(1)} %collective-permute-done.20.refs_8_), channel_id=1, source_target_pairs={{0,8},{4,12},{8,0},{12,4},{16,24},{20,28},{24,16},{28,20},{1,9},{5... | collective-permute-start | bytes 1105928 | tf_op jit(solution)/shard_map/ppermute | solution.py:504
  82.8 26.4 %collective-permute-start.22 = (bf16[240,768]{1,0:T(8,128)(2,1)S(1)}, bf16[240,768]{1,0:T(8,128)(2,1)}, u32[]{:S(2)}, u32[]{:S(2)}) collective-permute-start(bf16[240,768]{1,0:T(8,128)(2,1)S(1)} %collective-permute-done.20.refs_8_), channel_id=1, source_target_pairs={{0,16},{4,20},{8,24},{12,28},{16,0},{20,4},{24,8},{28,12},{1,17},{... | collective-permute-start | bytes 1105928 | tf_op jit(solution)/shard_map/ppermute | solution.py:504
  83.4 25.9 %collective-permute-start.23 = (bf16[240,768]{1,0:T(8,128)(2,1)S(1)}, bf16[240,768]{1,0:T(8,128)(2,1)}, u32[]{:S(2)}, u32[]{:S(2)}) collective-permute-start(bf16[240,768]{1,0:T(8,128)(2,1)S(1)} %collective-permute-done.20.refs_8_), channel_id=1, source_target_pairs={{0,24},{4,28},{8,16},{12,20},{16,8},{20,12},{24,0},{28,4},{1,25},{... | collective-permute-start | bytes 1105928 | tf_op jit(solution)/shard_map/ppermute | solution.py:504
  106.1 6.0 %collective-permute-start.11 = (bf16[256,192]{1,0:T(8,128)(2,1)}, bf16[256,192]{1,0:T(8,128)(2,1)S(1)}, u32[]{:S(2)}, u32[]{:S(2)}) collective-permute-start(bf16[256,192]{1,0:T(8,128)(2,1)} %get-tuple-element.106), channel_id=1, source_target_pairs={{0,12},{4,8},{8,4},{12,0},{16,28},{20,24},{24,20},{28,16},{1,13},{... | collective-permute-start | bytes 294920 | tf_op jit(solution)/shard_map/ppermute | solution.py:504
  106.1 6.0 %collective-permute-start.9 = (bf16[256,192]{1,0:T(8,128)(2,1)S(1)}, bf16[256,192]{1,0:T(8,128)(2,1)S(1)}, u32[]{:S(2)}, u32[]{:S(2)}) collective-permute-start(bf16[256,192]{1,0:T(8,128)(2,1)S(1)} %copy-done.74), channel_id=1, source_target_pairs={{0,4},{4,0},{8,12},{12,8},{16,20},{20,16},{24,28},{28,24},{1,5},{5... | collective-permute-start | bytes 294920 | tf_op jit(solution)/shard_map/ppermute | solution.py:504
  129.4 8.1 %collective-permute-start.25 = (f32[256,768]{1,0:T(8,128)}, f32[256,768]{1,0:T(8,128)S(1)}, u32[]{:S(2)}, u32[]{:S(2)}) collective-permute-start(f32[256,768]{1,0:T(8,128)} %get-tuple-element.115), channel_id=1, source_target_pairs={{0,4},{4,0},{8,12},{12,8},{16,20},{20,16},{24,28},{28,24},{1,5},{5... | collective-permute-start | bytes 2359304 | tf_op jit(solution)/shard_map/ppermute | solution.py:504
  130.5 7.0 %collective-permute-start.26 = (bf16[128,768]{1,0:T(8,128)(2,1)S(1)}, bf16[128,768]{1,0:T(8,128)(2,1)S(1)}, u32[]{:S(2)}, u32[]{:S(2)}) collective-permute-start(bf16[128,768]{1,0:T(8,128)(2,1)S(1)} %get-tuple-element.185), channel_id=1, source_target_pairs={{0,16},{4,20},{8,24},{12,28},{16,0},{20,4},{24,8},{28,12},{1,17},{... | collective-permute-start | bytes 589832 | tf_op jit(solution)/shard_map/ppermute | solution.py:504
  153.0 9.6 %collective-permute-start.29 = (f32[256,768]{1,0:T(8,128)}, f32[256,768]{1,0:T(8,128)S(1)}, u32[]{:S(2)}, u32[]{:S(2)}) collective-permute-start(f32[256,768]{1,0:T(8,128)} %get-tuple-element.126), channel_id=1, source_target_pairs={{0,4},{4,0},{8,12},{12,8},{16,20},{20,16},{24,28},{28,24},{1,5},{5... | collective-permute-start | bytes 2359304 | tf_op jit(solution)/shard_map/ppermute | solution.py:504
  160.5 83.5 %collective-permute-start.43 = (bf16[384,1536]{1,0:T(8,128)(2,1)}, bf16[384,1536]{1,0:T(8,128)(2,1)S(1)}, u32[]{:S(2)}, u32[]{:S(2)}) collective-permute-start(bf16[384,1536]{1,0:T(8,128)(2,1)} %get-tuple-element.150), channel_id=1, source_target_pairs={{0,8},{4,12},{8,0},{12,4},{16,24},{20,28},{24,16},{28,20},{1,9},{5... | collective-permute-start | bytes 3538952 | tf_op jit(solution)/shard_map/ppermute | solution.py:504
  161.9 82.1 %collective-permute-start.44 = (bf16[768,768]{1,0:T(8,128)(2,1)}, bf16[768,768]{1,0:T(8,128)(2,1)S(1)}, u32[]{:S(2)}, u32[]{:S(2)}) collective-permute-start(bf16[768,768]{1,0:T(8,128)(2,1)} %get-tuple-element.152), channel_id=1, source_target_pairs={{0,16},{4,20},{8,24},{12,28},{16,0},{20,4},{24,8},{28,12},{1,17},{... | collective-permute-start | bytes 3538952 | tf_op jit(solution)/shard_map/ppermute | solution.py:504
  170.9 81.6 %collective-permute-start.59 = (bf16[800,384]{1,0:T(8,128)(2,1)}, bf16[800,384]{1,0:T(8,128)(2,1)}, u32[]{:S(2)}, u32[]{:S(2)}) collective-permute-start(bf16[800,384]{1,0:T(8,128)(2,1)} %get-tuple-element.170), channel_id=1, source_target_pairs={{0,4},{4,0},{8,12},{12,8},{16,20},{20,16},{24,28},{28,24},{1,5},{5... | collective-permute-start | bytes 1843208 | tf_op jit(solution)/shard_map/ppermute | solution.py:504
  171.4 21.0 %collective-permute-start.31 = (bf16[256,192]{1,0:T(8,128)(2,1)}, bf16[256,192]{1,0:T(8,128)(2,1)S(1)}, u32[]{:S(2)}, u32[]{:S(2)}) collective-permute-start(bf16[256,192]{1,0:T(8,128)(2,1)} %get-tuple-element.130), channel_id=1, source_target_pairs={{0,8},{4,12},{8,0},{12,4},{16,24},{20,28},{24,16},{28,20},{1,9},{5... | collective-permute-start | bytes 294920 | tf_op jit(solution)/shard_map/ppermute | solution.py:504
  172.0 22.0 %collective-permute-start.32 = (bf16[256,192]{1,0:T(8,128)(2,1)}, bf16[256,192]{1,0:T(8,128)(2,1)S(1)}, u32[]{:S(2)}, u32[]{:S(2)}) collective-permute-start(bf16[256,192]{1,0:T(8,128)(2,1)} %get-tuple-element.131), channel_id=1, source_target_pairs={{0,12},{4,8},{8,4},{12,0},{16,28},{20,24},{24,20},{28,16},{1,13},{... | collective-permute-start | bytes 294920 | tf_op jit(solution)/shard_map/ppermute | solution.py:504
  212.5 9.9 %collective-permute-start.36 = (bf16[208,576]{1,0:T(8,128)(2,1)}, bf16[208,576]{1,0:T(8,128)(2,1)S(1)}, u32[]{:S(2)}, u32[]{:S(2)}) collective-permute-start(bf16[208,576]{1,0:T(8,128)(2,1)} %get-tuple-element.140), channel_id=1, source_target_pairs={{0,3},{1,0},{2,1},{3,2},{4,7},{5,4},{6,5},{7,6},{8,11},{9,8},{10,9... | collective-permute-start | bytes 718856 | tf_op jit(solution)/shard_map/ppermute | solution.py:508
  212.5 28.2 %collective-permute-start.37 = (bf16[208,576]{1,0:T(8,128)(2,1)}, bf16[208,576]{1,0:T(8,128)(2,1)S(1)}, u32[]{:S(2)}, u32[]{:S(2)}) collective-permute-start(bf16[208,576]{1,0:T(8,128)(2,1)} %get-tuple-element.141), channel_id=1, source_target_pairs={{0,2},{1,3},{2,0},{3,1},{4,6},{5,7},{6,4},{7,5},{8,10},{9,11},{10,... | collective-permute-start | bytes 718856 | tf_op jit(solution)/shard_map/ppermute | solution.py:508
  222.4 19.0 %collective-permute-start.38 = (bf16[208,576]{1,0:T(8,128)(2,1)}, bf16[208,576]{1,0:T(8,128)(2,1)}, u32[]{:S(2)}, u32[]{:S(2)}) collective-permute-start(bf16[208,576]{1,0:T(8,128)(2,1)} %get-tuple-element.142), channel_id=1, source_target_pairs={{0,1},{1,2},{2,3},{3,0},{4,5},{5,6},{6,7},{7,4},{8,9},{9,10},{10,1... | collective-permute-start | bytes 718856 | tf_op jit(solution)/shard_map/ppermute | solution.py:508
  241.4 40.8 %collective-permute-start.33 = (bf16[512,768]{1,0:T(8,128)(2,1)}, bf16[512,768]{1,0:T(8,128)(2,1)S(1)}, u32[]{:S(2)}, u32[]{:S(2)}) collective-permute-start(bf16[512,768]{1,0:T(8,128)(2,1)} %get-tuple-element.135), channel_id=1, source_target_pairs={{0,4},{4,0},{8,12},{12,8},{16,20},{20,16},{24,28},{28,24},{1,5},{5... | collective-permute-start | bytes 2359304 | tf_op jit(solution)/shard_map/ppermute | solution.py:504
  243.5 11.7 %collective-permute-start.39 = (bf16[208,576]{1,0:T(8,128)(2,1)}, bf16[208,576]{1,0:T(8,128)(2,1)S(1)}, u32[]{:S(2)}, u32[]{:S(2)}) collective-permute-start(bf16[208,576]{1,0:T(8,128)(2,1)} %shard_map.317.mine), channel_id=1, source_target_pairs={{0,16},{4,20},{8,24},{12,28},{16,0},{20,4},{24,8},{28,12},{1,17},{... | collective-permute-start | bytes 718856 | tf_op jit(solution)/shard_map/ppermute | solution.py:504
  249.5 13.7 %collective-permute-start.45 = (bf16[192,768]{1,0:T(8,128)(2,1)}, bf16[192,768]{1,0:T(8,128)(2,1)S(1)}, u32[]{:S(2)}, u32[]{:S(2)}) collective-permute-start(bf16[192,768]{1,0:T(8,128)(2,1)} %get-tuple-element.154), channel_id=1, source_target_pairs={{0,16},{4,20},{8,24},{12,28},{16,0},{20,4},{24,8},{28,12},{1,17},{... | collective-permute-start | bytes 884744 | tf_op jit(solution)/shard_map/ppermute | solution.py:504
  251.0 13.6 %collective-permute-start.46 = (bf16[384,384]{1,0:T(8,128)(2,1)}, bf16[384,384]{1,0:T(8,128)(2,1)S(1)}, u32[]{:S(2)}, u32[]{:S(2)}) collective-permute-start(bf16[384,384]{1,0:T(8,128)(2,1)} %get-tuple-element.156), channel_id=1, source_target_pairs={{0,8},{4,12},{8,0},{12,4},{16,24},{20,28},{24,16},{28,20},{1,9},{5... | collective-permute-start | bytes 884744 | tf_op jit(solution)/shard_map/ppermute | solution.py:504
  252.4 10.7 %collective-permute-start.27 = (bf16[128,768]{1,0:T(8,128)(2,1)}, bf16[128,768]{1,0:T(8,128)(2,1)}, u32[]{:S(2)}, u32[]{:S(2)}) collective-permute-start(bf16[128,768]{1,0:T(8,128)(2,1)} %get-tuple-element.117), channel_id=1, source_target_pairs={{0,16},{4,20},{8,24},{12,28},{16,0},{20,4},{24,8},{28,12},{1,17},{... | collective-permute-start | bytes 589832 | tf_op jit(solution)/shard_map/ppermute | solution.py:504
  255.2 23.7 %collective-permute-start.60 = (bf16[416,384]{1,0:T(8,128)(2,1)}, bf16[416,384]{1,0:T(8,128)(2,1)S(1)}, u32[]{:S(2)}, u32[]{:S(2)}) collective-permute-start(bf16[416,384]{1,0:T(8,128)(2,1)} %get-tuple-element.172), channel_id=1, source_target_pairs={{0,8},{4,12},{8,0},{12,4},{16,24},{20,28},{24,16},{28,20},{1,9},{5... | collective-permute-start | bytes 958472 | tf_op jit(solution)/shard_map/ppermute | solution.py:504
  263.2 9.9 %collective-permute-start.41 = (bf16[208,576]{1,0:T(8,128)(2,1)}, bf16[208,576]{1,0:T(8,128)(2,1)S(1)}, u32[]{:S(2)}, u32[]{:S(2)}) collective-permute-start(bf16[208,576]{1,0:T(8,128)(2,1)} %shard_map.318.s0), channel_id=1, source_target_pairs={{0,8},{4,12},{8,0},{12,4},{16,24},{20,28},{24,16},{28,20},{1,9},{5... | collective-permute-start | bytes 718856 | tf_op jit(solution)/shard_map/ppermute | solution.py:504
  264.7 13.3 %collective-permute-start.42 = (bf16[208,576]{1,0:T(8,128)(2,1)}, bf16[208,576]{1,0:T(8,128)(2,1)S(1)}, u32[]{:S(2)}, u32[]{:S(2)}) collective-permute-start(bf16[208,576]{1,0:T(8,128)(2,1)} %shard_map.318.s0), channel_id=1, source_target_pairs={{0,12},{4,8},{8,4},{12,0},{16,28},{20,24},{24,20},{28,16},{1,13},{... | collective-permute-start | bytes 718856 | tf_op jit(solution)/shard_map/ppermute | solution.py:504
  267.6 18.7 %collective-permute-start.47 = (bf16[96,768]{1,0:T(8,128)(2,1)}, bf16[96,768]{1,0:T(8,128)(2,1)S(1)}, u32[]{:S(2)}, u32[]{:S(2)}) collective-permute-start(bf16[96,768]{1,0:T(8,128)(2,1)} %get-tuple-element.158), channel_id=1, source_target_pairs={{0,3},{1,0},{2,1},{3,2},{4,7},{5,4},{6,5},{7,6},{8,11},{9,8},{10,9... | collective-permute-start | bytes 442376 | tf_op jit(solution)/shard_map/ppermute | solution.py:508
  273.1 14.6 %collective-permute-start.48 = (bf16[96,768]{1,0:T(8,128)(2,1)}, bf16[96,768]{1,0:T(8,128)(2,1)S(1)}, u32[]{:S(2)}, u32[]{:S(2)}) collective-permute-start(bf16[96,768]{1,0:T(8,128)(2,1)} %get-tuple-element.159), channel_id=1, source_target_pairs={{0,2},{1,3},{2,0},{3,1},{4,6},{5,7},{6,4},{7,5},{8,10},{9,11},{10,... | collective-permute-start | bytes 442376 | tf_op jit(solution)/shard_map/ppermute | solution.py:508
  277.9 20.8 %collective-permute-start.57 = (bf16[192,768]{1,0:T(8,128)(2,1)}, bf16[192,768]{1,0:T(8,128)(2,1)S(1)}, u32[]{:S(2)}, u32[]{:S(2)}) collective-permute-start(bf16[192,768]{1,0:T(8,128)(2,1)} %get-tuple-element.162), channel_id=1, source_target_pairs={{0,16},{4,20},{8,24},{12,28},{16,0},{20,4},{24,8},{28,12},{1,17},{... | collective-permute-start | bytes 884744 | tf_op jit(solution)/shard_map/ppermute | solution.py:504
  278.9 20.9 %collective-permute-start.58 = (bf16[384,384]{1,0:T(8,128)(2,1)}, bf16[384,384]{1,0:T(8,128)(2,1)S(1)}, u32[]{:S(2)}, u32[]{:S(2)}) collective-permute-start(bf16[384,384]{1,0:T(8,128)(2,1)} %get-tuple-element.164), channel_id=1, source_target_pairs={{0,8},{4,12},{8,0},{12,4},{16,24},{20,28},{24,16},{28,20},{1,9},{5... | collective-permute-start | bytes 884744 | tf_op jit(solution)/shard_map/ppermute | solution.py:504
  282.2 17.7 %collective-permute-start.61 = (bf16[224,384]{1,0:T(8,128)(2,1)}, bf16[224,384]{1,0:T(8,128)(2,1)}, u32[]{:S(2)}, u32[]{:S(2)}) collective-permute-start(bf16[224,384]{1,0:T(8,128)(2,1)} %get-tuple-element.174), channel_id=1, source_target_pairs={{0,16},{4,20},{8,24},{12,28},{16,0},{20,4},{24,8},{28,12},{1,17},{... | collective-permute-start | bytes 516104 | tf_op jit(solution)/shard_map/ppermute | solution.py:504
  286.9 20.5 %collective-permute-start.34 = (bf16[256,768]{1,0:T(8,128)(2,1)}, bf16[256,768]{1,0:T(8,128)(2,1)S(1)}, u32[]{:S(2)}, u32[]{:S(2)}) collective-permute-start(bf16[256,768]{1,0:T(8,128)(2,1)} %get-tuple-element.138), channel_id=1, source_target_pairs={{0,8},{4,12},{8,0},{12,4},{16,24},{20,28},{24,16},{28,20},{1,9},{5... | collective-permute-start | bytes 1179656 | tf_op jit(solution)/shard_map/ppermute | solution.py:504
  287.7 7.5 %collective-permute-start.49 = (bf16[96,768]{1,0:T(8,128)(2,1)}, bf16[96,768]{1,0:T(8,128)(2,1)S(1)}, u32[]{:S(2)}, u32[]{:S(2)}) collective-permute-start(bf16[96,768]{1,0:T(8,128)(2,1)} %get-tuple-element.160), channel_id=1, source_target_pairs={{0,1},{1,2},{2,3},{3,0},{4,5},{5,6},{6,7},{7,4},{8,9},{9,10},{10,1... | collective-permute-start | bytes 442376 | tf_op jit(solution)/shard_map/ppermute | solution.py:508
  297.7 9.2 %collective-permute-start.50 = (bf16[96,768]{1,0:T(8,128)(2,1)}, bf16[96,768]{1,0:T(8,128)(2,1)S(1)}, u32[]{:S(2)}, u32[]{:S(2)}) collective-permute-start(bf16[96,768]{1,0:T(8,128)(2,1)} %shard_map.323.refs_0_), channel_id=1, source_target_pairs={{0,8},{4,12},{8,0},{12,4},{16,24},{20,28},{24,16},{28,20},{1,9},{5... | collective-permute-start | bytes 442376 | tf_op jit(solution)/shard_map/ppermute | solution.py:504
  298.7 8.2 %collective-permute-start.51 = (bf16[96,768]{1,0:T(8,128)(2,1)}, bf16[96,768]{1,0:T(8,128)(2,1)S(1)}, u32[]{:S(2)}, u32[]{:S(2)}) collective-permute-start(bf16[96,768]{1,0:T(8,128)(2,1)} %shard_map.323.refs_0_), channel_id=1, source_target_pairs={{0,16},{4,20},{8,24},{12,28},{16,0},{20,4},{24,8},{28,12},{1,17},{... | collective-permute-start | bytes 442376 | tf_op jit(solution)/shard_map/ppermute | solution.py:504
  302.9 6.1 %collective-permute-start.62 = (bf16[144,768]{1,0:T(8,128)(2,1)}, bf16[144,768]{1,0:T(8,128)(2,1)S(1)}, u32[]{:S(2)}, u32[]{:S(2)}) collective-permute-start(bf16[144,768]{1,0:T(8,128)(2,1)} %get-tuple-element.176), channel_id=1, source_target_pairs={{0,3},{1,0},{2,1},{3,2},{4,7},{5,4},{6,5},{7,6},{8,11},{9,8},{10,9... | collective-permute-start | bytes 663560 | tf_op jit(solution)/shard_map/ppermute | solution.py:508
  305.5 23.1 %collective-permute-start.52 = (bf16[96,768]{1,0:T(8,128)(2,1)}, bf16[96,768]{1,0:T(8,128)(2,1)S(1)}, u32[]{:S(2)}, u32[]{:S(2)}) collective-permute-start(bf16[96,768]{1,0:T(8,128)(2,1)} %shard_map.323.refs_0_), channel_id=1, source_target_pairs={{0,24},{4,28},{8,16},{12,20},{16,8},{20,12},{24,0},{28,4},{1,25},{... | collective-permute-start | bytes 442376 | tf_op jit(solution)/shard_map/ppermute | solution.py:504
  306.9 22.8 %collective-permute-start.53 = (bf16[96,768]{1,0:T(8,128)(2,1)}, bf16[96,768]{1,0:T(8,128)(2,1)S(1)}, u32[]{:S(2)}, u32[]{:S(2)}) collective-permute-start(bf16[96,768]{1,0:T(8,128)(2,1)} %shard_map.323.refs_0_), channel_id=1, source_target_pairs={{0,4},{4,0},{8,12},{12,8},{16,20},{20,16},{24,28},{28,24},{1,5},{5... | collective-permute-start | bytes 442376 | tf_op jit(solution)/shard_map/ppermute | solution.py:504
  306.9 23.8 %collective-permute-start.54 = (bf16[96,768]{1,0:T(8,128)(2,1)S(1)}, bf16[96,768]{1,0:T(8,128)(2,1)S(1)}, u32[]{:S(2)}, u32[]{:S(2)}) collective-permute-start(bf16[96,768]{1,0:T(8,128)(2,1)S(1)} %collective-permute-done.50.refs_1_), channel_id=1, source_target_pairs={{0,4},{4,0},{8,12},{12,8},{16,20},{20,16},{24,28},{28,24},{1,5},{5... | collective-permute-start | bytes 442376 | tf_op jit(solution)/shard_map/ppermute | solution.py:504
  307.4 18.0 %collective-permute-start.63 = (bf16[144,768]{1,0:T(8,128)(2,1)}, bf16[144,768]{1,0:T(8,128)(2,1)S(1)}, u32[]{:S(2)}, u32[]{:S(2)}) collective-permute-start(bf16[144,768]{1,0:T(8,128)(2,1)} %get-tuple-element.177), channel_id=1, source_target_pairs={{0,2},{1,3},{2,0},{3,1},{4,6},{5,7},{6,4},{7,5},{8,10},{9,11},{10,... | collective-permute-start | bytes 663560 | tf_op jit(solution)/shard_map/ppermute | solution.py:508
  309.1 16.4 %collective-permute-start.64 = (bf16[144,768]{1,0:T(8,128)(2,1)}, bf16[144,768]{1,0:T(8,128)(2,1)S(1)}, u32[]{:S(2)}, u32[]{:S(2)}) collective-permute-start(bf16[144,768]{1,0:T(8,128)(2,1)} %get-tuple-element.178), channel_id=1, source_target_pairs={{0,1},{1,2},{2,3},{3,0},{4,5},{5,6},{6,7},{7,4},{8,9},{9,10},{10,1... | collective-permute-start | bytes 663560 | tf_op jit(solution)/shard_map/ppermute | solution.py:508
  325.4 6.8 %collective-permute-start.55 = (bf16[96,768]{1,0:T(8,128)(2,1)S(1)}, bf16[96,768]{1,0:T(8,128)(2,1)S(1)}, u32[]{:S(2)}, u32[]{:S(2)}) collective-permute-start(bf16[96,768]{1,0:T(8,128)(2,1)S(1)} %collective-permute-done.51.refs_2_), channel_id=1, source_target_pairs={{0,4},{4,0},{8,12},{12,8},{16,20},{20,16},{24,28},{28,24},{1,5},{5... | collective-permute-start | bytes 442376 | tf_op jit(solution)/shard_map/ppermute | solution.py:504
  325.5 7.7 %collective-permute-start.35 = (bf16[128,768]{1,0:T(8,128)(2,1)S(1)}, bf16[128,768]{1,0:T(8,128)(2,1)S(1)}, u32[]{:S(2)}, u32[]{:S(2)}) collective-permute-start(bf16[128,768]{1,0:T(8,128)(2,1)S(1)} %slice.69), channel_id=1, source_target_pairs={{0,16},{4,20},{8,24},{12,28},{16,0},{20,4},{24,8},{28,12},{1,17},{... | collective-permute-start | bytes 589832 | tf_op jit(solution)/shard_map/ppermute | solution.py:504
  328.6 8.6 %collective-permute-start.65 = (bf16[144,768]{1,0:T(8,128)(2,1)}, bf16[144,768]{1,0:T(8,128)(2,1)S(1)}, u32[]{:S(2)}, u32[]{:S(2)}) collective-permute-start(bf16[144,768]{1,0:T(8,128)(2,1)} %shard_map.328.refs_8_), channel_id=1, source_target_pairs={{0,8},{4,12},{8,0},{12,4},{16,24},{20,28},{24,16},{28,20},{1,9},{5... | collective-permute-start | bytes 663560 | tf_op jit(solution)/shard_map/ppermute | solution.py:504
  329.7 12.5 %collective-permute-start.66 = (bf16[144,768]{1,0:T(8,128)(2,1)}, bf16[144,768]{1,0:T(8,128)(2,1)S(1)}, u32[]{:S(2)}, u32[]{:S(2)}) collective-permute-start(bf16[144,768]{1,0:T(8,128)(2,1)} %shard_map.328.refs_8_), channel_id=1, source_target_pairs={{0,16},{4,20},{8,24},{12,28},{16,0},{20,4},{24,8},{28,12},{1,17},{... | collective-permute-start | bytes 663560 | tf_op jit(solution)/shard_map/ppermute | solution.py:504
  330.8 11.5 %collective-permute-start.67 = (bf16[144,768]{1,0:T(8,128)(2,1)}, bf16[144,768]{1,0:T(8,128)(2,1)S(1)}, u32[]{:S(2)}, u32[]{:S(2)}) collective-permute-start(bf16[144,768]{1,0:T(8,128)(2,1)} %shard_map.328.refs_8_), channel_id=1, source_target_pairs={{0,24},{4,28},{8,16},{12,20},{16,8},{20,12},{24,0},{28,4},{1,25},{... | collective-permute-start | bytes 663560 | tf_op jit(solution)/shard_map/ppermute | solution.py:504
  332.2 11.5 %collective-permute-start.56 = (bf16[96,768]{1,0:T(8,128)(2,1)S(1)}, bf16[96,768]{1,0:T(8,128)(2,1)S(1)}, u32[]{:S(2)}, u32[]{:S(2)}) collective-permute-start(bf16[96,768]{1,0:T(8,128)(2,1)S(1)} %collective-permute-done.52.refs_3_), channel_id=1, source_target_pairs={{0,4},{4,0},{8,12},{12,8},{16,20},{20,16},{24,28},{28,24},{1,5},{5... | collective-permute-start | bytes 442376 | tf_op jit(solution)/shard_map/ppermute | solution.py:504
  333.1 10.6 %collective-permute-start.68 = (bf16[144,768]{1,0:T(8,128)(2,1)}, bf16[144,768]{1,0:T(8,128)(2,1)S(1)}, u32[]{:S(2)}, u32[]{:S(2)}) collective-permute-start(bf16[144,768]{1,0:T(8,128)(2,1)} %shard_map.328.refs_8_), channel_id=1, source_target_pairs={{0,4},{4,0},{8,12},{12,8},{16,20},{20,16},{24,28},{28,24},{1,5},{5... | collective-permute-start | bytes 663560 | tf_op jit(solution)/shard_map/ppermute | solution.py:504
  337.2 6.6 %collective-permute-start.69 = (bf16[144,768]{1,0:T(8,128)(2,1)S(1)}, bf16[144,768]{1,0:T(8,128)(2,1)S(1)}, u32[]{:S(2)}, u32[]{:S(2)}) collective-permute-start(bf16[144,768]{1,0:T(8,128)(2,1)S(1)} %collective-permute-done.65.refs_9_), channel_id=1, source_target_pairs={{0,4},{4,0},{8,12},{12,8},{16,20},{20,16},{24,28},{28,24},{1,5},{5... | collective-permute-start | bytes 663560 | tf_op jit(solution)/shard_map/ppermute | solution.py:504
  (83 other events, 932.4 us)

commit v3 on v2

--- a/solution.py
+++ b/solution.py
@@ -561,7 +561,7 @@
     return inner * rise, rise + inner * bell
 
 
-def run(kernel, outs, args, scratch=(), scalars=(), specs=None, out_specs=None):
+def run(kernel, outs, args, scratch=(), scalars=(), specs=None, out_specs=None, aliases=None):
     shapes = tuple(jax.ShapeDtypeStruct(shape, dtype) for shape, dtype in outs)
     whole = pl.BlockSpec(memory_space=pltpu.VMEM)
     in_specs = [pl.BlockSpec(memory_space=pltpu.SMEM)] * len(scalars)
@@ -572,6 +572,7 @@
         in_specs=in_specs,
         out_specs=tuple([whole] * len(outs) if out_specs is None else out_specs),
         scratch_shapes=list(scratch),
+        input_output_aliases=aliases or {},
     )(*scalars, *args)
 
 
@@ -1019,32 +1020,55 @@
     refs[-1][...] = short(total)
 
 
-def finish_kernel(*refs):
-    pieces, (dwi, dwo2, dwo, small) = refs[:16], refs[16:]
+def finish_rows(pieces, part, half, spread):
     core, quarter, _, _ = where_am_i()
-    part, half = dwi.shape[0] // 4, dwi.shape[1] // 8
+    dwi, dwo2, dwo = spread
     for side in range(2):
 
         @pl.when(core == side)
         def _():
             for index, piece in enumerate(pieces):
-                lane, index = index // 8, index % 8
                 spot = quarter ^ (index % 4)
                 which = side if index < 4 else 1 - side
                 rows = some_rows(spot * part, part)
                 for block in range(2):
-                    at = (2 * lane + block) * 2 * half + which * half
+                    at = block * 2 * half + which * half
                     dwi[rows, at : at + half] = wide(piece[0:part, block * half : (block + 1) * half])
                     at = which * half + spot * 2 * part + block * part
-                    dwo2[some_rows(at, part), lane * half : (lane + 1) * half] = wide(
+                    dwo2[some_rows(at, part), :] = wide(
                         piece[part : 2 * part, block * half : (block + 1) * half]
                     )
-                if lane == 1:
+                if dwo is not None:
                     dwo[rows, which * half : (which + 1) * half] = wide(piece[2 * part :, 0:half])
 
-    last = pieces[8]
+
+def send_lane(lane, dwi, dwo2, wi_out, wo2_out, sems):
+    width, half = dwi.shape[1], dwo2.shape[1]
+    copies = [
+        pltpu.make_async_copy(dwi, wi_out.at[:, lane * width : (lane + 1) * width], sems.at[0]),
+        pltpu.make_async_copy(dwo2, wo2_out.at[:, lane * half : (lane + 1) * half], sems.at[1]),
+    ]
+    for copy in copies:
+        copy.start()
+    for copy in copies:
+        copy.wait()
+
+
+def finish_first_kernel(*refs):
+    pieces, (wi_out, wo2_out, dwi, dwo2, sems) = refs[:8], refs[8:]
+    part, half = dwi.shape[0] // 4, dwo2.shape[1]
+    finish_rows(pieces, part, half, (dwi, dwo2, None))
+    send_lane(0, dwi, dwo2, wi_out, wo2_out, sems)
+
+
+def finish_kernel(*refs):
+    pieces, (unused0, unused1, wi_out, wo2_out, dwo, small, dwi, dwo2, sems) = refs[:8], refs[8:]
+    part, half = dwi.shape[0] // 4, dwo2.shape[1]
+    finish_rows(pieces, part, half, (dwi, dwo2, dwo))
+    last = pieces[0]
     small[:, 0:half] = wide(last[2 * part : 2 * part + 16, half:])
     small[:, half:] = wide(last[2 * part + 16 : 2 * part + 32, half:])
+    send_lane(1, dwi, dwo2, wi_out, wo2_out, sems)
 
 
 def attend_back_kernel(
@@ -1117,11 +1141,15 @@
         + dot_sum(far[...], grads[rows:])
     )
     sums = jnp.sum(wide(grads[...]), axis=0, keepdims=True)
-    tail = jnp.concatenate([sums, jnp.zeros((15, sums.shape[1]), F32)])
+    lines = sums.shape[1] // HEAD_DIM
     for index, out in enumerate((h0, h1, h2, h3)):
         take = pl.ds(pl.multiple_of(((own - index) & 3) * width, 16), width)
-        out[0:width, :] = dweight[take, :].astype(out.dtype)
-        out[width:, :] = tail.astype(out.dtype)
+        out[:, 0 : 3 * width] = dweight[take, :].astype(out.dtype)
+        out[:, 3 * width :] = jnp.zeros((width, HEAD_DIM), out.dtype)
+        for line in range(lines):
+            out[line : line + 1, 3 * width :] = sums[
+                :, line * HEAD_DIM : (line + 1) * HEAD_DIM
+            ].astype(out.dtype)
 
 
 def tokens_kernel(grads, weight, keep, send):
@@ -1153,7 +1181,10 @@
 
                 @pl.when(own == index ^ code)
                 def _():
-                    bias[...] = wide(ref[shard:, :])
+                    for line in range(bias.shape[1] // HEAD_DIM):
+                        bias[0:1, line * HEAD_DIM : (line + 1) * HEAD_DIM] = wide(
+                            ref[line : line + 1, 3 * shard :]
+                        )
 
 
 def plane_steps(
@@ -1332,8 +1363,8 @@
 
     h0, h1, h2, h3, grads = run(
         attend_back_kernel,
-        [((shard + 16, 3 * shard), F32)]
-        + [((shard + 16, 3 * shard), BF)] * 3
+        [((shard, 3 * shard + HEAD_DIM), F32)]
+        + [((shard, 3 * shard + HEAD_DIM), BF)] * 3
         + [((4 * count, 3 * shard), BF)],
         (qkv, logsum0, logsum1, *segs, *dmixed, mine, other, far),
         [
@@ -1369,22 +1400,35 @@
         turned = [turn(p, step) for step, p in ((1, p1), (2, p2), (3, p3))]
         (piece,) = run(total_kernel, [((size, dim), BF)], (p0, *turned))
         near = [piece] + [flip(piece, bits) for bits in (2, 4, 6)]
-        plane += near + [flip(p, 1) for p in near]
+        plane.append(near + [flip(p, 1) for p in near])
+    staged = [
+        pltpu.VMEM((shard, 4 * half), F32),
+        pltpu.VMEM((hidden, half), F32),
+        pltpu.SemaphoreType.DMA((2,)),
+    ]
+    grown = [((shard, 8 * half), F32), ((hidden, dim), F32)]
+    first_lane = run(finish_first_kernel, grown, plane[0], staged, out_specs=[LEFT] * 2)
     dinner_w, douter_w, dout_w, small = run(
         finish_kernel,
-        [((shard, 8 * half), F32), ((hidden, dim), F32), ((shard, dim), F32), ((16, dim), F32)],
-        plane,
+        grown + [((shard, dim), F32), ((16, dim), F32)],
+        (*plane[1], *first_lane),
+        staged,
+        specs=[WHOLE] * 8 + [LEFT] * 2,
+        out_specs=[LEFT] * 2 + [WHOLE] * 2,
+        aliases={8: 0, 9: 1},
     )
     dinner_b = pick(small[6:10].reshape(2, 4, half), own, 1).reshape(hidden)
     small = lax.dynamic_slice_in_dim(small[:6], own * shard, shard, 1)
 
     (heads,) = run(
-        total_kernel, [((shard + 16, 3 * shard), BF)], (h0, turn(h1, 1), turn(h2, 2), turn(h3, 3))
-    )
-    (heads,) = run(total_kernel, [((shard + 16, 3 * shard), BF)], (heads, flip(heads, 4)))
+        total_kernel,
+        [((shard, 3 * shard + HEAD_DIM), BF)],
+        (h0, turn(h1, 1), turn(h2, 2), turn(h3, 3)),
+    )
+    (heads,) = run(total_kernel, [((shard, 3 * shard + HEAD_DIM), BF)], (heads, flip(heads, 4)))
     dquery_w, dkey_w, dvalue_w, heads_b = run(
         heads_kernel,
-        [((shard, dim), F32)] * 3 + [((16, 3 * shard), F32)],
+        [((shard, dim), F32)] * 3 + [((8, 3 * shard), F32)],
         (heads, flip(heads, 1), flip(heads, 2), flip(heads, 3)),
     )
 
@@ -1392,7 +1436,8 @@
         merge_kernel, [((count, dim), F32), ((count, dim), BF)], (keep, flip(send, 1), dfirst_sum)
     )
     dtokens = near_t + wide(flip(far_t, 2))
-    tokens_grad = pair(dtokens[:rows], wide(flip(short(dtokens[rows:]), 4)), y)
+    swapped = flip(short(dtokens[rows:]), 4)
+    tokens_grad = pair(dtokens[:rows], wide(swapped), y)
 
     return (
         output[:, None],

time: 354 us -> 343 us (0.969)
  starting transfers between devices: 84.5 us -> 75.3 us
    ppermute x15, starting transfers between devices: 38.3 us -> 28.9 us  [turn(): return lax.ppermute(value, 'wt', [(i, (i - step) % 4) for i in range(4)])]
    ppermute x57, waiting for transfers between devices: 84.5 us -> 76.1 us  [flip(): return lax.ppermute(value, 'ctx', [(i, i ^ bits) for i in range(8)])]
    ppermute x15, waiting for transfers between devices: 40.6 us -> 46.6 us  [turn(): return lax.ppermute(value, 'wt', [(i, (i - step) % 4) for i in range(4)])]
    pallas_call x25 -> x26, Pallas kernels: 117 us -> 119 us  [run(): pl.pallas_call(kernel, out_shape=shapes, in_specs=in_specs, out_specs=tup...]
    unnamed x150 -> x156, local copies, waits for them, and re-layouts: 11.3 us -> 9.52 us
  transfers between devices with their start and end apart: 72 -> 72, of which waited for: 28 -> 30; matrix products, arithmetic and copies ran while one was open for 3% -> 3% of each run, Pallas kernels for 25% -> 24%
where the time goes in v3:
time: 343 us; the launch traced here: 342 us
  waiting for transfers between devices  123 us (36%)
  Pallas kernels  119 us (35%)
  starting transfers between devices  75.3 us (22%)
  local copies, waits for them, and re-layouts  17.5 us (5%)
  other arithmetic  5.59 us (2%)
    pallas_call x26, Pallas kernels, run(): pl.pallas_call(kernel, out_shape=shapes, in_specs=in_specs, out_specs=tup...  119 us
    ppermute x57, waiting for transfers between devices, flip(): return lax.ppermute(value, 'ctx', [(i, i ^ bits) for i in range(8)])  76.1 us
    ppermute x15, waiting for transfers between devices, turn(): return lax.ppermute(value, 'wt', [(i, (i - step) % 4) for i in range(4)])  46.6 us
    ppermute x57, starting transfers between devices, flip(): return lax.ppermute(value, 'ctx', [(i, i ^ bits) for i in range(8)])  46.4 us
    ppermute x15, starting transfers between devices, turn(): return lax.ppermute(value, 'wt', [(i, (i - step) % 4) for i in range(4)])  28.9 us
    unnamed x156, local copies, waits for them, and re-layouts  9.52 us
  transfers between devices with their start and end apart: 72, of which 30 were waited for; matrix products, arithmetic and copies ran while one was open for 3% of the time, Pallas kernels for 24%

profile of v3, /device:TPU:0, one launch (start us, length us, event | category | flops | bytes accessed | tf_op | source)
XLA Modules:
  0.0 341.6 jit_solution(18153463692338394169)
XLA Ops:
  1.8 3.1 collective-permute-start
  5.9 3.9 %collective-permute-done = bf16[128,768]{1,0:T(8,128)(2,1)S(1)} collective-permute-done((bf16[128,768]{1,0:T(8,128)(2,1)S(1)}, bf16[128,768]{1,0:T(8,128)(2,1)S(1)}, u32[]{:S(2)}, u32[]{:S(2)}) %collective-permute-start) | collective-permute-done | bytes 196640 | tf_op jit(solution)/shard_map/ppermute | solution.py:504
  9.8 1.8 collective-permute-start.1
  12.4 2.0 shard_map.305
  14.4 3.6 %collective-permute-start.3 = (bf16[112,576]{1,0:T(8,128)(2,1)}, bf16[112,576]{1,0:T(8,128)(2,1)S(1)}, u32[]{:S(2)}, u32[]{:S(2)}) collective-permute-start(bf16[112,576]{1,0:T(8,128)(2,1)} %get-tuple-element.103), channel_id=1, source_target_pairs={{0,3},{1,0},{2,1},{3,2},{4,7},{5,4},{6,5},{7,6},{8,11},{9,8},{10,9... | collective-permute-start | bytes 387080 | tf_op jit(solution)/shard_map/ppermute | solution.py:508
  18.0 3.0 shard_map.308
  21.7 2.2 collective-permute-start.16
  24.0 2.0 collective-permute-start.5
  26.0 2.0 collective-permute-done.4.g2
  28.0 1.5 collective-permute-start.6
  30.9 12.3 %collective-permute-done.5.g3 = bf16[112,576]{1,0:T(8,128)(2,1)S(1)} collective-permute-done((bf16[112,576]{1,0:T(8,128)(2,1)S(1)}, bf16[112,576]{1,0:T(8,128)(2,1)S(1)}, u32[]{:S(2)}, u32[]{:S(2)}) %collective-permute-start.5) | collective-permute-done | bytes 129056 | tf_op jit(solution)/shard_map/ppermute | solution.py:508
  43.3 10.5 %collective-permute-start.20 = (bf16[240,768]{1,0:T(8,128)(2,1)S(1)}, bf16[240,768]{1,0:T(8,128)(2,1)S(1)}, u32[]{:S(2)}, u32[]{:S(2)}) collective-permute-start(bf16[240,768]{1,0:T(8,128)(2,1)S(1)} %copy-done.74), channel_id=1, source_target_pairs={{0,1},{1,2},{2,3},{3,0},{4,5},{5,6},{6,7},{7,4},{8,9},{9,10},{10,1... | collective-permute-start | bytes 1105928 | tf_op jit(solution)/shard_map/ppermute | solution.py:508
  53.8 1.5 collective-permute-start.8
  56.0 3.8 %collective-permute-done.8.h3 = bf16[112,576]{1,0:T(8,128)(2,1)} collective-permute-done((bf16[112,576]{1,0:T(8,128)(2,1)S(1)}, bf16[112,576]{1,0:T(8,128)(2,1)}, u32[]{:S(2)}, u32[]{:S(2)}) %collective-permute-start.8) | collective-permute-done | bytes 129056 | tf_op jit(solution)/shard_map/ppermute | solution.py:504
  59.8 1.5 collective-permute-start.14
  63.0 1.5 collective-permute-start.17
  64.8 2.1 collective-permute-done.13.refs_1_
  67.5 11.7 %collective-permute-done.14.refs_2_ = bf16[240,768]{1,0:T(8,128)(2,1)S(1)} collective-permute-done((bf16[240,768]{1,0:T(8,128)(2,1)S(1)}, bf16[240,768]{1,0:T(8,128)(2,1)S(1)}, u32[]{:S(2)}, u32[]{:S(2)}) %collective-permute-start.14) | collective-permute-done | bytes 368672 | tf_op jit(solution)/shard_map/ppermute | solution.py:504
  86.0 10.8 %shard_map.306 = (bf16[9,1024,64]{2,1,0:T(8,128)(2,1)}, bf16[256,192]{1,0:T(8,128)(2,1)}, bf16[256,192]{1,0:T(8,128)(2,1)}, f32[512,128]{1,0:T(8,128)}, bf16[768...) custom-call(bf16[256,768]{1,0:T(8,128)(2,1)} %copy-done, bf16[256,768]{1,0:T(8,128)(2,1)} %copy-done.1, ...), custom_call_target="tpu_custom_call" | custom-call | tf_op jit(solution)/shard_map/pallas_call | solution.py:569
  96.8 7.8 %shard_map.307 = (bf16[256,192]{1,0:T(8,128)(2,1)}, bf16[256,192]{1,0:T(8,128)(2,1)}, f32[512,128]{1,0:T(8,128)}) custom-call(bf16[9,1024,64]{2,1,0:T(8,128)(2,1)} %get-tuple-element.106.qkv, s32[1024,1]{1,0:T(8,128)} %copy.43.seg_col, s32[1,1024]{1,0:T(1,128)} %bitcast.52), custom_call_target="tpu_custom_call" | custom-call | tf_op jit(solution)/shard_map/pallas_call | solution.py:569
  106.7 2.5 collective-permute-done.22.refs_10_
  110.3 1.8 collective-permute-done.11.m3
  112.8 4.7 %shard_map.309 = (f32[256,768]{1,0:T(8,128)}, bf16[256,768]{1,0:T(8,128)(2,1)}, bf16[768,768]{1,0:T(8,128)(2,1)}) custom-call(bf16[256,192]{1,0:T(8,128)(2,1)} %get-tuple-element.104.m0, bf16[256,192]{1,0:T(8,128)(2,1)} %copy-done.21, bf16[256,192]{1,0:T(8,128)(2,1)} %copy-done.19, bf16[256,192]{1,0:T(8,128)(2,1)} %copy-done.20, bf16[256,768]{1,0:T(8,128)(2,1)} %copy-done, ...), custom_call_target="tpu_custom_call" | custom-call | tf_op jit(solution)/shard_map/pallas_call | solution.py:569
  117.9 1.6 collective-permute-done.24.far.first1
  120.2 9.1 %shard_map.310 = (f32[256,768]{1,0:T(8,128)}, f32[256,768]{1,0:T(8,128)}, bf16[512,1536]{1,0:T(8,128)(2,1)}, bf16[512,1536]{1,0:T(8,128)(2,1)}, bf16[768,1536]{1,0:T(8,128)(2,1)}, /*index=5*/bf16[1536,768]{1,0:T(8,128)(2,1)}) custom-call(bf16[256,768]{1,0:T(8,128)(2,1)} %get-tuple-element.112.near.first0, bf16[256,768]{1,0:T(8,128)(2,1)} %copy-done.3, ...), custom_call_target="tpu_custom_call" | custom-call | tf_op jit(solution)/shard_map/pallas_call | solution.py:569
  131.1 6.4 %collective-permute-done.26.cot1 = bf16[128,768]{1,0:T(8,128)(2,1)S(1)} collective-permute-done((bf16[128,768]{1,0:T(8,128)(2,1)S(1)}, bf16[128,768]{1,0:T(8,128)(2,1)S(1)}, u32[]{:S(2)}, u32[]{:S(2)}) %collective-permute-start.26) | collective-permute-done | bytes 196640 | tf_op jit(solution)/shard_map/ppermute | solution.py:504
  138.5 3.7 %shard_map.311 = (bf16[128,768]{1,0:T(8,128)(2,1)}, bf16[128,768]{1,0:T(8,128)(2,1)}, f32[256,768]{1,0:T(8,128)}, bf16[256,768]{1,0:T(8,128)(2,1)}, f32[8,768]{1,0:T(8,128)}) custom-call(f32[256,768]{1,0:T(8,128)} %get-tuple-element.111.first_sum, f32[256,768]{1,0:T(8,128)} %get-tuple-element.116.keep, f32[256,768]{1,0:T(8,128)} %copy-done.15, ...), custom_call_target="tpu_custom_call" | custom-call | tf_op jit(solution)/shard_map/pallas_call | solution.py:569
  142.3 1.9 collective-permute-done.28.far.douter1
  144.9 8.1 %shard_map.312 = (f32[256,768]{1,0:T(8,128)}, f32[256,768]{1,0:T(8,128)}, bf16[512,1536]{1,0:T(8,128)(2,1)}, f32[8,768]{1,0:T(8,128)}) custom-call(bf16[256,768]{1,0:T(8,128)(2,1)} %get-tuple-element.123.near.douter0, bf16[256,768]{1,0:T(8,128)(2,1)} %copy-done.4, bf16[512,1536]{1,0:T(8,128)(2,1)} %get-tuple-element.124.slope, ...), custom_call_target="tpu_custom_call" | custom-call | tf_op jit(solution)/shard_map/pallas_call | solution.py:569
  153.0 7.3 %shard_map.320 = (bf16[384,1536]{1,0:T(8,128)(2,1)}, bf16[384,1536]{1,0:T(8,128)(2,1)}, bf16[768,768]{1,0:T(8,128)(2,1)}, bf16[768,768]{1,0:T(8,128)(2,1)}) custom-call(bf16[256,768]{1,0:T(8,128)(2,1)} %get-tuple-element.112.near.first0, bf16[256,768]{1,0:T(8,128)(2,1)} %copy-done.3, bf16[256,768]{1,0:T(8,128)(2,1)} %get-tuple-element.123.near.douter0, ...), custom_call_target="tpu_custom_call" | custom-call | tf_op jit(solution)/shard_map/pallas_call | solution.py:569
  162.6 1.7 collective-permute-done.29.got
  165.1 4.4 %shard_map.313 = (f32[256,768]{1,0:T(8,128)}, bf16[256,768]{1,0:T(8,128)(2,1)}, bf16[256,192]{1,0:T(8,128)(2,1)}, bf16[256,192]{1,0:T(8,128)(2,1)}, bf16[256,192...) custom-call(f32[256,768]{1,0:T(8,128)} %get-tuple-element.111.first_sum, ...), custom_call_target="tpu_custom_call" | custom-call | tf_op jit(solution)/shard_map/pallas_call | solution.py:569
  169.5 3.0 shard_map.322
  175.9 16.4 %collective-permute-done.31.p2 = bf16[256,192]{1,0:T(8,128)(2,1)S(1)} collective-permute-done((bf16[256,192]{1,0:T(8,128)(2,1)}, bf16[256,192]{1,0:T(8,128)(2,1)S(1)}, u32[]{:S(2)}, u32[]{:S(2)}) %collective-permute-start.31) | collective-permute-done | bytes 98336 | tf_op jit(solution)/shard_map/ppermute | solution.py:504
  194.0 17.9 %shard_map.314 = (f32[192,640]{1,0:T(8,128)}, bf16[192,640]{1,0:T(8,128)(2,1)}, bf16[192,640]{1,0:T(8,128)(2,1)}, bf16[192,640]{1,0:T(8,128)(2,1)}, bf16[1024,576]{1,0:T(8,128)(2,1)}) custom-call(s32[2,4]{1,0:T(2,128)} %pad_add_fusion.bounds, bf16[9,1024,64]{2,1,0:T(8,128)(2,1)} %get-tuple-element.106.qkv, f32[512,128]{1,0:T(8,128)} %get-tuple-element.120.logsum0, ...), custom_call_target="tpu_custom_call" | custom-call | tf_op jit(solution)/shard_map/pallas_call | solution.py:569
  212.7 3.9 %collective-permute-start.37 = (bf16[192,640]{1,0:T(8,128)(2,1)}, bf16[192,640]{1,0:T(8,128)(2,1)S(1)}, u32[]{:S(2)}, u32[]{:S(2)}) collective-permute-start(bf16[192,640]{1,0:T(8,128)(2,1)} %get-tuple-element.143), channel_id=1, source_target_pairs={{0,2},{1,3},{2,0},{3,1},{4,6},{5,7},{6,4},{7,5},{8,10},{9,11},{10,... | collective-permute-start | bytes 737288 | tf_op jit(solution)/shard_map/ppermute | solution.py:508
  217.7 4.1 %shard_map.321 = (bf16[192,768]{1,0:T(8,128)(2,1)}, bf16[192,768]{1,0:T(8,128)(2,1)}, bf16[384,384]{1,0:T(8,128)(2,1)}, bf16[384,384]{1,0:T(8,128)(2,1)}, bf16[1...) custom-call(bf16[384,1536]{1,0:T(8,128)(2,1)} %get-tuple-element.151.ak, ...), custom_call_target="tpu_custom_call" | custom-call | tf_op jit(solution)/shard_map/pallas_call | solution.py:569
  221.8 1.5 collective-permute-start.60
  223.3 4.0 %shard_map.315 = (f32[512,768]{1,0:T(8,128)}, bf16[512,768]{1,0:T(8,128)(2,1)}) custom-call(bf16[1024,576]{1,0:T(8,128)(2,1)} %get-tuple-element.134.grads, bf16[768,576]{1,0:T(8,128)(2,1)} %get-tuple-element.135.weight), custom_call_target="tpu_custom_call" | custom-call | tf_op jit(solution)/shard_map/pallas_call | solution.py:569
  227.3 11.2 %collective-permute-done.37.refs_1_ = bf16[192,640]{1,0:T(8,128)(2,1)S(1)} collective-permute-done((bf16[192,640]{1,0:T(8,128)(2,1)}, bf16[192,640]{1,0:T(8,128)(2,1)S(1)}, u32[]{:S(2)}, u32[]{:S(2)}) %collective-permute-start.37) | collective-permute-done | bytes 245792 | tf_op jit(solution)/shard_map/ppermute | solution.py:508
  240.5 2.1 shard_map.317.mine
  244.7 2.2 shard_map.323
  249.8 2.1 shard_map.327
  252.0 1.9 collective-permute-done.39.refs_0_
  254.5 1.8 shard_map.318.s0
  256.4 3.7 %collective-permute-done.62.refs_0_ = bf16[96,768]{1,0:T(8,128)(2,1)S(1)} collective-permute-done((bf16[96,768]{1,0:T(8,128)(2,1)}, bf16[96,768]{1,0:T(8,128)(2,1)S(1)}, u32[]{:S(2)}, u32[]{:S(2)}) %collective-permute-start.62) | collective-permute-done | bytes 147488 | tf_op jit(solution)/shard_map/ppermute | solution.py:508
  260.8 2.4 collective-permute-done.63.refs_1_
  264.5 1.9 shard_map.324
  267.3 3.0 shard_map.316
  270.3 1.6 collective-permute-done.64.refs_2_
  273.9 1.9 shard_map.328.refs_0_
  277.1 2.2 collective-permute-start.67
  279.4 1.8 maximum_select_fusion.1
  281.2 3.0 shard_map.319
  284.2 3.7 %collective-permute-done.65.refs_1_ = bf16[96,768]{1,0:T(8,128)(2,1)S(1)} collective-permute-done((bf16[96,768]{1,0:T(8,128)(2,1)}, bf16[96,768]{1,0:T(8,128)(2,1)S(1)}, u32[]{:S(2)}, u32[]{:S(2)}) %collective-permute-start.65) | collective-permute-done | bytes 147488 | tf_op jit(solution)/shard_map/ppermute | solution.py:504
  291.7 2.4 shard_map.325
  294.1 2.9 collective-permute-start.50
  297.7 1.5 collective-permute-start.52
  299.3 2.9 shard_map.329
  303.5 13.1 %collective-permute-done.51.refs_1_ = bf16[144,768]{1,0:T(8,128)(2,1)S(1)} collective-permute-done((bf16[144,768]{1,0:T(8,128)(2,1)}, bf16[144,768]{1,0:T(8,128)(2,1)S(1)}, u32[]{:S(2)}, u32[]{:S(2)}) %collective-permute-start.51) | collective-permute-done | bytes 221216 | tf_op jit(solution)/shard_map/ppermute | solution.py:508
  317.4 2.0 shard_map.326.refs_0_
  323.0 4.9 %collective-permute-done.53.refs_1_ = bf16[144,768]{1,0:T(8,128)(2,1)S(1)} collective-permute-done((bf16[144,768]{1,0:T(8,128)(2,1)}, bf16[144,768]{1,0:T(8,128)(2,1)S(1)}, u32[]{:S(2)}, u32[]{:S(2)}) %collective-permute-start.53) | collective-permute-done | bytes 221216 | tf_op jit(solution)/shard_map/ppermute | solution.py:504
  328.0 4.4 %collective-permute-done.54.refs_2_ = bf16[144,768]{1,0:T(8,128)(2,1)S(1)} collective-permute-done((bf16[144,768]{1,0:T(8,128)(2,1)}, bf16[144,768]{1,0:T(8,128)(2,1)S(1)}, u32[]{:S(2)}, u32[]{:S(2)}) %collective-permute-start.54) | collective-permute-done | bytes 221216 | tf_op jit(solution)/shard_map/ppermute | solution.py:504
  334.8 4.0 %shard_map.330 = (f32[192,3072]{1,0:T(8,128)}, f32[768,768]{1,0:T(8,128)}, f32[192,768]{1,0:T(8,128)}, f32[16,768]{1,0:T(8,128)}) custom-call(bf16[144,768]{1,0:T(8,128)(2,1)} %shard_map.326.refs_0_, bf16[144,768]{1,0:T(8,128)(2,1)} %copy-done.34, bf16[144,768]{1,0:T(8,128)(2,1)} %copy-done.35, ...), custom_call_target="tpu_custom_call", output_to_operand_aliasing={{0}: (8, {}), {1}: (9, {})} | custom-call | tf_op jit(solution)/shard_map/pallas_call | solution.py:569
  (299 shorter events, 62.7 us)
Async XLA Ops:
  1.8 8.0 %collective-permute-start = (bf16[128,768]{1,0:T(8,128)(2,1)S(1)}, bf16[128,768]{1,0:T(8,128)(2,1)S(1)}, u32[]{:S(2)}, u32[]{:S(2)}) collective-permute-start(bf16[128,768]{1,0:T(8,128)(2,1)S(1)} %get-tuple-element.192), channel_id=1, source_target_pairs={{0,16},{4,20},{8,24},{12,28},{16,0},{20,4},{24,8},{28,12},{1,17},{... | collective-permute-start | bytes 589832 | tf_op jit(solution)/shard_map/ppermute | solution.py:504
  9.8 19.7 %collective-permute-start.1 = (bf16[256,768]{1,0:T(8,128)(2,1)S(1)}, bf16[256,768]{1,0:T(8,128)(2,1)S(1)}, u32[]{:S(2)}, u32[]{:S(2)}) collective-permute-start(bf16[256,768]{1,0:T(8,128)(2,1)S(1)} %pad_maximum_fusion.1.mine), channel_id=1, source_target_pairs={{0,8},{4,12},{8,0},{12,4},{16,24},{20,28},{24,16},{28,20},{1,9},{5... | collective-permute-start | bytes 1179656 | tf_op jit(solution)/shard_map/ppermute | solution.py:504
  14.4 9.6 %collective-permute-start.3 = (bf16[112,576]{1,0:T(8,128)(2,1)}, bf16[112,576]{1,0:T(8,128)(2,1)S(1)}, u32[]{:S(2)}, u32[]{:S(2)}) collective-permute-start(bf16[112,576]{1,0:T(8,128)(2,1)} %get-tuple-element.103), channel_id=1, source_target_pairs={{0,3},{1,0},{2,1},{3,2},{4,7},{5,4},{6,5},{7,6},{8,11},{9,8},{10,9... | collective-permute-start | bytes 387080 | tf_op jit(solution)/shard_map/ppermute | solution.py:508
  18.0 10.0 %collective-permute-start.4 = (bf16[112,576]{1,0:T(8,128)(2,1)}, bf16[112,576]{1,0:T(8,128)(2,1)S(1)}, u32[]{:S(2)}, u32[]{:S(2)}) collective-permute-start(bf16[112,576]{1,0:T(8,128)(2,1)} %get-tuple-element.103), channel_id=1, source_target_pairs={{0,2},{1,3},{2,0},{3,1},{4,6},{5,7},{6,4},{7,5},{8,10},{9,11},{10,... | collective-permute-start | bytes 387080 | tf_op jit(solution)/shard_map/ppermute | solution.py:508
  20.9 34.4 %collective-permute-start.12 = (bf16[240,768]{1,0:T(8,128)(2,1)}, bf16[240,768]{1,0:T(8,128)(2,1)S(1)}, u32[]{:S(2)}, u32[]{:S(2)}) collective-permute-start(bf16[240,768]{1,0:T(8,128)(2,1)} %get-tuple-element.110), channel_id=1, source_target_pairs={{0,3},{1,0},{2,1},{3,2},{4,7},{5,4},{6,5},{7,6},{8,11},{9,8},{10,9... | collective-permute-start | bytes 1105928 | tf_op jit(solution)/shard_map/ppermute | solution.py:508
  21.7 39.8 %collective-permute-start.16 = (bf16[240,768]{1,0:T(8,128)(2,1)}, bf16[240,768]{1,0:T(8,128)(2,1)S(1)}, u32[]{:S(2)}, u32[]{:S(2)}) collective-permute-start(bf16[240,768]{1,0:T(8,128)(2,1)} %get-tuple-element.110), channel_id=1, source_target_pairs={{0,2},{1,3},{2,0},{3,1},{4,6},{5,7},{6,4},{7,5},{8,10},{9,11},{10,... | collective-permute-start | bytes 1105928 | tf_op jit(solution)/shard_map/ppermute | solution.py:508
  24.0 19.3 %collective-permute-start.5 = (bf16[112,576]{1,0:T(8,128)(2,1)S(1)}, bf16[112,576]{1,0:T(8,128)(2,1)S(1)}, u32[]{:S(2)}, u32[]{:S(2)}) collective-permute-start(bf16[112,576]{1,0:T(8,128)(2,1)S(1)} %copy-done.76), channel_id=1, source_target_pairs={{0,1},{1,2},{2,3},{3,0},{4,5},{5,6},{6,7},{7,4},{8,9},{9,10},{10,1... | collective-permute-start | bytes 387080 | tf_op jit(solution)/shard_map/ppermute | solution.py:508
  28.0 15.3 %collective-permute-start.6 = (bf16[112,576]{1,0:T(8,128)(2,1)S(1)}, bf16[112,576]{1,0:T(8,128)(2,1)S(1)}, u32[]{:S(2)}, u32[]{:S(2)}) collective-permute-start(bf16[112,576]{1,0:T(8,128)(2,1)S(1)} %collective-permute-done.3.g1), channel_id=1, source_target_pairs={{0,16},{4,20},{8,24},{12,28},{16,0},{20,4},{24,8},{28,12},{1,17},{... | collective-permute-start | bytes 387080 | tf_op jit(solution)/shard_map/ppermute | solution.py:504
  29.5 24.3 %collective-permute-start.7 = (bf16[112,576]{1,0:T(8,128)(2,1)S(1)}, bf16[112,576]{1,0:T(8,128)(2,1)S(1)}, u32[]{:S(2)}, u32[]{:S(2)}) collective-permute-start(bf16[112,576]{1,0:T(8,128)(2,1)S(1)} %collective-permute-done.4.g2), channel_id=1, source_target_pairs={{0,16},{4,20},{8,24},{12,28},{16,0},{20,4},{24,8},{28,12},{1,17},{... | collective-permute-start | bytes 387080 | tf_op jit(solution)/shard_map/ppermute | solution.py:504
  43.2 40.2 %collective-permute-start.2 = (bf16[512,768]{1,0:T(8,128)(2,1)}, bf16[512,768]{1,0:T(8,128)(2,1)S(1)}, u32[]{:S(2)}, u32[]{:S(2)}) collective-permute-start(bf16[512,768]{1,0:T(8,128)(2,1)} %pad_maximum_fusion), channel_id=1, source_target_pairs={{0,4},{4,0},{8,12},{12,8},{16,20},{20,16},{24,28},{28,24},{1,5},{5... | collective-permute-start | bytes 2359304 | tf_op jit(solution)/shard_map/ppermute | solution.py:504
  43.3 19.7 %collective-permute-start.20 = (bf16[240,768]{1,0:T(8,128)(2,1)S(1)}, bf16[240,768]{1,0:T(8,128)(2,1)S(1)}, u32[]{:S(2)}, u32[]{:S(2)}) collective-permute-start(bf16[240,768]{1,0:T(8,128)(2,1)S(1)} %copy-done.74), channel_id=1, source_target_pairs={{0,1},{1,2},{2,3},{3,0},{4,5},{5,6},{6,7},{7,4},{8,9},{9,10},{10,1... | collective-permute-start | bytes 1105928 | tf_op jit(solution)/shard_map/ppermute | solution.py:508
  53.8 6.0 %collective-permute-start.8 = (bf16[112,576]{1,0:T(8,128)(2,1)S(1)}, bf16[112,576]{1,0:T(8,128)(2,1)}, u32[]{:S(2)}, u32[]{:S(2)}) collective-permute-start(bf16[112,576]{1,0:T(8,128)(2,1)S(1)} %collective-permute-done.5.g3), channel_id=1, source_target_pairs={{0,16},{4,20},{8,24},{12,28},{16,0},{20,4},{24,8},{28,12},{1,17},{... | collective-permute-start | bytes 387080 | tf_op jit(solution)/shard_map/ppermute | solution.py:504
  55.4 11.5 %collective-permute-start.13 = (bf16[240,768]{1,0:T(8,128)(2,1)S(1)}, bf16[240,768]{1,0:T(8,128)(2,1)S(1)}, u32[]{:S(2)}, u32[]{:S(2)}) collective-permute-start(bf16[240,768]{1,0:T(8,128)(2,1)S(1)} %collective-permute-done.12.refs_0_), channel_id=1, source_target_pairs={{0,8},{4,12},{8,0},{12,4},{16,24},{20,28},{24,16},{28,20},{1,9},{5... | collective-permute-start | bytes 1105928 | tf_op jit(solution)/shard_map/ppermute | solution.py:504
  59.8 19.4 %collective-permute-start.14 = (bf16[240,768]{1,0:T(8,128)(2,1)S(1)}, bf16[240,768]{1,0:T(8,128)(2,1)S(1)}, u32[]{:S(2)}, u32[]{:S(2)}) collective-permute-start(bf16[240,768]{1,0:T(8,128)(2,1)S(1)} %collective-permute-done.12.refs_0_), channel_id=1, source_target_pairs={{0,16},{4,20},{8,24},{12,28},{16,0},{20,4},{24,8},{28,12},{1,17},{... | collective-permute-start | bytes 1105928 | tf_op jit(solution)/shard_map/ppermute | solution.py:504
  61.5 19.1 %collective-permute-start.15 = (bf16[240,768]{1,0:T(8,128)(2,1)S(1)}, bf16[240,768]{1,0:T(8,128)(2,1)S(1)}, u32[]{:S(2)}, u32[]{:S(2)}) collective-permute-start(bf16[240,768]{1,0:T(8,128)(2,1)S(1)} %collective-permute-done.12.refs_0_), channel_id=1, source_target_pairs={{0,24},{4,28},{8,16},{12,20},{16,8},{20,12},{24,0},{28,4},{1,25},{... | collective-permute-start | bytes 1105928 | tf_op jit(solution)/shard_map/ppermute | solution.py:504
  63.0 19.8 %collective-permute-start.17 = (bf16[240,768]{1,0:T(8,128)(2,1)S(1)}, bf16[240,768]{1,0:T(8,128)(2,1)}, u32[]{:S(2)}, u32[]{:S(2)}) collective-permute-start(bf16[240,768]{1,0:T(8,128)(2,1)S(1)} %collective-permute-done.16.refs_4_), channel_id=1, source_target_pairs={{0,8},{4,12},{8,0},{12,4},{16,24},{20,28},{24,16},{28,20},{1,9},{5... | collective-permute-start | bytes 1105928 | tf_op jit(solution)/shard_map/ppermute | solution.py:504
  66.9 37.7 %collective-permute-start.18 = (bf16[240,768]{1,0:T(8,128)(2,1)S(1)}, bf16[240,768]{1,0:T(8,128)(2,1)}, u32[]{:S(2)}, u32[]{:S(2)}) collective-permute-start(bf16[240,768]{1,0:T(8,128)(2,1)S(1)} %collective-permute-done.16.refs_4_), channel_id=1, source_target_pairs={{0,16},{4,20},{8,24},{12,28},{16,0},{20,4},{24,8},{28,12},{1,17},{... | collective-permute-start | bytes 1105928 | tf_op jit(solution)/shard_map/ppermute | solution.py:504
  79.2 26.9 %collective-permute-start.19 = (bf16[240,768]{1,0:T(8,128)(2,1)S(1)}, bf16[240,768]{1,0:T(8,128)(2,1)}, u32[]{:S(2)}, u32[]{:S(2)}) collective-permute-start(bf16[240,768]{1,0:T(8,128)(2,1)S(1)} %collective-permute-done.16.refs_4_), channel_id=1, source_target_pairs={{0,24},{4,28},{8,16},{12,20},{16,8},{20,12},{24,0},{28,4},{1,25},{... | collective-permute-start | bytes 1105928 | tf_op jit(solution)/shard_map/ppermute | solution.py:504
  80.7 25.4 %collective-permute-start.21 = (bf16[240,768]{1,0:T(8,128)(2,1)S(1)}, bf16[240,768]{1,0:T(8,128)(2,1)}, u32[]{:S(2)}, u32[]{:S(2)}) collective-permute-start(bf16[240,768]{1,0:T(8,128)(2,1)S(1)} %collective-permute-done.20.refs_8_), channel_id=1, source_target_pairs={{0,8},{4,12},{8,0},{12,4},{16,24},{20,28},{24,16},{28,20},{1,9},{5... | collective-permute-start | bytes 1105928 | tf_op jit(solution)/shard_map/ppermute | solution.py:504
  82.8 26.4 %collective-permute-start.22 = (bf16[240,768]{1,0:T(8,128)(2,1)S(1)}, bf16[240,768]{1,0:T(8,128)(2,1)}, u32[]{:S(2)}, u32[]{:S(2)}) collective-permute-start(bf16[240,768]{1,0:T(8,128)(2,1)S(1)} %collective-permute-done.20.refs_8_), channel_id=1, source_target_pairs={{0,16},{4,20},{8,24},{12,28},{16,0},{20,4},{24,8},{28,12},{1,17},{... | collective-permute-start | bytes 1105928 | tf_op jit(solution)/shard_map/ppermute | solution.py:504
  83.4 25.8 %collective-permute-start.23 = (bf16[240,768]{1,0:T(8,128)(2,1)S(1)}, bf16[240,768]{1,0:T(8,128)(2,1)}, u32[]{:S(2)}, u32[]{:S(2)}) collective-permute-start(bf16[240,768]{1,0:T(8,128)(2,1)S(1)} %collective-permute-done.20.refs_8_), channel_id=1, source_target_pairs={{0,24},{4,28},{8,16},{12,20},{16,8},{20,12},{24,0},{28,4},{1,25},{... | collective-permute-start | bytes 1105928 | tf_op jit(solution)/shard_map/ppermute | solution.py:504
  106.1 6.0 %collective-permute-start.11 = (bf16[256,192]{1,0:T(8,128)(2,1)}, bf16[256,192]{1,0:T(8,128)(2,1)S(1)}, u32[]{:S(2)}, u32[]{:S(2)}) collective-permute-start(bf16[256,192]{1,0:T(8,128)(2,1)} %get-tuple-element.108), channel_id=1, source_target_pairs={{0,12},{4,8},{8,4},{12,0},{16,28},{20,24},{24,20},{28,16},{1,13},{... | collective-permute-start | bytes 294920 | tf_op jit(solution)/shard_map/ppermute | solution.py:504
  106.1 6.0 %collective-permute-start.9 = (bf16[256,192]{1,0:T(8,128)(2,1)S(1)}, bf16[256,192]{1,0:T(8,128)(2,1)S(1)}, u32[]{:S(2)}, u32[]{:S(2)}) collective-permute-start(bf16[256,192]{1,0:T(8,128)(2,1)S(1)} %copy-done.77), channel_id=1, source_target_pairs={{0,4},{4,0},{8,12},{12,8},{16,20},{20,16},{24,28},{28,24},{1,5},{5... | collective-permute-start | bytes 294920 | tf_op jit(solution)/shard_map/ppermute | solution.py:504
  129.4 8.1 %collective-permute-start.25 = (f32[256,768]{1,0:T(8,128)}, f32[256,768]{1,0:T(8,128)S(1)}, u32[]{:S(2)}, u32[]{:S(2)}) collective-permute-start(f32[256,768]{1,0:T(8,128)} %get-tuple-element.117), channel_id=1, source_target_pairs={{0,4},{4,0},{8,12},{12,8},{16,20},{20,16},{24,28},{28,24},{1,5},{5... | collective-permute-start | bytes 2359304 | tf_op jit(solution)/shard_map/ppermute | solution.py:504
  130.5 7.0 %collective-permute-start.26 = (bf16[128,768]{1,0:T(8,128)(2,1)S(1)}, bf16[128,768]{1,0:T(8,128)(2,1)S(1)}, u32[]{:S(2)}, u32[]{:S(2)}) collective-permute-start(bf16[128,768]{1,0:T(8,128)(2,1)S(1)} %get-tuple-element.189), channel_id=1, source_target_pairs={{0,16},{4,20},{8,24},{12,28},{16,0},{20,4},{24,8},{28,12},{1,17},{... | collective-permute-start | bytes 589832 | tf_op jit(solution)/shard_map/ppermute | solution.py:504
  160.4 52.4 %collective-permute-start.43 = (bf16[384,1536]{1,0:T(8,128)(2,1)}, bf16[384,1536]{1,0:T(8,128)(2,1)S(1)}, u32[]{:S(2)}, u32[]{:S(2)}) collective-permute-start(bf16[384,1536]{1,0:T(8,128)(2,1)} %get-tuple-element.152), channel_id=1, source_target_pairs={{0,8},{4,12},{8,0},{12,4},{16,24},{20,28},{24,16},{28,20},{1,9},{5... | collective-permute-start | bytes 3538952 | tf_op jit(solution)/shard_map/ppermute | solution.py:504
  161.8 54.9 %collective-permute-start.44 = (bf16[768,768]{1,0:T(8,128)(2,1)}, bf16[768,768]{1,0:T(8,128)(2,1)S(1)}, u32[]{:S(2)}, u32[]{:S(2)}) collective-permute-start(bf16[768,768]{1,0:T(8,128)(2,1)} %get-tuple-element.154), channel_id=1, source_target_pairs={{0,16},{4,20},{8,24},{12,28},{16,0},{20,4},{24,8},{28,12},{1,17},{... | collective-permute-start | bytes 3538952 | tf_op jit(solution)/shard_map/ppermute | solution.py:504
  172.5 70.2 %collective-permute-start.47 = (bf16[800,384]{1,0:T(8,128)(2,1)}, bf16[800,384]{1,0:T(8,128)(2,1)S(1)}, u32[]{:S(2)}, u32[]{:S(2)}) collective-permute-start(bf16[800,384]{1,0:T(8,128)(2,1)} %get-tuple-element.164), channel_id=1, source_target_pairs={{0,4},{4,0},{8,12},{12,8},{16,20},{20,16},{24,28},{28,24},{1,5},{5... | collective-permute-start | bytes 1843208 | tf_op jit(solution)/shard_map/ppermute | solution.py:504
  173.0 19.2 %collective-permute-start.31 = (bf16[256,192]{1,0:T(8,128)(2,1)}, bf16[256,192]{1,0:T(8,128)(2,1)S(1)}, u32[]{:S(2)}, u32[]{:S(2)}) collective-permute-start(bf16[256,192]{1,0:T(8,128)(2,1)} %get-tuple-element.132), channel_id=1, source_target_pairs={{0,8},{4,12},{8,0},{12,4},{16,24},{20,28},{24,16},{28,20},{1,9},{5... | collective-permute-start | bytes 294920 | tf_op jit(solution)/shard_map/ppermute | solution.py:504
  174.9 18.4 %collective-permute-start.32 = (bf16[256,192]{1,0:T(8,128)(2,1)}, bf16[256,192]{1,0:T(8,128)(2,1)S(1)}, u32[]{:S(2)}, u32[]{:S(2)}) collective-permute-start(bf16[256,192]{1,0:T(8,128)(2,1)} %get-tuple-element.133), channel_id=1, source_target_pairs={{0,12},{4,8},{8,4},{12,0},{16,28},{20,24},{24,20},{28,16},{1,13},{... | collective-permute-start | bytes 294920 | tf_op jit(solution)/shard_map/ppermute | solution.py:504
  211.9 15.4 %collective-permute-start.36 = (bf16[192,640]{1,0:T(8,128)(2,1)}, bf16[192,640]{1,0:T(8,128)(2,1)S(1)}, u32[]{:S(2)}, u32[]{:S(2)}) collective-permute-start(bf16[192,640]{1,0:T(8,128)(2,1)} %get-tuple-element.142), channel_id=1, source_target_pairs={{0,3},{1,0},{2,1},{3,2},{4,7},{5,4},{6,5},{7,6},{8,11},{9,8},{10,9... | collective-permute-start | bytes 737288 | tf_op jit(solution)/shard_map/ppermute | solution.py:508
  211.9 9.9 %collective-permute-start.27 = (bf16[128,768]{1,0:T(8,128)(2,1)}, bf16[128,768]{1,0:T(8,128)(2,1)}, u32[]{:S(2)}, u32[]{:S(2)}) collective-permute-start(bf16[128,768]{1,0:T(8,128)(2,1)} %get-tuple-element.119), channel_id=1, source_target_pairs={{0,16},{4,20},{8,24},{12,28},{16,0},{20,4},{24,8},{28,12},{1,17},{... | collective-permute-start | bytes 589832 | tf_op jit(solution)/shard_map/ppermute | solution.py:504
  212.7 25.8 %collective-permute-start.37 = (bf16[192,640]{1,0:T(8,128)(2,1)}, bf16[192,640]{1,0:T(8,128)(2,1)S(1)}, u32[]{:S(2)}, u32[]{:S(2)}) collective-permute-start(bf16[192,640]{1,0:T(8,128)(2,1)} %get-tuple-element.143), channel_id=1, source_target_pairs={{0,2},{1,3},{2,0},{3,1},{4,6},{5,7},{6,4},{7,5},{8,10},{9,11},{10,... | collective-permute-start | bytes 737288 | tf_op jit(solution)/shard_map/ppermute | solution.py:508
  216.6 23.3 %collective-permute-start.38 = (bf16[192,640]{1,0:T(8,128)(2,1)}, bf16[192,640]{1,0:T(8,128)(2,1)}, u32[]{:S(2)}, u32[]{:S(2)}) collective-permute-start(bf16[192,640]{1,0:T(8,128)(2,1)} %get-tuple-element.144), channel_id=1, source_target_pairs={{0,1},{1,2},{2,3},{3,0},{4,5},{5,6},{6,7},{7,4},{8,9},{9,10},{10,1... | collective-permute-start | bytes 737288 | tf_op jit(solution)/shard_map/ppermute | solution.py:508
  221.8 22.3 %collective-permute-start.60 = (bf16[192,768]{1,0:T(8,128)(2,1)}, bf16[192,768]{1,0:T(8,128)(2,1)S(1)}, u32[]{:S(2)}, u32[]{:S(2)}) collective-permute-start(bf16[192,768]{1,0:T(8,128)(2,1)} %get-tuple-element.174), channel_id=1, source_target_pairs={{0,16},{4,20},{8,24},{12,28},{16,0},{20,4},{24,8},{28,12},{1,17},{... | collective-permute-start | bytes 884744 | tf_op jit(solution)/shard_map/ppermute | solution.py:504
  227.3 39.1 %collective-permute-start.33 = (bf16[512,768]{1,0:T(8,128)(2,1)}, bf16[512,768]{1,0:T(8,128)(2,1)S(1)}, u32[]{:S(2)}, u32[]{:S(2)}) collective-permute-start(bf16[512,768]{1,0:T(8,128)(2,1)} %get-tuple-element.137), channel_id=1, source_target_pairs={{0,4},{4,0},{8,12},{12,8},{16,20},{20,16},{24,28},{28,24},{1,5},{5... | collective-permute-start | bytes 2359304 | tf_op jit(solution)/shard_map/ppermute | solution.py:504
  238.6 9.9 %collective-permute-start.61 = (bf16[384,384]{1,0:T(8,128)(2,1)S(1)}, bf16[384,384]{1,0:T(8,128)(2,1)S(1)}, u32[]{:S(2)}, u32[]{:S(2)}) collective-permute-start(bf16[384,384]{1,0:T(8,128)(2,1)S(1)} %copy-done.75), channel_id=1, source_target_pairs={{0,8},{4,12},{8,0},{12,4},{16,24},{20,28},{24,16},{28,20},{1,9},{5... | collective-permute-start | bytes 884744 | tf_op jit(solution)/shard_map/ppermute | solution.py:504
  239.9 13.9 %collective-permute-start.45 = (bf16[192,768]{1,0:T(8,128)(2,1)}, bf16[192,768]{1,0:T(8,128)(2,1)S(1)}, u32[]{:S(2)}, u32[]{:S(2)}) collective-permute-start(bf16[192,768]{1,0:T(8,128)(2,1)} %get-tuple-element.156), channel_id=1, source_target_pairs={{0,16},{4,20},{8,24},{12,28},{16,0},{20,4},{24,8},{28,12},{1,17},{... | collective-permute-start | bytes 884744 | tf_op jit(solution)/shard_map/ppermute | solution.py:504
  242.6 11.2 %collective-permute-start.39 = (bf16[192,640]{1,0:T(8,128)(2,1)}, bf16[192,640]{1,0:T(8,128)(2,1)S(1)}, u32[]{:S(2)}, u32[]{:S(2)}) collective-permute-start(bf16[192,640]{1,0:T(8,128)(2,1)} %shard_map.317.mine), channel_id=1, source_target_pairs={{0,16},{4,20},{8,24},{12,28},{16,0},{20,4},{24,8},{28,12},{1,17},{... | collective-permute-start | bytes 737288 | tf_op jit(solution)/shard_map/ppermute | solution.py:504
  244.1 12.3 %collective-permute-start.46 = (bf16[384,384]{1,0:T(8,128)(2,1)}, bf16[384,384]{1,0:T(8,128)(2,1)S(1)}, u32[]{:S(2)}, u32[]{:S(2)}) collective-permute-start(bf16[384,384]{1,0:T(8,128)(2,1)} %get-tuple-element.158), channel_id=1, source_target_pairs={{0,8},{4,12},{8,0},{12,4},{16,24},{20,28},{24,16},{28,20},{1,9},{5... | collective-permute-start | bytes 884744 | tf_op jit(solution)/shard_map/ppermute | solution.py:504
  248.4 14.7 %collective-permute-start.48 = (bf16[416,384]{1,0:T(8,128)(2,1)}, bf16[416,384]{1,0:T(8,128)(2,1)S(1)}, u32[]{:S(2)}, u32[]{:S(2)}) collective-permute-start(bf16[416,384]{1,0:T(8,128)(2,1)} %get-tuple-element.166), channel_id=1, source_target_pairs={{0,8},{4,12},{8,0},{12,4},{16,24},{20,28},{24,16},{28,20},{1,9},{5... | collective-permute-start | bytes 958472 | tf_op jit(solution)/shard_map/ppermute | solution.py:504
  253.8 6.3 %collective-permute-start.62 = (bf16[96,768]{1,0:T(8,128)(2,1)}, bf16[96,768]{1,0:T(8,128)(2,1)S(1)}, u32[]{:S(2)}, u32[]{:S(2)}) collective-permute-start(bf16[96,768]{1,0:T(8,128)(2,1)} %get-tuple-element.178), channel_id=1, source_target_pairs={{0,3},{1,0},{2,1},{3,2},{4,7},{5,4},{6,5},{7,6},{8,11},{9,8},{10,9... | collective-permute-start | bytes 442376 | tf_op jit(solution)/shard_map/ppermute | solution.py:508
  253.9 9.3 %collective-permute-start.63 = (bf16[96,768]{1,0:T(8,128)(2,1)}, bf16[96,768]{1,0:T(8,128)(2,1)S(1)}, u32[]{:S(2)}, u32[]{:S(2)}) collective-permute-start(bf16[96,768]{1,0:T(8,128)(2,1)} %get-tuple-element.179), channel_id=1, source_target_pairs={{0,2},{1,3},{2,0},{3,1},{4,6},{5,7},{6,4},{7,5},{8,10},{9,11},{10,... | collective-permute-start | bytes 442376 | tf_op jit(solution)/shard_map/ppermute | solution.py:508
  256.4 19.4 %collective-permute-start.40 = (bf16[192,640]{1,0:T(8,128)(2,1)}, bf16[192,640]{1,0:T(8,128)(2,1)S(1)}, u32[]{:S(2)}, u32[]{:S(2)}) collective-permute-start(bf16[192,640]{1,0:T(8,128)(2,1)} %shard_map.318.s0), channel_id=1, source_target_pairs={{0,4},{4,0},{8,12},{12,8},{16,20},{20,16},{24,28},{28,24},{1,5},{5... | collective-permute-start | bytes 737288 | tf_op jit(solution)/shard_map/ppermute | solution.py:504
  260.1 16.4 %collective-permute-start.41 = (bf16[192,640]{1,0:T(8,128)(2,1)}, bf16[192,640]{1,0:T(8,128)(2,1)S(1)}, u32[]{:S(2)}, u32[]{:S(2)}) collective-permute-start(bf16[192,640]{1,0:T(8,128)(2,1)} %shard_map.318.s0), channel_id=1, source_target_pairs={{0,8},{4,12},{8,0},{12,4},{16,24},{20,28},{24,16},{28,20},{1,9},{5... | collective-permute-start | bytes 737288 | tf_op jit(solution)/shard_map/ppermute | solution.py:504
  263.1 14.0 %collective-permute-start.42 = (bf16[192,640]{1,0:T(8,128)(2,1)}, bf16[192,640]{1,0:T(8,128)(2,1)S(1)}, u32[]{:S(2)}, u32[]{:S(2)}) collective-permute-start(bf16[192,640]{1,0:T(8,128)(2,1)} %shard_map.318.s0), channel_id=1, source_target_pairs={{0,12},{4,8},{8,4},{12,0},{16,28},{20,24},{24,20},{28,16},{1,13},{... | collective-permute-start | bytes 737288 | tf_op jit(solution)/shard_map/ppermute | solution.py:504
  263.2 8.7 %collective-permute-start.64 = (bf16[96,768]{1,0:T(8,128)(2,1)}, bf16[96,768]{1,0:T(8,128)(2,1)S(1)}, u32[]{:S(2)}, u32[]{:S(2)}) collective-permute-start(bf16[96,768]{1,0:T(8,128)(2,1)} %get-tuple-element.180), channel_id=1, source_target_pairs={{0,1},{1,2},{2,3},{3,0},{4,5},{5,6},{6,7},{7,4},{8,9},{9,10},{10,1... | collective-permute-start | bytes 442376 | tf_op jit(solution)/shard_map/ppermute | solution.py:508
  266.4 23.5 %collective-permute-start.49 = (bf16[224,384]{1,0:T(8,128)(2,1)}, bf16[224,384]{1,0:T(8,128)(2,1)S(1)}, u32[]{:S(2)}, u32[]{:S(2)}) collective-permute-start(bf16[224,384]{1,0:T(8,128)(2,1)} %get-tuple-element.168), channel_id=1, source_target_pairs={{0,16},{4,20},{8,24},{12,28},{16,0},{20,4},{24,8},{28,12},{1,17},{... | collective-permute-start | bytes 516104 | tf_op jit(solution)/shard_map/ppermute | solution.py:504
  272.5 29.7 %collective-permute-start.34 = (bf16[256,768]{1,0:T(8,128)(2,1)}, bf16[256,768]{1,0:T(8,128)(2,1)S(1)}, u32[]{:S(2)}, u32[]{:S(2)}) collective-permute-start(bf16[256,768]{1,0:T(8,128)(2,1)} %get-tuple-element.140), channel_id=1, source_target_pairs={{0,8},{4,12},{8,0},{12,4},{16,24},{20,28},{24,16},{28,20},{1,9},{5... | collective-permute-start | bytes 1179656 | tf_op jit(solution)/shard_map/ppermute | solution.py:504
  275.8 12.1 %collective-permute-start.65 = (bf16[96,768]{1,0:T(8,128)(2,1)}, bf16[96,768]{1,0:T(8,128)(2,1)S(1)}, u32[]{:S(2)}, u32[]{:S(2)}) collective-permute-start(bf16[96,768]{1,0:T(8,128)(2,1)} %shard_map.328.refs_0_), channel_id=1, source_target_pairs={{0,8},{4,12},{8,0},{12,4},{16,24},{20,28},{24,16},{28,20},{1,9},{5... | collective-permute-start | bytes 442376 | tf_op jit(solution)/shard_map/ppermute | solution.py:504
  276.5 11.4 %collective-permute-start.66 = (bf16[96,768]{1,0:T(8,128)(2,1)}, bf16[96,768]{1,0:T(8,128)(2,1)S(1)}, u32[]{:S(2)}, u32[]{:S(2)}) collective-permute-start(bf16[96,768]{1,0:T(8,128)(2,1)} %shard_map.328.refs_0_), channel_id=1, source_target_pairs={{0,16},{4,20},{8,24},{12,28},{16,0},{20,4},{24,8},{28,12},{1,17},{... | collective-permute-start | bytes 442376 | tf_op jit(solution)/shard_map/ppermute | solution.py:504
  277.1 12.7 %collective-permute-start.67 = (bf16[96,768]{1,0:T(8,128)(2,1)}, bf16[96,768]{1,0:T(8,128)(2,1)S(1)}, u32[]{:S(2)}, u32[]{:S(2)}) collective-permute-start(bf16[96,768]{1,0:T(8,128)(2,1)} %shard_map.328.refs_0_), channel_id=1, source_target_pairs={{0,24},{4,28},{8,16},{12,20},{16,8},{20,12},{24,0},{28,4},{1,25},{... | collective-permute-start | bytes 442376 | tf_op jit(solution)/shard_map/ppermute | solution.py:504
  287.9 6.1 %collective-permute-start.68 = (bf16[96,768]{1,0:T(8,128)(2,1)S(1)}, bf16[96,768]{1,0:T(8,128)(2,1)S(1)}, u32[]{:S(2)}, u32[]{:S(2)}) collective-permute-start(bf16[96,768]{1,0:T(8,128)(2,1)S(1)} %copy-done.18), channel_id=1, source_target_pairs={{0,4},{4,0},{8,12},{12,8},{16,20},{20,16},{24,28},{28,24},{1,5},{5... | collective-permute-start | bytes 442376 | tf_op jit(solution)/shard_map/ppermute | solution.py:504
  287.9 9.0 %collective-permute-start.69 = (bf16[96,768]{1,0:T(8,128)(2,1)S(1)}, bf16[96,768]{1,0:T(8,128)(2,1)S(1)}, u32[]{:S(2)}, u32[]{:S(2)}) collective-permute-start(bf16[96,768]{1,0:T(8,128)(2,1)S(1)} %collective-permute-done.65.refs_1_), channel_id=1, source_target_pairs={{0,4},{4,0},{8,12},{12,8},{16,20},{20,16},{24,28},{28,24},{1,5},{5... | collective-permute-start | bytes 442376 | tf_op jit(solution)/shard_map/ppermute | solution.py:504
  289.9 7.1 %collective-permute-start.70 = (bf16[96,768]{1,0:T(8,128)(2,1)S(1)}, bf16[96,768]{1,0:T(8,128)(2,1)S(1)}, u32[]{:S(2)}, u32[]{:S(2)}) collective-permute-start(bf16[96,768]{1,0:T(8,128)(2,1)S(1)} %collective-permute-done.66.refs_2_), channel_id=1, source_target_pairs={{0,4},{4,0},{8,12},{12,8},{16,20},{20,16},{24,28},{28,24},{1,5},{5... | collective-permute-start | bytes 442376 | tf_op jit(solution)/shard_map/ppermute | solution.py:504
  289.9 9.3 %collective-permute-start.71 = (bf16[96,768]{1,0:T(8,128)(2,1)S(1)}, bf16[96,768]{1,0:T(8,128)(2,1)}, u32[]{:S(2)}, u32[]{:S(2)}) collective-permute-start(bf16[96,768]{1,0:T(8,128)(2,1)S(1)} %collective-permute-done.67.refs_3_), channel_id=1, source_target_pairs={{0,4},{4,0},{8,12},{12,8},{16,20},{20,16},{24,28},{28,24},{1,5},{5... | collective-permute-start | bytes 442376 | tf_op jit(solution)/shard_map/ppermute | solution.py:504
  294.1 9.5 %collective-permute-start.50 = (bf16[144,768]{1,0:T(8,128)(2,1)}, bf16[144,768]{1,0:T(8,128)(2,1)S(1)}, u32[]{:S(2)}, u32[]{:S(2)}) collective-permute-start(bf16[144,768]{1,0:T(8,128)(2,1)} %get-tuple-element.170), channel_id=1, source_target_pairs={{0,3},{1,0},{2,1},{3,2},{4,7},{5,4},{6,5},{7,6},{8,11},{9,8},{10,9... | collective-permute-start | bytes 663560 | tf_op jit(solution)/shard_map/ppermute | solution.py:508
  297.0 19.7 %collective-permute-start.51 = (bf16[144,768]{1,0:T(8,128)(2,1)}, bf16[144,768]{1,0:T(8,128)(2,1)S(1)}, u32[]{:S(2)}, u32[]{:S(2)}) collective-permute-start(bf16[144,768]{1,0:T(8,128)(2,1)} %get-tuple-element.171), channel_id=1, source_target_pairs={{0,2},{1,3},{2,0},{3,1},{4,6},{5,7},{6,4},{7,5},{8,10},{9,11},{10,... | collective-permute-start | bytes 663560 | tf_op jit(solution)/shard_map/ppermute | solution.py:508
  297.7 19.0 %collective-permute-start.52 = (bf16[144,768]{1,0:T(8,128)(2,1)}, bf16[144,768]{1,0:T(8,128)(2,1)S(1)}, u32[]{:S(2)}, u32[]{:S(2)}) collective-permute-start(bf16[144,768]{1,0:T(8,128)(2,1)} %get-tuple-element.172), channel_id=1, source_target_pairs={{0,1},{1,2},{2,3},{3,0},{4,5},{5,6},{6,7},{7,4},{8,9},{9,10},{10,1... | collective-permute-start | bytes 663560 | tf_op jit(solution)/shard_map/ppermute | solution.py:508
  302.3 30.5 %collective-permute-start.35 = (bf16[128,768]{1,0:T(8,128)(2,1)S(1)}, bf16[128,768]{1,0:T(8,128)(2,1)S(1)}, u32[]{:S(2)}, u32[]{:S(2)}) collective-permute-start(bf16[128,768]{1,0:T(8,128)(2,1)S(1)} %slice.69), channel_id=1, source_target_pairs={{0,16},{4,20},{8,24},{12,28},{16,0},{20,4},{24,8},{28,12},{1,17},{... | collective-permute-start | bytes 589832 | tf_op jit(solution)/shard_map/ppermute | solution.py:504
  319.4 8.5 %collective-permute-start.53 = (bf16[144,768]{1,0:T(8,128)(2,1)}, bf16[144,768]{1,0:T(8,128)(2,1)S(1)}, u32[]{:S(2)}, u32[]{:S(2)}) collective-permute-start(bf16[144,768]{1,0:T(8,128)(2,1)} %shard_map.326.refs_0_), channel_id=1, source_target_pairs={{0,8},{4,12},{8,0},{12,4},{16,24},{20,28},{24,16},{28,20},{1,9},{5... | collective-permute-start | bytes 663560 | tf_op jit(solution)/shard_map/ppermute | solution.py:504
  320.8 11.5 %collective-permute-start.54 = (bf16[144,768]{1,0:T(8,128)(2,1)}, bf16[144,768]{1,0:T(8,128)(2,1)S(1)}, u32[]{:S(2)}, u32[]{:S(2)}) collective-permute-start(bf16[144,768]{1,0:T(8,128)(2,1)} %shard_map.326.refs_0_), channel_id=1, source_target_pairs={{0,16},{4,20},{8,24},{12,28},{16,0},{20,4},{24,8},{28,12},{1,17},{... | collective-permute-start | bytes 663560 | tf_op jit(solution)/shard_map/ppermute | solution.py:504
  321.9 10.4 %collective-permute-start.55 = (bf16[144,768]{1,0:T(8,128)(2,1)}, bf16[144,768]{1,0:T(8,128)(2,1)S(1)}, u32[]{:S(2)}, u32[]{:S(2)}) collective-permute-start(bf16[144,768]{1,0:T(8,128)(2,1)} %shard_map.326.refs_0_), channel_id=1, source_target_pairs={{0,24},{4,28},{8,16},{12,20},{16,8},{20,12},{24,0},{28,4},{1,25},{... | collective-permute-start | bytes 663560 | tf_op jit(solution)/shard_map/ppermute | solution.py:504
  323.0 10.8 %collective-permute-start.56 = (bf16[144,768]{1,0:T(8,128)(2,1)}, bf16[144,768]{1,0:T(8,128)(2,1)S(1)}, u32[]{:S(2)}, u32[]{:S(2)}) collective-permute-start(bf16[144,768]{1,0:T(8,128)(2,1)} %shard_map.326.refs_0_), channel_id=1, source_target_pairs={{0,4},{4,0},{8,12},{12,8},{16,20},{20,16},{24,28},{28,24},{1,5},{5... | collective-permute-start | bytes 663560 | tf_op jit(solution)/shard_map/ppermute | solution.py:504
  (86 other events, 922.8 us)

commit v4 on v3

--- a/solution.py
+++ b/solution.py
@@ -877,24 +877,43 @@
     sums[2:, :] = jnp.zeros_like(sums[2:, :])
 
 
-def weights_kernel(first0, first1, douter0, douter1, dinner, active, ak, az, bk, bz, left, right):
+def weights_kernel(
+    first0, first1, dinner, douter0, douter1, active, ak, az, bk, bz, left, right, held, grads, sems
+):
     _, quarter, _, _ = where_am_i()
     x, y = quarter & 1, quarter >> 1
     count = first0.shape[0]
     part, step = first0.shape[1] // 16, active.shape[1] // 16
+    loads = [
+        pltpu.make_async_copy(source, target, sems.at[index])
+        for index, (source, target) in enumerate(
+            ((active, held), (douter0, grads.at[:count, :]), (douter1, grads.at[count:, :]))
+        )
+    ]
+    for copy in loads:
+        copy.start()
     left[...] = short(dot_sum(first0[...], dinner[:count]) + dot_sum(first1[...], dinner[count:]))
+    stores = []
     for block in range(8):
         rows = slice(block * part, (block + 1) * part)
-        ak[rows, :] = left[some_rows((2 * block + x) * part, part), :]
-        az[rows, :] = left[some_rows((2 * block + 1 - x) * part, part), :]
-    right[...] = short(
-        dot_sum(active[:count], douter0[...]) + dot_sum(active[count:], douter1[...])
-    )
+        for ref, side in ((ak, x), (az, 1 - x)):
+            take = some_rows((2 * block + side) * part, part)
+            at = 3 + len(stores)
+            stores.append(pltpu.make_async_copy(left.at[take, :], ref.at[rows, :], sems.at[at]))
+            stores[-1].start()
+    for copy in loads:
+        copy.wait()
+    right[...] = short(dot_sum(held[...], grads[...]))
     for block in range(8):
         row, side = block // 2, block % 2
         rows = slice(block * step, (block + 1) * step)
-        bk[rows, :] = right[some_rows((4 * row + 2 * y + side) * step, step), :]
-        bz[rows, :] = right[some_rows((4 * row + 2 * (1 - y) + side) * step, step), :]
+        for ref, place in ((bk, y), (bz, 1 - y)):
+            take = some_rows((4 * row + 2 * place + side) * step, step)
+            at = 3 + len(stores)
+            stores.append(pltpu.make_async_copy(right.at[take, :], ref.at[rows, :], sems.at[at]))
+            stores[-1].start()
+    for copy in stores:
+        copy.wait()
 
 
 def branch_kernel(first_sum, dsecond, keep, got, vec, out_full, dfirst_sum, dbranch, d0, d1, d2, d3, sums):
@@ -1072,8 +1091,8 @@
 
 
 def attend_back_kernel(
-    bounds, qkv, logsum0, logsum1, seg_col, seg_row, p0, p1, p2, p3, mine, other, far,
-    h0, h1, h2, h3, grads, dqueries, dkeys, dvalues, dweight, dmixed, logsum, whole,
+    bounds, qkv, logsum0, logsum1, seg_col, seg_row, p0, p1, p2, p3, mine_in, other_in, far_in,
+    h0, h1, h2, h3, grads, dqueries, dkeys, dvalues, dweight, dmixed, logsum, whole, tokens, sems,
 ):
     _, quarter, _, own = where_am_i()
     ctx = lax.axis_index("ctx")
@@ -1082,6 +1101,12 @@
     group = qkv.shape[0] // 3
     width = group * HEAD_DIM
     block = p0.shape[0]
+    loads = [
+        pltpu.make_async_copy(source, tokens.at[at : at + source.shape[0], :], sems.at[index])
+        for index, (source, at) in enumerate(((mine_in, 0), (other_in, block), (far_in, 2 * block)))
+    ]
+    for copy in loads:
+        copy.start()
     dkeys[...] = jnp.zeros_like(dkeys)
     dvalues[...] = jnp.zeros_like(dvalues)
     for index, part in enumerate((p0, p2, p1, p3)):
@@ -1134,12 +1159,9 @@
         grads[index * CHUNK : (index + 1) * CHUNK, :] = whole[
             some_chunks(chunk_of(ctx, index), 1), :
         ]
-    rows = 2 * block
-    dweight[...] = (
-        dot_sum(mine[...], grads[:block])
-        + dot_sum(other[...], grads[block:rows])
-        + dot_sum(far[...], grads[rows:])
-    )
+    for copy in loads:
+        copy.wait()
+    dweight[...] = dot_sum(tokens[...], grads[...])
     sums = jnp.sum(wide(grads[...]), axis=0, keepdims=True)
     lines = sums.shape[1] // HEAD_DIM
     for index, out in enumerate((h0, h1, h2, h3)):
@@ -1348,8 +1370,16 @@
     ak, az, bk, bz = run(
         weights_kernel,
         [((dim // 2, 4 * half), BF)] * 2 + [((2 * half, dim), BF)] * 2,
-        (first_low, first_far, douter, douter_far, dinner, active),
-        [pltpu.VMEM((dim, 4 * half), BF), pltpu.VMEM((4 * half, dim), BF)],
+        (first_low, first_far, dinner, douter, douter_far, active),
+        [
+            pltpu.VMEM((dim, 4 * half), BF),
+            pltpu.VMEM((4 * half, dim), BF),
+            pltpu.VMEM((2 * count, 4 * half), BF),
+            pltpu.VMEM((2 * count, dim), BF),
+            pltpu.SemaphoreType.DMA((35,)),
+        ],
+        specs=[WHOLE] * 3 + [LEFT] * 3,
+        out_specs=[LEFT] * 4,
     )
     ar, br = flip(az, 2), flip(bz, 4)
     ck, cz = run(
@@ -1375,8 +1405,11 @@
             pltpu.VMEM((3, total, HEAD_DIM), BF),
             pltpu.VMEM((total, 128), F32),
             pltpu.VMEM((total, 3 * shard), BF),
+            pltpu.VMEM((total, dim), BF),
+            pltpu.SemaphoreType.DMA((3,)),
         ],
         scalars=(bounds,),
+        specs=[WHOLE] * 9 + [LEFT] * 3,
     )
     keep, send = run(
         tokens_kernel, [((2 * count, dim), F32), ((2 * count, dim), BF)], (grads, heads_weight)

time: 343 us -> 342 us (level)
  no operation moved by 1% of the time
where the time goes in v4:
time: 342 us; the launch traced here: 340 us
  waiting for transfers between devices  123 us (36%)
  Pallas kernels  118 us (35%)
  starting transfers between devices  75.1 us (22%)
  local copies, waits for them, and re-layouts  17.6 us (5%)
  other arithmetic  5.59 us (2%)
    pallas_call x26, Pallas kernels, run(): pl.pallas_call(kernel, out_shape=shapes, in_specs=in_specs, out_specs=tup...  118 us
    ppermute x57, waiting for transfers between devices, flip(): return lax.ppermute(value, 'ctx', [(i, i ^ bits) for i in range(8)])  76.1 us
    ppermute x15, waiting for transfers between devices, turn(): return lax.ppermute(value, 'wt', [(i, (i - step) % 4) for i in range(4)])  46.6 us
    ppermute x57, starting transfers between devices, flip(): return lax.ppermute(value, 'ctx', [(i, i ^ bits) for i in range(8)])  46.3 us
    ppermute x15, starting transfers between devices, turn(): return lax.ppermute(value, 'wt', [(i, (i - step) % 4) for i in range(4)])  28.8 us
    unnamed x156, local copies, waits for them, and re-layouts  9.57 us
  transfers between devices with their start and end apart: 72, of which 30 were waited for; matrix products, arithmetic and copies ran while one was open for 3% of the time, Pallas kernels for 24%

profile of v4, /device:TPU:0, one launch (start us, length us, event | category | flops | bytes accessed | tf_op | source)
XLA Modules:
  0.0 340.4 jit_solution(16698207677434696578)
XLA Ops:
  1.8 3.1 collective-permute-start
  5.9 3.9 %collective-permute-done = bf16[128,768]{1,0:T(8,128)(2,1)S(1)} collective-permute-done((bf16[128,768]{1,0:T(8,128)(2,1)S(1)}, bf16[128,768]{1,0:T(8,128)(2,1)S(1)}, u32[]{:S(2)}, u32[]{:S(2)}) %collective-permute-start) | collective-permute-done | bytes 196640 | tf_op jit(solution)/shard_map/ppermute | solution.py:504
  9.8 1.8 collective-permute-start.1
  12.4 2.0 shard_map.305
  14.4 3.6 %collective-permute-start.3 = (bf16[112,576]{1,0:T(8,128)(2,1)}, bf16[112,576]{1,0:T(8,128)(2,1)S(1)}, u32[]{:S(2)}, u32[]{:S(2)}) collective-permute-start(bf16[112,576]{1,0:T(8,128)(2,1)} %get-tuple-element.103), channel_id=1, source_target_pairs={{0,3},{1,0},{2,1},{3,2},{4,7},{5,4},{6,5},{7,6},{8,11},{9,8},{10,9... | collective-permute-start | bytes 387080 | tf_op jit(solution)/shard_map/ppermute | solution.py:508
  18.0 3.0 shard_map.308
  21.7 2.2 collective-permute-start.16
  24.0 2.0 collective-permute-start.5
  26.0 2.0 collective-permute-done.4.g2
  28.0 1.5 collective-permute-start.6
  30.9 12.3 %collective-permute-done.5.g3 = bf16[112,576]{1,0:T(8,128)(2,1)S(1)} collective-permute-done((bf16[112,576]{1,0:T(8,128)(2,1)S(1)}, bf16[112,576]{1,0:T(8,128)(2,1)S(1)}, u32[]{:S(2)}, u32[]{:S(2)}) %collective-permute-start.5) | collective-permute-done | bytes 129056 | tf_op jit(solution)/shard_map/ppermute | solution.py:508
  43.3 10.5 %collective-permute-start.20 = (bf16[240,768]{1,0:T(8,128)(2,1)S(1)}, bf16[240,768]{1,0:T(8,128)(2,1)S(1)}, u32[]{:S(2)}, u32[]{:S(2)}) collective-permute-start(bf16[240,768]{1,0:T(8,128)(2,1)S(1)} %copy-done.74), channel_id=1, source_target_pairs={{0,1},{1,2},{2,3},{3,0},{4,5},{5,6},{6,7},{7,4},{8,9},{9,10},{10,1... | collective-permute-start | bytes 1105928 | tf_op jit(solution)/shard_map/ppermute | solution.py:508
  53.8 1.5 collective-permute-start.8
  56.0 3.8 %collective-permute-done.8.h3 = bf16[112,576]{1,0:T(8,128)(2,1)} collective-permute-done((bf16[112,576]{1,0:T(8,128)(2,1)S(1)}, bf16[112,576]{1,0:T(8,128)(2,1)}, u32[]{:S(2)}, u32[]{:S(2)}) %collective-permute-start.8) | collective-permute-done | bytes 129056 | tf_op jit(solution)/shard_map/ppermute | solution.py:504
  59.8 1.5 collective-permute-start.14
  64.8 2.1 collective-permute-done.13.refs_1_
  67.5 11.7 %collective-permute-done.14.refs_2_ = bf16[240,768]{1,0:T(8,128)(2,1)S(1)} collective-permute-done((bf16[240,768]{1,0:T(8,128)(2,1)S(1)}, bf16[240,768]{1,0:T(8,128)(2,1)S(1)}, u32[]{:S(2)}, u32[]{:S(2)}) %collective-permute-start.14) | collective-permute-done | bytes 368672 | tf_op jit(solution)/shard_map/ppermute | solution.py:504
  86.0 10.8 %shard_map.306 = (bf16[9,1024,64]{2,1,0:T(8,128)(2,1)}, bf16[256,192]{1,0:T(8,128)(2,1)}, bf16[256,192]{1,0:T(8,128)(2,1)}, f32[512,128]{1,0:T(8,128)}, bf16[768...) custom-call(bf16[256,768]{1,0:T(8,128)(2,1)} %copy-done, bf16[256,768]{1,0:T(8,128)(2,1)} %copy-done.1, ...), custom_call_target="tpu_custom_call" | custom-call | tf_op jit(solution)/shard_map/pallas_call | solution.py:569
  96.8 7.8 %shard_map.307 = (bf16[256,192]{1,0:T(8,128)(2,1)}, bf16[256,192]{1,0:T(8,128)(2,1)}, f32[512,128]{1,0:T(8,128)}) custom-call(bf16[9,1024,64]{2,1,0:T(8,128)(2,1)} %get-tuple-element.106.qkv, s32[1024,1]{1,0:T(8,128)} %copy.43.seg_col, s32[1,1024]{1,0:T(1,128)} %bitcast.52), custom_call_target="tpu_custom_call" | custom-call | tf_op jit(solution)/shard_map/pallas_call | solution.py:569
  106.7 2.5 collective-permute-done.22.refs_10_
  110.3 1.8 collective-permute-done.11.m3
  112.8 4.7 %shard_map.309 = (f32[256,768]{1,0:T(8,128)}, bf16[256,768]{1,0:T(8,128)(2,1)}, bf16[768,768]{1,0:T(8,128)(2,1)}) custom-call(bf16[256,192]{1,0:T(8,128)(2,1)} %get-tuple-element.104.m0, bf16[256,192]{1,0:T(8,128)(2,1)} %copy-done.21, bf16[256,192]{1,0:T(8,128)(2,1)} %copy-done.19, bf16[256,192]{1,0:T(8,128)(2,1)} %copy-done.20, bf16[256,768]{1,0:T(8,128)(2,1)} %copy-done, ...), custom_call_target="tpu_custom_call" | custom-call | tf_op jit(solution)/shard_map/pallas_call | solution.py:569
  117.9 1.6 collective-permute-done.24.far.first1
  120.2 9.1 %shard_map.310 = (f32[256,768]{1,0:T(8,128)}, f32[256,768]{1,0:T(8,128)}, bf16[512,1536]{1,0:T(8,128)(2,1)}, bf16[512,1536]{1,0:T(8,128)(2,1)}, bf16[768,1536]{1,0:T(8,128)(2,1)}, /*index=5*/bf16[1536,768]{1,0:T(8,128)(2,1)}) custom-call(bf16[256,768]{1,0:T(8,128)(2,1)} %get-tuple-element.112.near.first0, bf16[256,768]{1,0:T(8,128)(2,1)} %copy-done.3, ...), custom_call_target="tpu_custom_call" | custom-call | tf_op jit(solution)/shard_map/pallas_call | solution.py:569
  131.1 6.4 %collective-permute-done.26.cot1 = bf16[128,768]{1,0:T(8,128)(2,1)S(1)} collective-permute-done((bf16[128,768]{1,0:T(8,128)(2,1)S(1)}, bf16[128,768]{1,0:T(8,128)(2,1)S(1)}, u32[]{:S(2)}, u32[]{:S(2)}) %collective-permute-start.26) | collective-permute-done | bytes 196640 | tf_op jit(solution)/shard_map/ppermute | solution.py:504
  138.5 3.7 %shard_map.311 = (bf16[128,768]{1,0:T(8,128)(2,1)}, bf16[128,768]{1,0:T(8,128)(2,1)}, f32[256,768]{1,0:T(8,128)}, bf16[256,768]{1,0:T(8,128)(2,1)}, f32[8,768]{1,0:T(8,128)}) custom-call(f32[256,768]{1,0:T(8,128)} %get-tuple-element.111.first_sum, f32[256,768]{1,0:T(8,128)} %get-tuple-element.116.keep, f32[256,768]{1,0:T(8,128)} %copy-done.15, ...), custom_call_target="tpu_custom_call" | custom-call | tf_op jit(solution)/shard_map/pallas_call | solution.py:569
  142.3 1.9 collective-permute-done.28.far.douter1
  144.9 8.1 %shard_map.312 = (f32[256,768]{1,0:T(8,128)}, f32[256,768]{1,0:T(8,128)}, bf16[512,1536]{1,0:T(8,128)(2,1)}, f32[8,768]{1,0:T(8,128)}) custom-call(bf16[256,768]{1,0:T(8,128)(2,1)} %get-tuple-element.123.near.douter0, bf16[256,768]{1,0:T(8,128)(2,1)} %copy-done.4, bf16[512,1536]{1,0:T(8,128)(2,1)} %get-tuple-element.124.slope, ...), custom_call_target="tpu_custom_call" | custom-call | tf_op jit(solution)/shard_map/pallas_call | solution.py:569
  153.0 6.4 %shard_map.320 = (bf16[384,1536]{1,0:T(8,128)(2,1)}, bf16[384,1536]{1,0:T(8,128)(2,1)}, bf16[768,768]{1,0:T(8,128)(2,1)}, bf16[768,768]{1,0:T(8,128)(2,1)}) custom-call(bf16[256,768]{1,0:T(8,128)(2,1)} %get-tuple-element.112.near.first0, bf16[256,768]{1,0:T(8,128)(2,1)} %copy-done.3, bf16[512,1536]{1,0:T(8,128)(2,1)} %get-tuple-element.149.dinner, ...), custom_call_target="tpu_custom_call" | custom-call | tf_op jit(solution)/shard_map/pallas_call | solution.py:569
  161.7 1.7 collective-permute-done.29.got
  164.3 4.3 %shard_map.313 = (f32[256,768]{1,0:T(8,128)}, bf16[256,768]{1,0:T(8,128)(2,1)}, bf16[256,192]{1,0:T(8,128)(2,1)}, bf16[256,192]{1,0:T(8,128)(2,1)}, bf16[256,192...) custom-call(f32[256,768]{1,0:T(8,128)} %get-tuple-element.111.first_sum, ...), custom_call_target="tpu_custom_call" | custom-call | tf_op jit(solution)/shard_map/pallas_call | solution.py:569
  168.6 3.0 shard_map.322
  174.9 16.4 %collective-permute-done.31.p2 = bf16[256,192]{1,0:T(8,128)(2,1)S(1)} collective-permute-done((bf16[256,192]{1,0:T(8,128)(2,1)}, bf16[256,192]{1,0:T(8,128)(2,1)S(1)}, u32[]{:S(2)}, u32[]{:S(2)}) %collective-permute-start.31) | collective-permute-done | bytes 98336 | tf_op jit(solution)/shard_map/ppermute | solution.py:504
  193.2 17.5 %shard_map.314 = (f32[192,640]{1,0:T(8,128)}, bf16[192,640]{1,0:T(8,128)(2,1)}, bf16[192,640]{1,0:T(8,128)(2,1)}, bf16[192,640]{1,0:T(8,128)(2,1)}, bf16[1024,576]{1,0:T(8,128)(2,1)}) custom-call(s32[2,4]{1,0:T(2,128)} %pad_add_fusion.bounds, bf16[9,1024,64]{2,1,0:T(8,128)(2,1)} %get-tuple-element.106.qkv, f32[512,128]{1,0:T(8,128)} %get-tuple-element.120.logsum0, ...), custom_call_target="tpu_custom_call" | custom-call | tf_op jit(solution)/shard_map/pallas_call | solution.py:569
  211.6 3.9 %collective-permute-start.37 = (bf16[192,640]{1,0:T(8,128)(2,1)}, bf16[192,640]{1,0:T(8,128)(2,1)S(1)}, u32[]{:S(2)}, u32[]{:S(2)}) collective-permute-start(bf16[192,640]{1,0:T(8,128)(2,1)} %get-tuple-element.143), channel_id=1, source_target_pairs={{0,2},{1,3},{2,0},{3,1},{4,6},{5,7},{6,4},{7,5},{8,10},{9,11},{10,... | collective-permute-start | bytes 737288 | tf_op jit(solution)/shard_map/ppermute | solution.py:508
  216.5 4.1 %shard_map.321 = (bf16[192,768]{1,0:T(8,128)(2,1)}, bf16[192,768]{1,0:T(8,128)(2,1)}, bf16[384,384]{1,0:T(8,128)(2,1)}, bf16[384,384]{1,0:T(8,128)(2,1)}, bf16[1...) custom-call(bf16[384,1536]{1,0:T(8,128)(2,1)} %get-tuple-element.151.ak, ...), custom_call_target="tpu_custom_call" | custom-call | tf_op jit(solution)/shard_map/pallas_call | solution.py:569
  220.6 1.5 collective-permute-start.60
  222.1 4.0 %shard_map.315 = (f32[512,768]{1,0:T(8,128)}, bf16[512,768]{1,0:T(8,128)(2,1)}) custom-call(bf16[1024,576]{1,0:T(8,128)(2,1)} %get-tuple-element.134.grads, bf16[768,576]{1,0:T(8,128)(2,1)} %get-tuple-element.135.weight), custom_call_target="tpu_custom_call" | custom-call | tf_op jit(solution)/shard_map/pallas_call | solution.py:569
  226.1 11.2 %collective-permute-done.37.refs_1_ = bf16[192,640]{1,0:T(8,128)(2,1)S(1)} collective-permute-done((bf16[192,640]{1,0:T(8,128)(2,1)}, bf16[192,640]{1,0:T(8,128)(2,1)S(1)}, u32[]{:S(2)}, u32[]{:S(2)}) %collective-permute-start.37) | collective-permute-done | bytes 245792 | tf_op jit(solution)/shard_map/ppermute | solution.py:508
  239.4 2.1 shard_map.317.mine
  243.6 2.2 shard_map.323
  248.6 2.1 shard_map.327
  250.8 1.9 collective-permute-done.39.refs_0_
  253.4 1.8 shard_map.318.s0
  255.2 3.7 %collective-permute-done.62.refs_0_ = bf16[96,768]{1,0:T(8,128)(2,1)S(1)} collective-permute-done((bf16[96,768]{1,0:T(8,128)(2,1)}, bf16[96,768]{1,0:T(8,128)(2,1)S(1)}, u32[]{:S(2)}, u32[]{:S(2)}) %collective-permute-start.62) | collective-permute-done | bytes 147488 | tf_op jit(solution)/shard_map/ppermute | solution.py:508
  259.6 2.4 collective-permute-done.63.refs_1_
  263.3 1.9 shard_map.324
  266.1 3.0 shard_map.316
  269.1 1.6 collective-permute-done.64.refs_2_
  272.7 1.9 shard_map.328.refs_0_
  275.9 2.2 collective-permute-start.67
  278.2 1.8 maximum_select_fusion.1
  280.0 3.3 shard_map.319
  283.3 3.4 %collective-permute-done.65.refs_1_ = bf16[96,768]{1,0:T(8,128)(2,1)S(1)} collective-permute-done((bf16[96,768]{1,0:T(8,128)(2,1)}, bf16[96,768]{1,0:T(8,128)(2,1)S(1)}, u32[]{:S(2)}, u32[]{:S(2)}) %collective-permute-start.65) | collective-permute-done | bytes 147488 | tf_op jit(solution)/shard_map/ppermute | solution.py:504
  287.2 1.6 collective-permute-done.67.refs_3_
  290.6 2.4 shard_map.325
  293.0 2.8 collective-permute-start.50
  296.5 1.5 collective-permute-start.52
  298.1 2.9 shard_map.329
  302.4 13.1 %collective-permute-done.51.refs_1_ = bf16[144,768]{1,0:T(8,128)(2,1)S(1)} collective-permute-done((bf16[144,768]{1,0:T(8,128)(2,1)}, bf16[144,768]{1,0:T(8,128)(2,1)S(1)}, u32[]{:S(2)}, u32[]{:S(2)}) %collective-permute-start.51) | collective-permute-done | bytes 221216 | tf_op jit(solution)/shard_map/ppermute | solution.py:508
  316.2 2.0 shard_map.326.refs_0_
  321.9 4.9 %collective-permute-done.53.refs_1_ = bf16[144,768]{1,0:T(8,128)(2,1)S(1)} collective-permute-done((bf16[144,768]{1,0:T(8,128)(2,1)}, bf16[144,768]{1,0:T(8,128)(2,1)S(1)}, u32[]{:S(2)}, u32[]{:S(2)}) %collective-permute-start.53) | collective-permute-done | bytes 221216 | tf_op jit(solution)/shard_map/ppermute | solution.py:504
  326.8 4.3 %collective-permute-done.54.refs_2_ = bf16[144,768]{1,0:T(8,128)(2,1)S(1)} collective-permute-done((bf16[144,768]{1,0:T(8,128)(2,1)}, bf16[144,768]{1,0:T(8,128)(2,1)S(1)}, u32[]{:S(2)}, u32[]{:S(2)}) %collective-permute-start.54) | collective-permute-done | bytes 221216 | tf_op jit(solution)/shard_map/ppermute | solution.py:504
  333.6 4.0 %shard_map.330 = (f32[192,3072]{1,0:T(8,128)}, f32[768,768]{1,0:T(8,128)}, f32[192,768]{1,0:T(8,128)}, f32[16,768]{1,0:T(8,128)}) custom-call(bf16[144,768]{1,0:T(8,128)(2,1)} %shard_map.326.refs_0_, bf16[144,768]{1,0:T(8,128)(2,1)} %copy-done.34, bf16[144,768]{1,0:T(8,128)(2,1)} %copy-done.35, ...), custom_call_target="tpu_custom_call", output_to_operand_aliasing={{0}: (8, {}), {1}: (9, {})} | custom-call | tf_op jit(solution)/shard_map/pallas_call | solution.py:569
  (299 shorter events, 62.8 us)
Async XLA Ops:
  1.8 8.0 %collective-permute-start = (bf16[128,768]{1,0:T(8,128)(2,1)S(1)}, bf16[128,768]{1,0:T(8,128)(2,1)S(1)}, u32[]{:S(2)}, u32[]{:S(2)}) collective-permute-start(bf16[128,768]{1,0:T(8,128)(2,1)S(1)} %get-tuple-element.192), channel_id=1, source_target_pairs={{0,16},{4,20},{8,24},{12,28},{16,0},{20,4},{24,8},{28,12},{1,17},{... | collective-permute-start | bytes 589832 | tf_op jit(solution)/shard_map/ppermute | solution.py:504
  9.8 19.7 %collective-permute-start.1 = (bf16[256,768]{1,0:T(8,128)(2,1)S(1)}, bf16[256,768]{1,0:T(8,128)(2,1)S(1)}, u32[]{:S(2)}, u32[]{:S(2)}) collective-permute-start(bf16[256,768]{1,0:T(8,128)(2,1)S(1)} %pad_maximum_fusion.1.mine.mine_in), channel_id=1, source_target_pairs={{0,8},{4,12},{8,0},{12,4},{16,24},{20,28},{24,16},{28,20},{1,9},{5... | collective-permute-start | bytes 1179656 | tf_op jit(solution)/shard_map/ppermute | solution.py:504
  14.4 9.6 %collective-permute-start.3 = (bf16[112,576]{1,0:T(8,128)(2,1)}, bf16[112,576]{1,0:T(8,128)(2,1)S(1)}, u32[]{:S(2)}, u32[]{:S(2)}) collective-permute-start(bf16[112,576]{1,0:T(8,128)(2,1)} %get-tuple-element.103), channel_id=1, source_target_pairs={{0,3},{1,0},{2,1},{3,2},{4,7},{5,4},{6,5},{7,6},{8,11},{9,8},{10,9... | collective-permute-start | bytes 387080 | tf_op jit(solution)/shard_map/ppermute | solution.py:508
  18.0 10.0 %collective-permute-start.4 = (bf16[112,576]{1,0:T(8,128)(2,1)}, bf16[112,576]{1,0:T(8,128)(2,1)S(1)}, u32[]{:S(2)}, u32[]{:S(2)}) collective-permute-start(bf16[112,576]{1,0:T(8,128)(2,1)} %get-tuple-element.103), channel_id=1, source_target_pairs={{0,2},{1,3},{2,0},{3,1},{4,6},{5,7},{6,4},{7,5},{8,10},{9,11},{10,... | collective-permute-start | bytes 387080 | tf_op jit(solution)/shard_map/ppermute | solution.py:508
  20.9 34.4 %collective-permute-start.12 = (bf16[240,768]{1,0:T(8,128)(2,1)}, bf16[240,768]{1,0:T(8,128)(2,1)S(1)}, u32[]{:S(2)}, u32[]{:S(2)}) collective-permute-start(bf16[240,768]{1,0:T(8,128)(2,1)} %get-tuple-element.110), channel_id=1, source_target_pairs={{0,3},{1,0},{2,1},{3,2},{4,7},{5,4},{6,5},{7,6},{8,11},{9,8},{10,9... | collective-permute-start | bytes 1105928 | tf_op jit(solution)/shard_map/ppermute | solution.py:508
  21.7 39.8 %collective-permute-start.16 = (bf16[240,768]{1,0:T(8,128)(2,1)}, bf16[240,768]{1,0:T(8,128)(2,1)S(1)}, u32[]{:S(2)}, u32[]{:S(2)}) collective-permute-start(bf16[240,768]{1,0:T(8,128)(2,1)} %get-tuple-element.110), channel_id=1, source_target_pairs={{0,2},{1,3},{2,0},{3,1},{4,6},{5,7},{6,4},{7,5},{8,10},{9,11},{10,... | collective-permute-start | bytes 1105928 | tf_op jit(solution)/shard_map/ppermute | solution.py:508
  24.0 19.3 %collective-permute-start.5 = (bf16[112,576]{1,0:T(8,128)(2,1)S(1)}, bf16[112,576]{1,0:T(8,128)(2,1)S(1)}, u32[]{:S(2)}, u32[]{:S(2)}) collective-permute-start(bf16[112,576]{1,0:T(8,128)(2,1)S(1)} %copy-done.76), channel_id=1, source_target_pairs={{0,1},{1,2},{2,3},{3,0},{4,5},{5,6},{6,7},{7,4},{8,9},{9,10},{10,1... | collective-permute-start | bytes 387080 | tf_op jit(solution)/shard_map/ppermute | solution.py:508
  28.0 15.3 %collective-permute-start.6 = (bf16[112,576]{1,0:T(8,128)(2,1)S(1)}, bf16[112,576]{1,0:T(8,128)(2,1)S(1)}, u32[]{:S(2)}, u32[]{:S(2)}) collective-permute-start(bf16[112,576]{1,0:T(8,128)(2,1)S(1)} %collective-permute-done.3.g1), channel_id=1, source_target_pairs={{0,16},{4,20},{8,24},{12,28},{16,0},{20,4},{24,8},{28,12},{1,17},{... | collective-permute-start | bytes 387080 | tf_op jit(solution)/shard_map/ppermute | solution.py:504
  29.5 24.3 %collective-permute-start.7 = (bf16[112,576]{1,0:T(8,128)(2,1)S(1)}, bf16[112,576]{1,0:T(8,128)(2,1)S(1)}, u32[]{:S(2)}, u32[]{:S(2)}) collective-permute-start(bf16[112,576]{1,0:T(8,128)(2,1)S(1)} %collective-permute-done.4.g2), channel_id=1, source_target_pairs={{0,16},{4,20},{8,24},{12,28},{16,0},{20,4},{24,8},{28,12},{1,17},{... | collective-permute-start | bytes 387080 | tf_op jit(solution)/shard_map/ppermute | solution.py:504
  43.2 40.2 %collective-permute-start.2 = (bf16[512,768]{1,0:T(8,128)(2,1)}, bf16[512,768]{1,0:T(8,128)(2,1)S(1)}, u32[]{:S(2)}, u32[]{:S(2)}) collective-permute-start(bf16[512,768]{1,0:T(8,128)(2,1)} %pad_maximum_fusion), channel_id=1, source_target_pairs={{0,4},{4,0},{8,12},{12,8},{16,20},{20,16},{24,28},{28,24},{1,5},{5... | collective-permute-start | bytes 2359304 | tf_op jit(solution)/shard_map/ppermute | solution.py:504
  43.3 19.7 %collective-permute-start.20 = (bf16[240,768]{1,0:T(8,128)(2,1)S(1)}, bf16[240,768]{1,0:T(8,128)(2,1)S(1)}, u32[]{:S(2)}, u32[]{:S(2)}) collective-permute-start(bf16[240,768]{1,0:T(8,128)(2,1)S(1)} %copy-done.74), channel_id=1, source_target_pairs={{0,1},{1,2},{2,3},{3,0},{4,5},{5,6},{6,7},{7,4},{8,9},{9,10},{10,1... | collective-permute-start | bytes 1105928 | tf_op jit(solution)/shard_map/ppermute | solution.py:508
  53.8 6.0 %collective-permute-start.8 = (bf16[112,576]{1,0:T(8,128)(2,1)S(1)}, bf16[112,576]{1,0:T(8,128)(2,1)}, u32[]{:S(2)}, u32[]{:S(2)}) collective-permute-start(bf16[112,576]{1,0:T(8,128)(2,1)S(1)} %collective-permute-done.5.g3), channel_id=1, source_target_pairs={{0,16},{4,20},{8,24},{12,28},{16,0},{20,4},{24,8},{28,12},{1,17},{... | collective-permute-start | bytes 387080 | tf_op jit(solution)/shard_map/ppermute | solution.py:504
  55.4 11.5 %collective-permute-start.13 = (bf16[240,768]{1,0:T(8,128)(2,1)S(1)}, bf16[240,768]{1,0:T(8,128)(2,1)S(1)}, u32[]{:S(2)}, u32[]{:S(2)}) collective-permute-start(bf16[240,768]{1,0:T(8,128)(2,1)S(1)} %collective-permute-done.12.refs_0_), channel_id=1, source_target_pairs={{0,8},{4,12},{8,0},{12,4},{16,24},{20,28},{24,16},{28,20},{1,9},{5... | collective-permute-start | bytes 1105928 | tf_op jit(solution)/shard_map/ppermute | solution.py:504
  59.8 19.4 %collective-permute-start.14 = (bf16[240,768]{1,0:T(8,128)(2,1)S(1)}, bf16[240,768]{1,0:T(8,128)(2,1)S(1)}, u32[]{:S(2)}, u32[]{:S(2)}) collective-permute-start(bf16[240,768]{1,0:T(8,128)(2,1)S(1)} %collective-permute-done.12.refs_0_), channel_id=1, source_target_pairs={{0,16},{4,20},{8,24},{12,28},{16,0},{20,4},{24,8},{28,12},{1,17},{... | collective-permute-start | bytes 1105928 | tf_op jit(solution)/shard_map/ppermute | solution.py:504
  61.5 19.1 %collective-permute-start.15 = (bf16[240,768]{1,0:T(8,128)(2,1)S(1)}, bf16[240,768]{1,0:T(8,128)(2,1)S(1)}, u32[]{:S(2)}, u32[]{:S(2)}) collective-permute-start(bf16[240,768]{1,0:T(8,128)(2,1)S(1)} %collective-permute-done.12.refs_0_), channel_id=1, source_target_pairs={{0,24},{4,28},{8,16},{12,20},{16,8},{20,12},{24,0},{28,4},{1,25},{... | collective-permute-start | bytes 1105928 | tf_op jit(solution)/shard_map/ppermute | solution.py:504
  63.0 19.8 %collective-permute-start.17 = (bf16[240,768]{1,0:T(8,128)(2,1)S(1)}, bf16[240,768]{1,0:T(8,128)(2,1)}, u32[]{:S(2)}, u32[]{:S(2)}) collective-permute-start(bf16[240,768]{1,0:T(8,128)(2,1)S(1)} %collective-permute-done.16.refs_4_), channel_id=1, source_target_pairs={{0,8},{4,12},{8,0},{12,4},{16,24},{20,28},{24,16},{28,20},{1,9},{5... | collective-permute-start | bytes 1105928 | tf_op jit(solution)/shard_map/ppermute | solution.py:504
  66.9 37.7 %collective-permute-start.18 = (bf16[240,768]{1,0:T(8,128)(2,1)S(1)}, bf16[240,768]{1,0:T(8,128)(2,1)}, u32[]{:S(2)}, u32[]{:S(2)}) collective-permute-start(bf16[240,768]{1,0:T(8,128)(2,1)S(1)} %collective-permute-done.16.refs_4_), channel_id=1, source_target_pairs={{0,16},{4,20},{8,24},{12,28},{16,0},{20,4},{24,8},{28,12},{1,17},{... | collective-permute-start | bytes 1105928 | tf_op jit(solution)/shard_map/ppermute | solution.py:504
  79.2 26.9 %collective-permute-start.19 = (bf16[240,768]{1,0:T(8,128)(2,1)S(1)}, bf16[240,768]{1,0:T(8,128)(2,1)}, u32[]{:S(2)}, u32[]{:S(2)}) collective-permute-start(bf16[240,768]{1,0:T(8,128)(2,1)S(1)} %collective-permute-done.16.refs_4_), channel_id=1, source_target_pairs={{0,24},{4,28},{8,16},{12,20},{16,8},{20,12},{24,0},{28,4},{1,25},{... | collective-permute-start | bytes 1105928 | tf_op jit(solution)/shard_map/ppermute | solution.py:504
  80.7 25.4 %collective-permute-start.21 = (bf16[240,768]{1,0:T(8,128)(2,1)S(1)}, bf16[240,768]{1,0:T(8,128)(2,1)}, u32[]{:S(2)}, u32[]{:S(2)}) collective-permute-start(bf16[240,768]{1,0:T(8,128)(2,1)S(1)} %collective-permute-done.20.refs_8_), channel_id=1, source_target_pairs={{0,8},{4,12},{8,0},{12,4},{16,24},{20,28},{24,16},{28,20},{1,9},{5... | collective-permute-start | bytes 1105928 | tf_op jit(solution)/shard_map/ppermute | solution.py:504
  82.8 26.4 %collective-permute-start.22 = (bf16[240,768]{1,0:T(8,128)(2,1)S(1)}, bf16[240,768]{1,0:T(8,128)(2,1)}, u32[]{:S(2)}, u32[]{:S(2)}) collective-permute-start(bf16[240,768]{1,0:T(8,128)(2,1)S(1)} %collective-permute-done.20.refs_8_), channel_id=1, source_target_pairs={{0,16},{4,20},{8,24},{12,28},{16,0},{20,4},{24,8},{28,12},{1,17},{... | collective-permute-start | bytes 1105928 | tf_op jit(solution)/shard_map/ppermute | solution.py:504
  83.4 25.8 %collective-permute-start.23 = (bf16[240,768]{1,0:T(8,128)(2,1)S(1)}, bf16[240,768]{1,0:T(8,128)(2,1)}, u32[]{:S(2)}, u32[]{:S(2)}) collective-permute-start(bf16[240,768]{1,0:T(8,128)(2,1)S(1)} %collective-permute-done.20.refs_8_), channel_id=1, source_target_pairs={{0,24},{4,28},{8,16},{12,20},{16,8},{20,12},{24,0},{28,4},{1,25},{... | collective-permute-start | bytes 1105928 | tf_op jit(solution)/shard_map/ppermute | solution.py:504
  106.1 6.0 %collective-permute-start.11 = (bf16[256,192]{1,0:T(8,128)(2,1)}, bf16[256,192]{1,0:T(8,128)(2,1)S(1)}, u32[]{:S(2)}, u32[]{:S(2)}) collective-permute-start(bf16[256,192]{1,0:T(8,128)(2,1)} %get-tuple-element.108), channel_id=1, source_target_pairs={{0,12},{4,8},{8,4},{12,0},{16,28},{20,24},{24,20},{28,16},{1,13},{... | collective-permute-start | bytes 294920 | tf_op jit(solution)/shard_map/ppermute | solution.py:504
  106.1 6.0 %collective-permute-start.9 = (bf16[256,192]{1,0:T(8,128)(2,1)S(1)}, bf16[256,192]{1,0:T(8,128)(2,1)S(1)}, u32[]{:S(2)}, u32[]{:S(2)}) collective-permute-start(bf16[256,192]{1,0:T(8,128)(2,1)S(1)} %copy-done.77), channel_id=1, source_target_pairs={{0,4},{4,0},{8,12},{12,8},{16,20},{20,16},{24,28},{28,24},{1,5},{5... | collective-permute-start | bytes 294920 | tf_op jit(solution)/shard_map/ppermute | solution.py:504
  129.4 8.1 %collective-permute-start.25 = (f32[256,768]{1,0:T(8,128)}, f32[256,768]{1,0:T(8,128)S(1)}, u32[]{:S(2)}, u32[]{:S(2)}) collective-permute-start(f32[256,768]{1,0:T(8,128)} %get-tuple-element.117), channel_id=1, source_target_pairs={{0,4},{4,0},{8,12},{12,8},{16,20},{20,16},{24,28},{28,24},{1,5},{5... | collective-permute-start | bytes 2359304 | tf_op jit(solution)/shard_map/ppermute | solution.py:504
  130.5 7.0 %collective-permute-start.26 = (bf16[128,768]{1,0:T(8,128)(2,1)S(1)}, bf16[128,768]{1,0:T(8,128)(2,1)S(1)}, u32[]{:S(2)}, u32[]{:S(2)}) collective-permute-start(bf16[128,768]{1,0:T(8,128)(2,1)S(1)} %get-tuple-element.189), channel_id=1, source_target_pairs={{0,16},{4,20},{8,24},{12,28},{16,0},{20,4},{24,8},{28,12},{1,17},{... | collective-permute-start | bytes 589832 | tf_op jit(solution)/shard_map/ppermute | solution.py:504
  159.5 52.1 %collective-permute-start.43 = (bf16[384,1536]{1,0:T(8,128)(2,1)}, bf16[384,1536]{1,0:T(8,128)(2,1)S(1)}, u32[]{:S(2)}, u32[]{:S(2)}) collective-permute-start(bf16[384,1536]{1,0:T(8,128)(2,1)} %get-tuple-element.152), channel_id=1, source_target_pairs={{0,8},{4,12},{8,0},{12,4},{16,24},{20,28},{24,16},{28,20},{1,9},{5... | collective-permute-start | bytes 3538952 | tf_op jit(solution)/shard_map/ppermute | solution.py:504
  160.9 54.6 %collective-permute-start.44 = (bf16[768,768]{1,0:T(8,128)(2,1)}, bf16[768,768]{1,0:T(8,128)(2,1)S(1)}, u32[]{:S(2)}, u32[]{:S(2)}) collective-permute-start(bf16[768,768]{1,0:T(8,128)(2,1)} %get-tuple-element.154), channel_id=1, source_target_pairs={{0,16},{4,20},{8,24},{12,28},{16,0},{20,4},{24,8},{28,12},{1,17},{... | collective-permute-start | bytes 3538952 | tf_op jit(solution)/shard_map/ppermute | solution.py:504
  171.5 69.9 %collective-permute-start.47 = (bf16[800,384]{1,0:T(8,128)(2,1)}, bf16[800,384]{1,0:T(8,128)(2,1)S(1)}, u32[]{:S(2)}, u32[]{:S(2)}) collective-permute-start(bf16[800,384]{1,0:T(8,128)(2,1)} %get-tuple-element.164), channel_id=1, source_target_pairs={{0,4},{4,0},{8,12},{12,8},{16,20},{20,16},{24,28},{28,24},{1,5},{5... | collective-permute-start | bytes 1843208 | tf_op jit(solution)/shard_map/ppermute | solution.py:504
  172.1 19.3 %collective-permute-start.31 = (bf16[256,192]{1,0:T(8,128)(2,1)}, bf16[256,192]{1,0:T(8,128)(2,1)S(1)}, u32[]{:S(2)}, u32[]{:S(2)}) collective-permute-start(bf16[256,192]{1,0:T(8,128)(2,1)} %get-tuple-element.132), channel_id=1, source_target_pairs={{0,8},{4,12},{8,0},{12,4},{16,24},{20,28},{24,16},{28,20},{1,9},{5... | collective-permute-start | bytes 294920 | tf_op jit(solution)/shard_map/ppermute | solution.py:504
  174.0 18.5 %collective-permute-start.32 = (bf16[256,192]{1,0:T(8,128)(2,1)}, bf16[256,192]{1,0:T(8,128)(2,1)S(1)}, u32[]{:S(2)}, u32[]{:S(2)}) collective-permute-start(bf16[256,192]{1,0:T(8,128)(2,1)} %get-tuple-element.133), channel_id=1, source_target_pairs={{0,12},{4,8},{8,4},{12,0},{16,28},{20,24},{24,20},{28,16},{1,13},{... | collective-permute-start | bytes 294920 | tf_op jit(solution)/shard_map/ppermute | solution.py:504
  210.7 15.5 %collective-permute-start.36 = (bf16[192,640]{1,0:T(8,128)(2,1)}, bf16[192,640]{1,0:T(8,128)(2,1)S(1)}, u32[]{:S(2)}, u32[]{:S(2)}) collective-permute-start(bf16[192,640]{1,0:T(8,128)(2,1)} %get-tuple-element.142), channel_id=1, source_target_pairs={{0,3},{1,0},{2,1},{3,2},{4,7},{5,4},{6,5},{7,6},{8,11},{9,8},{10,9... | collective-permute-start | bytes 737288 | tf_op jit(solution)/shard_map/ppermute | solution.py:508
  210.8 9.8 %collective-permute-start.27 = (bf16[128,768]{1,0:T(8,128)(2,1)}, bf16[128,768]{1,0:T(8,128)(2,1)}, u32[]{:S(2)}, u32[]{:S(2)}) collective-permute-start(bf16[128,768]{1,0:T(8,128)(2,1)} %get-tuple-element.119), channel_id=1, source_target_pairs={{0,16},{4,20},{8,24},{12,28},{16,0},{20,4},{24,8},{28,12},{1,17},{... | collective-permute-start | bytes 589832 | tf_op jit(solution)/shard_map/ppermute | solution.py:504
  211.6 25.8 %collective-permute-start.37 = (bf16[192,640]{1,0:T(8,128)(2,1)}, bf16[192,640]{1,0:T(8,128)(2,1)S(1)}, u32[]{:S(2)}, u32[]{:S(2)}) collective-permute-start(bf16[192,640]{1,0:T(8,128)(2,1)} %get-tuple-element.143), channel_id=1, source_target_pairs={{0,2},{1,3},{2,0},{3,1},{4,6},{5,7},{6,4},{7,5},{8,10},{9,11},{10,... | collective-permute-start | bytes 737288 | tf_op jit(solution)/shard_map/ppermute | solution.py:508
  215.5 23.3 %collective-permute-start.38 = (bf16[192,640]{1,0:T(8,128)(2,1)}, bf16[192,640]{1,0:T(8,128)(2,1)}, u32[]{:S(2)}, u32[]{:S(2)}) collective-permute-start(bf16[192,640]{1,0:T(8,128)(2,1)} %get-tuple-element.144), channel_id=1, source_target_pairs={{0,1},{1,2},{2,3},{3,0},{4,5},{5,6},{6,7},{7,4},{8,9},{9,10},{10,1... | collective-permute-start | bytes 737288 | tf_op jit(solution)/shard_map/ppermute | solution.py:508
  220.6 22.3 %collective-permute-start.60 = (bf16[192,768]{1,0:T(8,128)(2,1)}, bf16[192,768]{1,0:T(8,128)(2,1)S(1)}, u32[]{:S(2)}, u32[]{:S(2)}) collective-permute-start(bf16[192,768]{1,0:T(8,128)(2,1)} %get-tuple-element.174), channel_id=1, source_target_pairs={{0,16},{4,20},{8,24},{12,28},{16,0},{20,4},{24,8},{28,12},{1,17},{... | collective-permute-start | bytes 884744 | tf_op jit(solution)/shard_map/ppermute | solution.py:504
  226.1 39.0 %collective-permute-start.33 = (bf16[512,768]{1,0:T(8,128)(2,1)}, bf16[512,768]{1,0:T(8,128)(2,1)S(1)}, u32[]{:S(2)}, u32[]{:S(2)}) collective-permute-start(bf16[512,768]{1,0:T(8,128)(2,1)} %get-tuple-element.137), channel_id=1, source_target_pairs={{0,4},{4,0},{8,12},{12,8},{16,20},{20,16},{24,28},{28,24},{1,5},{5... | collective-permute-start | bytes 2359304 | tf_op jit(solution)/shard_map/ppermute | solution.py:504
  237.4 9.9 %collective-permute-start.61 = (bf16[384,384]{1,0:T(8,128)(2,1)S(1)}, bf16[384,384]{1,0:T(8,128)(2,1)S(1)}, u32[]{:S(2)}, u32[]{:S(2)}) collective-permute-start(bf16[384,384]{1,0:T(8,128)(2,1)S(1)} %copy-done.75), channel_id=1, source_target_pairs={{0,8},{4,12},{8,0},{12,4},{16,24},{20,28},{24,16},{28,20},{1,9},{5... | collective-permute-start | bytes 884744 | tf_op jit(solution)/shard_map/ppermute | solution.py:504
  238.8 13.9 %collective-permute-start.45 = (bf16[192,768]{1,0:T(8,128)(2,1)}, bf16[192,768]{1,0:T(8,128)(2,1)S(1)}, u32[]{:S(2)}, u32[]{:S(2)}) collective-permute-start(bf16[192,768]{1,0:T(8,128)(2,1)} %get-tuple-element.156), channel_id=1, source_target_pairs={{0,16},{4,20},{8,24},{12,28},{16,0},{20,4},{24,8},{28,12},{1,17},{... | collective-permute-start | bytes 884744 | tf_op jit(solution)/shard_map/ppermute | solution.py:504
  241.5 11.2 %collective-permute-start.39 = (bf16[192,640]{1,0:T(8,128)(2,1)}, bf16[192,640]{1,0:T(8,128)(2,1)S(1)}, u32[]{:S(2)}, u32[]{:S(2)}) collective-permute-start(bf16[192,640]{1,0:T(8,128)(2,1)} %shard_map.317.mine), channel_id=1, source_target_pairs={{0,16},{4,20},{8,24},{12,28},{16,0},{20,4},{24,8},{28,12},{1,17},{... | collective-permute-start | bytes 737288 | tf_op jit(solution)/shard_map/ppermute | solution.py:504
  242.9 12.3 %collective-permute-start.46 = (bf16[384,384]{1,0:T(8,128)(2,1)}, bf16[384,384]{1,0:T(8,128)(2,1)S(1)}, u32[]{:S(2)}, u32[]{:S(2)}) collective-permute-start(bf16[384,384]{1,0:T(8,128)(2,1)} %get-tuple-element.158), channel_id=1, source_target_pairs={{0,8},{4,12},{8,0},{12,4},{16,24},{20,28},{24,16},{28,20},{1,9},{5... | collective-permute-start | bytes 884744 | tf_op jit(solution)/shard_map/ppermute | solution.py:504
  247.3 14.7 %collective-permute-start.48 = (bf16[416,384]{1,0:T(8,128)(2,1)}, bf16[416,384]{1,0:T(8,128)(2,1)S(1)}, u32[]{:S(2)}, u32[]{:S(2)}) collective-permute-start(bf16[416,384]{1,0:T(8,128)(2,1)} %get-tuple-element.166), channel_id=1, source_target_pairs={{0,8},{4,12},{8,0},{12,4},{16,24},{20,28},{24,16},{28,20},{1,9},{5... | collective-permute-start | bytes 958472 | tf_op jit(solution)/shard_map/ppermute | solution.py:504
  252.7 6.3 %collective-permute-start.62 = (bf16[96,768]{1,0:T(8,128)(2,1)}, bf16[96,768]{1,0:T(8,128)(2,1)S(1)}, u32[]{:S(2)}, u32[]{:S(2)}) collective-permute-start(bf16[96,768]{1,0:T(8,128)(2,1)} %get-tuple-element.178), channel_id=1, source_target_pairs={{0,3},{1,0},{2,1},{3,2},{4,7},{5,4},{6,5},{7,6},{8,11},{9,8},{10,9... | collective-permute-start | bytes 442376 | tf_op jit(solution)/shard_map/ppermute | solution.py:508
  252.7 9.3 %collective-permute-start.63 = (bf16[96,768]{1,0:T(8,128)(2,1)}, bf16[96,768]{1,0:T(8,128)(2,1)S(1)}, u32[]{:S(2)}, u32[]{:S(2)}) collective-permute-start(bf16[96,768]{1,0:T(8,128)(2,1)} %get-tuple-element.179), channel_id=1, source_target_pairs={{0,2},{1,3},{2,0},{3,1},{4,6},{5,7},{6,4},{7,5},{8,10},{9,11},{10,... | collective-permute-start | bytes 442376 | tf_op jit(solution)/shard_map/ppermute | solution.py:508
  255.2 19.4 %collective-permute-start.40 = (bf16[192,640]{1,0:T(8,128)(2,1)}, bf16[192,640]{1,0:T(8,128)(2,1)S(1)}, u32[]{:S(2)}, u32[]{:S(2)}) collective-permute-start(bf16[192,640]{1,0:T(8,128)(2,1)} %shard_map.318.s0), channel_id=1, source_target_pairs={{0,4},{4,0},{8,12},{12,8},{16,20},{20,16},{24,28},{28,24},{1,5},{5... | collective-permute-start | bytes 737288 | tf_op jit(solution)/shard_map/ppermute | solution.py:504
  258.9 16.4 %collective-permute-start.41 = (bf16[192,640]{1,0:T(8,128)(2,1)}, bf16[192,640]{1,0:T(8,128)(2,1)S(1)}, u32[]{:S(2)}, u32[]{:S(2)}) collective-permute-start(bf16[192,640]{1,0:T(8,128)(2,1)} %shard_map.318.s0), channel_id=1, source_target_pairs={{0,8},{4,12},{8,0},{12,4},{16,24},{20,28},{24,16},{28,20},{1,9},{5... | collective-permute-start | bytes 737288 | tf_op jit(solution)/shard_map/ppermute | solution.py:504
  262.0 14.0 %collective-permute-start.42 = (bf16[192,640]{1,0:T(8,128)(2,1)}, bf16[192,640]{1,0:T(8,128)(2,1)S(1)}, u32[]{:S(2)}, u32[]{:S(2)}) collective-permute-start(bf16[192,640]{1,0:T(8,128)(2,1)} %shard_map.318.s0), channel_id=1, source_target_pairs={{0,12},{4,8},{8,4},{12,0},{16,28},{20,24},{24,20},{28,16},{1,13},{... | collective-permute-start | bytes 737288 | tf_op jit(solution)/shard_map/ppermute | solution.py:504
  262.0 8.7 %collective-permute-start.64 = (bf16[96,768]{1,0:T(8,128)(2,1)}, bf16[96,768]{1,0:T(8,128)(2,1)S(1)}, u32[]{:S(2)}, u32[]{:S(2)}) collective-permute-start(bf16[96,768]{1,0:T(8,128)(2,1)} %get-tuple-element.180), channel_id=1, source_target_pairs={{0,1},{1,2},{2,3},{3,0},{4,5},{5,6},{6,7},{7,4},{8,9},{9,10},{10,1... | collective-permute-start | bytes 442376 | tf_op jit(solution)/shard_map/ppermute | solution.py:508
  265.2 23.7 %collective-permute-start.49 = (bf16[224,384]{1,0:T(8,128)(2,1)}, bf16[224,384]{1,0:T(8,128)(2,1)S(1)}, u32[]{:S(2)}, u32[]{:S(2)}) collective-permute-start(bf16[224,384]{1,0:T(8,128)(2,1)} %get-tuple-element.168), channel_id=1, source_target_pairs={{0,16},{4,20},{8,24},{12,28},{16,0},{20,4},{24,8},{28,12},{1,17},{... | collective-permute-start | bytes 516104 | tf_op jit(solution)/shard_map/ppermute | solution.py:504
  271.4 29.7 %collective-permute-start.34 = (bf16[256,768]{1,0:T(8,128)(2,1)}, bf16[256,768]{1,0:T(8,128)(2,1)S(1)}, u32[]{:S(2)}, u32[]{:S(2)}) collective-permute-start(bf16[256,768]{1,0:T(8,128)(2,1)} %get-tuple-element.140), channel_id=1, source_target_pairs={{0,8},{4,12},{8,0},{12,4},{16,24},{20,28},{24,16},{28,20},{1,9},{5... | collective-permute-start | bytes 1179656 | tf_op jit(solution)/shard_map/ppermute | solution.py:504
  274.6 12.1 %collective-permute-start.65 = (bf16[96,768]{1,0:T(8,128)(2,1)}, bf16[96,768]{1,0:T(8,128)(2,1)S(1)}, u32[]{:S(2)}, u32[]{:S(2)}) collective-permute-start(bf16[96,768]{1,0:T(8,128)(2,1)} %shard_map.328.refs_0_), channel_id=1, source_target_pairs={{0,8},{4,12},{8,0},{12,4},{16,24},{20,28},{24,16},{28,20},{1,9},{5... | collective-permute-start | bytes 442376 | tf_op jit(solution)/shard_map/ppermute | solution.py:504
  275.4 11.4 %collective-permute-start.66 = (bf16[96,768]{1,0:T(8,128)(2,1)}, bf16[96,768]{1,0:T(8,128)(2,1)S(1)}, u32[]{:S(2)}, u32[]{:S(2)}) collective-permute-start(bf16[96,768]{1,0:T(8,128)(2,1)} %shard_map.328.refs_0_), channel_id=1, source_target_pairs={{0,16},{4,20},{8,24},{12,28},{16,0},{20,4},{24,8},{28,12},{1,17},{... | collective-permute-start | bytes 442376 | tf_op jit(solution)/shard_map/ppermute | solution.py:504
  275.9 12.9 %collective-permute-start.67 = (bf16[96,768]{1,0:T(8,128)(2,1)}, bf16[96,768]{1,0:T(8,128)(2,1)S(1)}, u32[]{:S(2)}, u32[]{:S(2)}) collective-permute-start(bf16[96,768]{1,0:T(8,128)(2,1)} %shard_map.328.refs_0_), channel_id=1, source_target_pairs={{0,24},{4,28},{8,16},{12,20},{16,8},{20,12},{24,0},{28,4},{1,25},{... | collective-permute-start | bytes 442376 | tf_op jit(solution)/shard_map/ppermute | solution.py:504
  286.7 6.3 %collective-permute-start.68 = (bf16[96,768]{1,0:T(8,128)(2,1)S(1)}, bf16[96,768]{1,0:T(8,128)(2,1)S(1)}, u32[]{:S(2)}, u32[]{:S(2)}) collective-permute-start(bf16[96,768]{1,0:T(8,128)(2,1)S(1)} %copy-done.18), channel_id=1, source_target_pairs={{0,4},{4,0},{8,12},{12,8},{16,20},{20,16},{24,28},{28,24},{1,5},{5... | collective-permute-start | bytes 442376 | tf_op jit(solution)/shard_map/ppermute | solution.py:504
  286.8 9.0 %collective-permute-start.69 = (bf16[96,768]{1,0:T(8,128)(2,1)S(1)}, bf16[96,768]{1,0:T(8,128)(2,1)S(1)}, u32[]{:S(2)}, u32[]{:S(2)}) collective-permute-start(bf16[96,768]{1,0:T(8,128)(2,1)S(1)} %collective-permute-done.65.refs_1_), channel_id=1, source_target_pairs={{0,4},{4,0},{8,12},{12,8},{16,20},{20,16},{24,28},{28,24},{1,5},{5... | collective-permute-start | bytes 442376 | tf_op jit(solution)/shard_map/ppermute | solution.py:504
  288.8 7.0 %collective-permute-start.70 = (bf16[96,768]{1,0:T(8,128)(2,1)S(1)}, bf16[96,768]{1,0:T(8,128)(2,1)S(1)}, u32[]{:S(2)}, u32[]{:S(2)}) collective-permute-start(bf16[96,768]{1,0:T(8,128)(2,1)S(1)} %collective-permute-done.66.refs_2_), channel_id=1, source_target_pairs={{0,4},{4,0},{8,12},{12,8},{16,20},{20,16},{24,28},{28,24},{1,5},{5... | collective-permute-start | bytes 442376 | tf_op jit(solution)/shard_map/ppermute | solution.py:504
  288.9 9.2 %collective-permute-start.71 = (bf16[96,768]{1,0:T(8,128)(2,1)S(1)}, bf16[96,768]{1,0:T(8,128)(2,1)}, u32[]{:S(2)}, u32[]{:S(2)}) collective-permute-start(bf16[96,768]{1,0:T(8,128)(2,1)S(1)} %collective-permute-done.67.refs_3_), channel_id=1, source_target_pairs={{0,4},{4,0},{8,12},{12,8},{16,20},{20,16},{24,28},{28,24},{1,5},{5... | collective-permute-start | bytes 442376 | tf_op jit(solution)/shard_map/ppermute | solution.py:504
  293.0 9.3 %collective-permute-start.50 = (bf16[144,768]{1,0:T(8,128)(2,1)}, bf16[144,768]{1,0:T(8,128)(2,1)S(1)}, u32[]{:S(2)}, u32[]{:S(2)}) collective-permute-start(bf16[144,768]{1,0:T(8,128)(2,1)} %get-tuple-element.170), channel_id=1, source_target_pairs={{0,3},{1,0},{2,1},{3,2},{4,7},{5,4},{6,5},{7,6},{8,11},{9,8},{10,9... | collective-permute-start | bytes 663560 | tf_op jit(solution)/shard_map/ppermute | solution.py:508
  295.8 19.7 %collective-permute-start.51 = (bf16[144,768]{1,0:T(8,128)(2,1)}, bf16[144,768]{1,0:T(8,128)(2,1)S(1)}, u32[]{:S(2)}, u32[]{:S(2)}) collective-permute-start(bf16[144,768]{1,0:T(8,128)(2,1)} %get-tuple-element.171), channel_id=1, source_target_pairs={{0,2},{1,3},{2,0},{3,1},{4,6},{5,7},{6,4},{7,5},{8,10},{9,11},{10,... | collective-permute-start | bytes 663560 | tf_op jit(solution)/shard_map/ppermute | solution.py:508
  296.5 19.0 %collective-permute-start.52 = (bf16[144,768]{1,0:T(8,128)(2,1)}, bf16[144,768]{1,0:T(8,128)(2,1)S(1)}, u32[]{:S(2)}, u32[]{:S(2)}) collective-permute-start(bf16[144,768]{1,0:T(8,128)(2,1)} %get-tuple-element.172), channel_id=1, source_target_pairs={{0,1},{1,2},{2,3},{3,0},{4,5},{5,6},{6,7},{7,4},{8,9},{9,10},{10,1... | collective-permute-start | bytes 663560 | tf_op jit(solution)/shard_map/ppermute | solution.py:508
  301.1 30.5 %collective-permute-start.35 = (bf16[128,768]{1,0:T(8,128)(2,1)S(1)}, bf16[128,768]{1,0:T(8,128)(2,1)S(1)}, u32[]{:S(2)}, u32[]{:S(2)}) collective-permute-start(bf16[128,768]{1,0:T(8,128)(2,1)S(1)} %slice.69), channel_id=1, source_target_pairs={{0,16},{4,20},{8,24},{12,28},{16,0},{20,4},{24,8},{28,12},{1,17},{... | collective-permute-start | bytes 589832 | tf_op jit(solution)/shard_map/ppermute | solution.py:504
  318.3 8.5 %collective-permute-start.53 = (bf16[144,768]{1,0:T(8,128)(2,1)}, bf16[144,768]{1,0:T(8,128)(2,1)S(1)}, u32[]{:S(2)}, u32[]{:S(2)}) collective-permute-start(bf16[144,768]{1,0:T(8,128)(2,1)} %shard_map.326.refs_0_), channel_id=1, source_target_pairs={{0,8},{4,12},{8,0},{12,4},{16,24},{20,28},{24,16},{28,20},{1,9},{5... | collective-permute-start | bytes 663560 | tf_op jit(solution)/shard_map/ppermute | solution.py:504
  319.6 11.5 %collective-permute-start.54 = (bf16[144,768]{1,0:T(8,128)(2,1)}, bf16[144,768]{1,0:T(8,128)(2,1)S(1)}, u32[]{:S(2)}, u32[]{:S(2)}) collective-permute-start(bf16[144,768]{1,0:T(8,128)(2,1)} %shard_map.326.refs_0_), channel_id=1, source_target_pairs={{0,16},{4,20},{8,24},{12,28},{16,0},{20,4},{24,8},{28,12},{1,17},{... | collective-permute-start | bytes 663560 | tf_op jit(solution)/shard_map/ppermute | solution.py:504
  320.8 10.4 %collective-permute-start.55 = (bf16[144,768]{1,0:T(8,128)(2,1)}, bf16[144,768]{1,0:T(8,128)(2,1)S(1)}, u32[]{:S(2)}, u32[]{:S(2)}) collective-permute-start(bf16[144,768]{1,0:T(8,128)(2,1)} %shard_map.326.refs_0_), channel_id=1, source_target_pairs={{0,24},{4,28},{8,16},{12,20},{16,8},{20,12},{24,0},{28,4},{1,25},{... | collective-permute-start | bytes 663560 | tf_op jit(solution)/shard_map/ppermute | solution.py:504
  321.8 10.8 %collective-permute-start.56 = (bf16[144,768]{1,0:T(8,128)(2,1)}, bf16[144,768]{1,0:T(8,128)(2,1)S(1)}, u32[]{:S(2)}, u32[]{:S(2)}) collective-permute-start(bf16[144,768]{1,0:T(8,128)(2,1)} %shard_map.326.refs_0_), channel_id=1, source_target_pairs={{0,4},{4,0},{8,12},{12,8},{16,20},{20,16},{24,28},{28,24},{1,5},{5... | collective-permute-start | bytes 663560 | tf_op jit(solution)/shard_map/ppermute | solution.py:504
  (86 other events, 922.3 us)
